TPU v7x, 256 devices: a whole 4x4x8 slice. The times are simulated.
256 devices in a mesh: section: 2 (over core), row: 8 (over z), col: 16 (over y, x).
Axes of the slice: x: 4, y: 4, z: 8, core: 2. Of those that a mesh axis runs over, the one named last changes fastest.
Arguments:
- inputs: bfloat16 [2, 1024, 6144], P(None, 'row'), may hold values from -6 to 6
- norm_gain: float32 [2, 6144], P('section'), may hold values from 0.1 to 1.9
- w_in: bfloat16 [2, 8, 16, 8, 128, 128], P('section', 'row', 'col'), may hold values from -0.3125 to 0.3125
- w_in_slot: int32 [2, 8, 16, 8], P('section', 'row', 'col'), may hold values from 0 to 71, as said below
- w_in_count: int32 [2, 8, 16], P('section', 'row', 'col'), may hold values from 2 to 8, as said below
- w_out: bfloat16 [2, 8, 16, 8, 128, 128], P('section', 'row', 'col'), may hold values from -0.15625 to 0.15625
- w_out_slot: int32 [2, 8, 16, 8], P('section', 'row', 'col'), may hold values from 0 to 71, as said below
- w_out_count: int32 [2, 8, 16], P('section', 'row', 'col'), may hold values from 2 to 8, as said below
Outputs:
- phase_outputs: bfloat16 [2, 2, 1024, 6144], P('section', None, 'row', 'col')
Inputs may be any that keep to these rules, and one draw needn't show every extreme that they name: `w_in_slot`: positions p = d * 12 + f of a block in its cell's 6 x 12 grid of blocks; distinct within a cell; slots at or beyond the cell's count are ignored. `w_in_count`: used slots are the leading ones; in every phase each grid row has a cell with exactly 8. `w_out_slot`: positions p = d * 12 + f of a block in its cell's 6 x 12 grid of blocks; distinct within a cell; slots at or beyond the cell's count are ignored. `w_out_count`: used slots are the leading ones; in every phase each grid row has a cell with exactly 8.
All inputs are finite; a program needn't handle non-finite values.
Results may differ from a plain program's by a relative error of at most 0.012.
Values may be sent and summed in bfloat16 or wider, within the bound.
No kernel may reach another device: no remote copies, remote signals or barrier semaphores. Data moves between devices by JAX's collectives and lax.ppermute only.
A program may use at most 64 MiB of HBM per device.

v0:
```python
import functools

import jax
import jax.numpy as jnp
from jax import lax
from jax.experimental import pallas as pl
from jax.experimental.pallas import tpu as pltpu
from jax.sharding import PartitionSpec as P


EPSILON = 1e-05
BLK = 128
SLOTS = 8
UNROLL = 4
GRID_ROWS = 8
OFFSETS = (0, -1, -2, -3, -4, 1, 2, 3)
SIDE = 4
DBL = 6
FBL = 12
BLOCKS = 48
CHUNK = 3
TOK = 128
WIDTH = CHUNK * BLK


F32 = jnp.float32
BF16 = jnp.bfloat16


def vmem():
    return pl.BlockSpec(memory_space=pltpu.VMEM)


def smem():
    return pl.BlockSpec(memory_space=pltpu.SMEM)


def chunk_of(place_ref, first, second):
    core = place_ref[0]
    return jnp.where(core == 0, second * SIDE + first, first * SIDE + second)


def digit(value):
    return lax.rem(value + 2 * SIDE, SIDE)


def fetch(cells, offset, weights, sems):
    copies = [
        pltpu.make_async_copy(
            cell.at[pl.ds(offset, SLOTS)], weights.at[pl.ds(i * SLOTS, SLOTS)], sems.at[i]
        )
        for i, cell in enumerate(cells)
    ]
    for copy in copies:
        copy.start()
    return copies


def list_blocks(place_ref, meta_ref, phase, inward, blocks):
    sign = 1 - 2 * place_ref[0]
    used = 0
    for i, offset in enumerate(OFFSETS):
        row = lax.rem(place_ref[4] + sign * offset + 2 * GRID_ROWS, GRID_ROWS)
        base = phase * GRID_ROWS + row
        start = 0 if inward else SLOTS + 1
        for n in range(SLOTS):
            slot = meta_ref[base, start + n]
            model, hid = row * DBL + slot // FBL, lax.rem(slot, FBL)
            blocks[0, used + n] = i * SLOTS + n
            blocks[1, used + n] = model if inward else hid
            blocks[2, used + n] = hid if inward else model
        used = used + meta_ref[base, start + SLOTS]
    for n in range(UNROLL):
        blocks[0, used + n] = 0
        blocks[1, used + n] = 0
        blocks[2, used + n] = FBL if inward else BLOCKS
    return used


def block_sum(dense, weights, blocks, used, total):
    def group(step, carry):
        at = step * UNROLL
        products = [
            jnp.dot(
                dense[blocks[1, at + u]],
                weights[blocks[0, at + u]],
                preferred_element_type=F32,
            )
            for u in range(UNROLL)
        ]
        for u, product in enumerate(products):
            total[blocks[2, at + u]] += product
        return carry

    lax.fori_loop(0, (used + UNROLL - 1) // UNROLL, group, 0)


def gelu_into(total, hidden):
    for f in range(FBL):
        hidden[f] = jax.nn.gelu(total[f], approximate=True).astype(BF16)


def first_norm_kernel(micro_ref, place_ref, x_ref, gain_ref, normed_ref, own_ref):
    squares = jnp.zeros((TOK, BLK), F32)
    for k in range(BLOCKS):
        part = x_ref[0, :, k * BLK : (k + 1) * BLK].astype(F32)
        squares = squares + part * part
    mean = jnp.sum(squares, axis=1, keepdims=True) / (BLOCKS * BLK)
    scale = lax.rsqrt(mean + EPSILON)
    for k in range(BLOCKS):
        part = x_ref[0, :, k * BLK : (k + 1) * BLK].astype(F32)
        normed_ref[k] = (part * scale * gain_ref[k]).astype(BF16)
    start = pl.multiple_of(place_ref[1] * WIDTH, BLK)
    own_ref[...] = x_ref[0, :, pl.ds(start, WIDTH)]


def first_in_kernel(place_ref, meta_ref, normed_ref, *refs):
    cells = refs[:GRID_ROWS]
    hidden_ref, total, weights, blocks, sems = refs[GRID_ROWS:]
    copies = fetch(cells, 0, weights, sems)
    used = list_blocks(place_ref, meta_ref, 0, True, blocks)
    total[...] = jnp.zeros_like(total)
    for copy in copies:
        copy.wait()
    block_sum(normed_ref, weights, blocks, used, total)
    gelu_into(total, hidden_ref)


def later_in_kernel(place_ref, meta_ref, gain_ref, *refs):
    bundles = refs[:SIDE]
    cells = refs[SIDE : SIDE + GRID_ROWS]
    hidden_ref, normed, total, weights, blocks, sems = refs[SIDE + GRID_ROWS :]
    copies = fetch(cells, 0, weights, sems)
    used = list_blocks(place_ref, meta_ref, 1, True, blocks)
    squares = jnp.zeros((TOK, BLK), F32)
    for d in range(SIDE):
        for e in range(SIDE):
            for q in range(CHUNK):
                part = bundles[d][e, :, q * BLK : (q + 1) * BLK].astype(F32)
                squares = squares + part * part
    mean = jnp.sum(squares, axis=1, keepdims=True) / (BLOCKS * BLK)
    scale = lax.rsqrt(mean + EPSILON)
    for d in range(SIDE):
        for e in range(SIDE):
            chunk = chunk_of(place_ref, digit(place_ref[2] - d), digit(place_ref[3] - e))
            for q in range(CHUNK):
                k = chunk * CHUNK + q
                part = bundles[d][e, :, q * BLK : (q + 1) * BLK].astype(F32)
                normed[k] = (part * scale * gain_ref[k]).astype(BF16)
    total[...] = jnp.zeros_like(total)
    for copy in copies:
        copy.wait()
    block_sum(normed, weights, blocks, used, total)
    gelu_into(total, hidden_ref)


def out_kernel(phase, place_ref, meta_ref, hidden_ref, *refs):
    cells = refs[:GRID_ROWS]
    sends = refs[GRID_ROWS : GRID_ROWS + SIDE]
    total, weights, blocks, sems = refs[GRID_ROWS + SIDE :]
    copies = fetch(cells, phase * SLOTS, weights, sems)
    used = list_blocks(place_ref, meta_ref, phase, False, blocks)
    total[...] = jnp.zeros_like(total)
    for copy in copies:
        copy.wait()
    block_sum(hidden_ref, weights, blocks, used, total)
    for d in range(SIDE):
        for e in range(SIDE):
            chunk = chunk_of(place_ref, digit(place_ref[2] + d), digit(place_ref[3] + e))
            for q in range(CHUNK):
                sends[d][e, :, q * BLK : (q + 1) * BLK] = total[chunk * CHUNK + q].astype(BF16)


def sum_kernel(own_ref, one_ref, two_ref, three_ref, *sums):
    for e in range(SIDE):
        value = (
            own_ref[e].astype(F32)
            + one_ref[e].astype(F32)
            + two_ref[e].astype(F32)
            + three_ref[e].astype(F32)
        )
        sums[e][...] = value.astype(sums[e].dtype)


def cost(blocks, moved):
    return pl.CostEstimate(flops=blocks * 2 * BLK**3, bytes_accessed=moved, transcendentals=0)


WORK = [
    pltpu.VMEM((GRID_ROWS * SLOTS, BLK, BLK), BF16),
    pltpu.SMEM((3, GRID_ROWS * SLOTS + 2 * SLOTS), jnp.int32),
    pltpu.SemaphoreType.DMA((GRID_ROWS,)),
]
PARAMS = pltpu.CompilerParams(vmem_limit_bytes=16 << 20)
NORMED = jax.ShapeDtypeStruct((BLOCKS, TOK, BLK), BF16)
HIDDEN = jax.ShapeDtypeStruct((FBL, TOK, BLK), BF16)
BUNDLE = jax.ShapeDtypeStruct((SIDE, TOK, WIDTH), BF16)
PIECE = jax.ShapeDtypeStruct((TOK, WIDTH), BF16)


def first_norm(micro, place, inputs, gain):
    return pl.pallas_call(
        first_norm_kernel,
        grid_spec=pltpu.PrefetchScalarGridSpec(
            num_scalar_prefetch=2,
            grid=(1,),
            in_specs=[
                pl.BlockSpec((1, TOK, BLOCKS * BLK), lambda i, micro, place: (micro[0], 0, 0)),
                pl.BlockSpec((BLOCKS, 1, BLK), lambda i, micro, place: (0, 0, 0)),
            ],
            out_specs=[
                pl.BlockSpec((BLOCKS, TOK, BLK), lambda i, micro, place: (0, 0, 0)),
                pl.BlockSpec((TOK, WIDTH), lambda i, micro, place: (0, 0)),
            ],
        ),
        out_shape=[NORMED, PIECE],
        cost_estimate=cost(1, 6 << 20),
        compiler_params=PARAMS,
        name="first_norm",
    )(micro, place, inputs, gain)


def anywhere():
    return pl.BlockSpec(memory_space=pl.ANY)


def first_in(place, meta, normed, cells):
    return pl.pallas_call(
        first_in_kernel,
        in_specs=[smem(), smem(), vmem()] + [anywhere()] * GRID_ROWS,
        out_specs=vmem(),
        out_shape=HIDDEN,
        scratch_shapes=[pltpu.VMEM((FBL + 1, TOK, BLK), F32)] + WORK,
        cost_estimate=cost(512, 8 << 20),
        compiler_params=PARAMS,
        name="first_in",
    )(place, meta, normed, *cells)


def later_in(place, meta, gain, bundles, cells):
    return pl.pallas_call(
        later_in_kernel,
        in_specs=[smem(), smem()] + [vmem()] * (1 + SIDE) + [anywhere()] * GRID_ROWS,
        out_specs=vmem(),
        out_shape=HIDDEN,
        scratch_shapes=[
            pltpu.VMEM((BLOCKS, TOK, BLK), BF16),
            pltpu.VMEM((FBL + 1, TOK, BLK), F32),
        ]
        + WORK,
        cost_estimate=cost(512, 12 << 20),
        compiler_params=PARAMS,
        name="later_in",
    )(place, meta, gain, *bundles, *cells)


def project_out(phase, place, meta, hidden, cells):
    return pl.pallas_call(
        functools.partial(out_kernel, phase),
        in_specs=[smem(), smem(), vmem()] + [anywhere()] * GRID_ROWS,
        out_specs=[vmem()] * SIDE,
        out_shape=[BUNDLE] * SIDE,
        scratch_shapes=[pltpu.VMEM((BLOCKS + 1, TOK, BLK), F32)] + WORK,
        cost_estimate=cost(512, 8 << 20),
        compiler_params=PARAMS,
        name="project_out",
    )(place, meta, hidden, *cells)


def sum_bundles(bundles):
    return pl.pallas_call(
        sum_kernel,
        in_specs=[vmem()] * SIDE,
        out_specs=[vmem()] * SIDE,
        out_shape=[jax.ShapeDtypeStruct((TOK, WIDTH), F32)] + [PIECE] * (SIDE - 1),
        cost_estimate=cost(0, 2 << 20),
        compiler_params=PARAMS,
        name="sum_bundles",
    )(*bundles)


def on_rows(value, perm):
    return lax.ppermute(value, ("section", "row"), perm)


def on_cols(value, perm):
    return lax.ppermute(value, ("section", "col"), perm)


SWAP = [(i, (i + GRID_ROWS) % (2 * GRID_ROWS)) for i in range(2 * GRID_ROWS)]
AROUND = [(r, (r + 1) % GRID_ROWS) for r in range(GRID_ROWS)] + [
    (GRID_ROWS + r, GRID_ROWS + (r - 1) % GRID_ROWS) for r in range(GRID_ROWS)
]


def column_shift(first, distance):
    pairs = []
    for core in range(2):
        for y in range(SIDE):
            for x in range(SIDE):
                along_x = (core == 0) == first
                to_y = y if along_x else (y + distance) % SIDE
                to_x = (x + distance) % SIDE if along_x else x
                base = core * SIDE * SIDE
                pairs.append((base + y * SIDE + x, base + to_y * SIDE + to_x))
    return pairs


def ring_gather(cell):
    ring = [cell]
    other = []
    for step in range(1, GRID_ROWS // 2 + 1):
        ring.append(on_rows(ring[-1], AROUND))
        if step < GRID_ROWS // 2:
            other.append(on_rows(ring[-1], SWAP))
    return ring + other


def reduce_columns(bundles):
    landed = []
    for d in range(1, SIDE):
        landed.append(on_cols(bundles[d], column_shift(True, d)))
    sums = sum_bundles([bundles[0]] + landed)
    last = []
    for e in range(1, SIDE):
        last.append(on_cols(sums[e], column_shift(False, e)))
    return sums[0], last


def gather_columns(piece):
    pieces = [piece]
    for e in range(1, SIDE):
        pieces.append(on_cols(piece, column_shift(False, e)))
    bundle = jnp.stack(pieces)
    bundles = [bundle]
    for d in range(1, SIDE):
        bundles.append(on_cols(bundle, column_shift(True, d)))
    return bundles


def add_branch(piece, own_sum, last):
    total = own_sum
    for value in last:
        total = total + value.astype(F32)
    return (piece.astype(F32) + total).astype(BF16)


def shards(inputs, norm_gain, w_in, w_in_slot, w_in_count, w_out, w_out_slot, w_out_count):
    core = lax.axis_index("section")
    row = lax.axis_index("row")
    col = lax.axis_index("col")
    y, x = col // SIDE, col % SIDE
    first = jnp.where(core == 0, x, y)
    second = jnp.where(core == 0, y, x)
    place = jnp.stack([core, col, first, second, row]).astype(jnp.int32)
    micro = jnp.reshape(core, (1,)).astype(jnp.int32)

    own_meta = jnp.concatenate(
        [
            w_in_slot.reshape(SLOTS),
            w_in_count.reshape(1),
            w_out_slot.reshape(SLOTS),
            w_out_count.reshape(1),
            jnp.zeros((BLK - 2 * SLOTS - 2,), jnp.int32),
        ]
    )
    meta = lax.all_to_all(
        jnp.broadcast_to(own_meta, (2 * GRID_ROWS, 1, BLK)),
        ("section", "row"),
        0,
        0,
        tiled=True,
    ).reshape(2 * GRID_ROWS, BLK)
    own_in = w_in.reshape(SLOTS, BLK, BLK)
    own_out = w_out.reshape(SLOTS, BLK, BLK)
    other_in = on_rows(own_in, SWAP)
    other_out = on_rows(own_out, SWAP)
    mine = core == 0
    cells_in = ring_gather(jnp.where(mine, own_in, other_in))
    cells_out = ring_gather(jnp.where(mine, own_out, other_out))
    own_in, own_out, other_in, other_out, _ = lax.optimization_barrier(
        (own_in, own_out, other_in, other_out, cells_in[1])
    )
    later_cells = ring_gather(
        jnp.concatenate(
            [jnp.where(mine, other_in, own_in), jnp.where(mine, other_out, own_out)]
        ),
    )

    own_gain = norm_gain.reshape(BLOCKS, 1, BLK)
    other_gain = on_rows(own_gain, SWAP)
    gains = [jnp.where(mine, own_gain, other_gain), jnp.where(mine, other_gain, own_gain)]

    normed, piece = first_norm(micro, place, inputs, gains[0])
    hidden = first_in(place, meta, normed, cells_in)
    bundles = project_out(0, place, meta, hidden, cells_out)
    own_sum, last = reduce_columns(bundles)
    middle = add_branch(piece, own_sum, last)

    bundles = gather_columns(middle)
    hidden = later_in(place, meta, gains[1], bundles, later_cells)
    bundles = project_out(1, place, meta, hidden, later_cells)
    own_sum, last = reduce_columns(bundles)
    final = add_branch(middle, own_sum, last)

    other = on_rows(jnp.where(mine, final, middle), SWAP)
    return jnp.stack([jnp.where(mine, middle, other), jnp.where(mine, other, final)])[None]


def solution(mesh):
    placed = (
        P(None, "row", None),
        P("section", None),
        P("section", "row", "col", None, None, None),
        P("section", "row", "col", None),
        P("section", "row", "col"),
        P("section", "row", "col", None, None, None),
        P("section", "row", "col", None),
        P("section", "row", "col"),
    )

    return jax.shard_map(
        shards,
        mesh=mesh,
        in_specs=placed,
        out_specs=P("section", None, "row", "col"),
        check_vma=False,
    )
```

profile of v0, /device:TPU:2, one launch (start us, length us, event | category | flops | bytes accessed | tf_op | source)
XLA Modules:
  0.0 143.7 jit_solution(16435119188083536551)
XLA Ops:
  7.9 5.3 %collective-permute-done.2.refs_1_ = bf16[8,128,128]{2,1,0:T(8,128)(2,1)S(1)} collective-permute-done((bf16[8,128,128]{2,1,0:T(8,128)(2,1)S(1)}, bf16[8,128,128]{2,1,0:T(8,128)(2,1)S(1)}, u32[]{:S(2)}, u32[]{:S(2)}) %collective-permute-start.2) | collective-permute-done | bytes 262176 | tf_op jit(solution)/shard_map/ppermute | solution.py:283
  13.2 2.8 %collective-permute-done.10.refs_1_ = bf16[8,128,128]{2,1,0:T(8,128)(2,1)S(1)} collective-permute-done((bf16[8,128,128]{2,1,0:T(8,128)(2,1)S(1)}, bf16[8,128,128]{2,1,0:T(8,128)(2,1)S(1)}, u32[]{:S(2)}, u32[]{:S(2)}) %collective-permute-start.10) | collective-permute-done | bytes 262176 | tf_op jit(solution)/shard_map/ppermute | solution.py:283
  18.8 2.1 %collective-permute-done.3.refs_2_ = bf16[8,128,128]{2,1,0:T(8,128)(2,1)} collective-permute-done((bf16[8,128,128]{2,1,0:T(8,128)(2,1)S(1)}, bf16[8,128,128]{2,1,0:T(8,128)(2,1)}, u32[]{:S(2)}, u32[]{:S(2)}) %collective-permute-start.3) | collective-permute-done | bytes 262176 | tf_op jit(solution)/shard_map/ppermute | solution.py:283
  23.9 2.7 %collective-permute-start.12 = (bf16[8,128,128]{2,1,0:T(8,128)(2,1)}, bf16[8,128,128]{2,1,0:T(8,128)(2,1)}, u32[]{:S(2)}, u32[]{:S(2)}) collective-permute-start(bf16[8,128,128]{2,1,0:T(8,128)(2,1)} %collective-permute-done.11.refs_2_), channel_id=1, source_target_pairs={{0,16},{16,32},{32,48},{48,64},{64,80},{80,96},{96,112},{112,0},{1... | collective-permute-start | bytes 786440 | tf_op jit(solution)/shard_map/ppermute | solution.py:283
  26.7 5.5 %collective-permute-done.4.refs_3_ = bf16[8,128,128]{2,1,0:T(8,128)(2,1)} collective-permute-done((bf16[8,128,128]{2,1,0:T(8,128)(2,1)}, bf16[8,128,128]{2,1,0:T(8,128)(2,1)}, u32[]{:S(2)}, u32[]{:S(2)}) %collective-permute-start.4) | collective-permute-done | bytes 262176 | tf_op jit(solution)/shard_map/ppermute | solution.py:283
  35.7 5.8 %all-to-all-start = ((s32[16,1,128]{2,1,0:T(1,128)}), s32[16,1,128]{2,1,0:T(1,128)S(1)}, u32[]{:S(2)}, u32[]{:S(2)}) async-start(s32[16,1,128]{2,1,0:T(1,128)} %broadcast_in_dim.10), calls=%async_computation | async-start | bytes 16384 | tf_op jit(solution)/shard_map/all_to_all | solution.py:367
  53.4 3.9 %first_in.1.hidden_ref = bf16[12,128,128]{2,1,0:T(8,128)(2,1)S(1)} custom-call(s32[5]{0:T(128)S(1)} %stack.44.place_ref, s32[16,128]{1,0:T(8,128)S(1)} %bitcast.29, bf16[48,128,128]{2,1,0:T(8,128)(2,1)S(1)} %copy-done.4, bf16[8,128,128]{2,1,0:T(8,128)(2,1)S(1)} %copy-done.2, bf16[8,128,128]{2,1,0:T(8,128)(2,1)S(1)} %copy-done.8, ...), custom_call_target="tpu_custom_call" | custom-call | flops 2147483648 | bytes 8388608 | tf_op jit(solution)/shard_map/first_in/pallas_call | solution.py:228
  57.4 3.4 %project_out.2 = (bf16[4,128,384]{2,1,0:T(8,128)(2,1)S(1)}, bf16[4,128,384]{2,1,0:T(8,128)(2,1)S(1)}, bf16[4,128,384]{2,1,0:T(8,128)(2,1)S(1)}, bf16[4,128,384]{2,1,0:T(8,128)(2,1)S(1)}) custom-call(s32[5]{0:T(128)S(1)} %stack.44.place_ref, s32[16,128]{1,0:T(8,128)S(1)} %bitcast.30, bf16[12,128,128]{2,1,0:T(8,128)(2,1)S(1)} %first_in.1.hidden_ref, ...), custom_call_target="tpu_custom_call" | custom-call | flops 2147483648 | bytes 8388608 | tf_op jit(solution)/shard_map/project_out/pallas_call | solution.py:258
  63.5 2.5 %collective-permute-start.19 = (bf16[4,128,384]{2,1,0:T(8,128)(2,1)S(1)}, bf16[4,128,384]{2,1,0:T(8,128)(2,1)S(1)}, u32[]{:S(2)}, u32[]{:S(2)}) collective-permute-start(bf16[4,128,384]{2,1,0:T(8,128)(2,1)S(1)} %get-tuple-element.32), channel_id=1, source_target_pairs={{0,3},{1,0},{2,1},{3,2},{4,7},{5,4},{6,5},{7,6},{8,11},{9,8},{10,9... | collective-permute-start | bytes 1179656 | tf_op jit(solution)/shard_map/ppermute | solution.py:287
  66.0 2.7 %collective-permute-done.17.one_ref = bf16[4,128,384]{2,1,0:T(8,128)(2,1)S(1)} collective-permute-done((bf16[4,128,384]{2,1,0:T(8,128)(2,1)S(1)}, bf16[4,128,384]{2,1,0:T(8,128)(2,1)S(1)}, u32[]{:S(2)}, u32[]{:S(2)}) %collective-permute-start.17) | collective-permute-done | bytes 393248 | tf_op jit(solution)/shard_map/ppermute | solution.py:287
  68.7 2.9 %collective-permute-done.18.two_ref = bf16[4,128,384]{2,1,0:T(8,128)(2,1)S(1)} collective-permute-done((bf16[4,128,384]{2,1,0:T(8,128)(2,1)S(1)}, bf16[4,128,384]{2,1,0:T(8,128)(2,1)S(1)}, u32[]{:S(2)}, u32[]{:S(2)}) %collective-permute-start.18) | collective-permute-done | bytes 393248 | tf_op jit(solution)/shard_map/ppermute | solution.py:287
  71.6 3.9 %collective-permute-done.19.three_ref = bf16[4,128,384]{2,1,0:T(8,128)(2,1)S(1)} collective-permute-done((bf16[4,128,384]{2,1,0:T(8,128)(2,1)S(1)}, bf16[4,128,384]{2,1,0:T(8,128)(2,1)S(1)}, u32[]{:S(2)}, u32[]{:S(2)}) %collective-permute-start.19) | collective-permute-done | bytes 393248 | tf_op jit(solution)/shard_map/ppermute | solution.py:287
  75.7 2.9 %collective-permute-start.22 = (bf16[128,384]{1,0:T(8,128)(2,1)S(1)}, bf16[128,384]{1,0:T(8,128)(2,1)S(1)}, u32[]{:S(2)}, u32[]{:S(2)}) collective-permute-start(bf16[128,384]{1,0:T(8,128)(2,1)S(1)} %get-tuple-element.36), channel_id=1, source_target_pairs={{0,12},{1,13},{2,14},{3,15},{4,0},{5,1},{6,2},{7,3},{8,4},{9,5},{1... | collective-permute-start | bytes 294920 | tf_op jit(solution)/shard_map/ppermute | solution.py:287
  81.8 2.9 %collective-permute-done.21 = bf16[128,384]{1,0:T(8,128)(2,1)S(1)} collective-permute-done((bf16[128,384]{1,0:T(8,128)(2,1)S(1)}, bf16[128,384]{1,0:T(8,128)(2,1)S(1)}, u32[]{:S(2)}, u32[]{:S(2)}) %collective-permute-start.21) | collective-permute-done | bytes 98336 | tf_op jit(solution)/shard_map/ppermute | solution.py:287
  87.5 3.1 %collective-permute-done.25 = bf16[128,384]{1,0:T(8,128)(2,1)S(1)} collective-permute-done((bf16[128,384]{1,0:T(8,128)(2,1)S(1)}, bf16[128,384]{1,0:T(8,128)(2,1)S(1)}, u32[]{:S(2)}, u32[]{:S(2)}) %collective-permute-start.25) | collective-permute-done | bytes 98336 | tf_op jit(solution)/shard_map/ppermute | solution.py:287
  92.6 3.8 %collective-permute-done.23 = bf16[128,384]{1,0:T(8,128)(2,1)S(1)} collective-permute-done((bf16[128,384]{1,0:T(8,128)(2,1)S(1)}, bf16[128,384]{1,0:T(8,128)(2,1)S(1)}, u32[]{:S(2)}, u32[]{:S(2)}) %collective-permute-start.23) | collective-permute-done | bytes 98336 | tf_op jit(solution)/shard_map/ppermute | solution.py:287
  100.6 3.6 %collective-permute-done.26.refs_1_ = bf16[4,128,384]{2,1,0:T(8,128)(2,1)S(1)} collective-permute-done((bf16[4,128,384]{2,1,0:T(8,128)(2,1)S(1)}, bf16[4,128,384]{2,1,0:T(8,128)(2,1)S(1)}, u32[]{:S(2)}, u32[]{:S(2)}) %collective-permute-start.26) | collective-permute-done | bytes 393248 | tf_op jit(solution)/shard_map/ppermute | solution.py:287
  104.3 2.4 %collective-permute-done.27.refs_2_ = bf16[4,128,384]{2,1,0:T(8,128)(2,1)S(1)} collective-permute-done((bf16[4,128,384]{2,1,0:T(8,128)(2,1)S(1)}, bf16[4,128,384]{2,1,0:T(8,128)(2,1)S(1)}, u32[]{:S(2)}, u32[]{:S(2)}) %collective-permute-start.27) | collective-permute-done | bytes 393248 | tf_op jit(solution)/shard_map/ppermute | solution.py:287
  106.7 4.0 %collective-permute-done.28.refs_3_ = bf16[4,128,384]{2,1,0:T(8,128)(2,1)S(1)} collective-permute-done((bf16[4,128,384]{2,1,0:T(8,128)(2,1)S(1)}, bf16[4,128,384]{2,1,0:T(8,128)(2,1)S(1)}, u32[]{:S(2)}, u32[]{:S(2)}) %collective-permute-start.28) | collective-permute-done | bytes 393248 | tf_op jit(solution)/shard_map/ppermute | solution.py:287
  110.7 3.8 %later_in.1.hidden_ref = bf16[12,128,128]{2,1,0:T(8,128)(2,1)S(1)} custom-call(s32[5]{0:T(128)S(1)} %stack.44.place_ref, s32[16,128]{1,0:T(8,128)S(1)} %bitcast.31, f32[48,1,128]{2,1,0:T(1,128)S(1)} %get-tuple-element.53.gain_ref, bf16[4,128,384]{2,1,0:T(8,128)(2,1)S(1)} %pad_maximum_fusion.1.refs_0_, ...), custom_call_target="tpu_custom_call" | custom-call | flops 2147483648 | bytes 12582912 | tf_op jit(solution)/shard_map/later_in/pallas_call | solution.py:241
  114.5 3.6 %project_out.3 = (bf16[4,128,384]{2,1,0:T(8,128)(2,1)S(1)}, bf16[4,128,384]{2,1,0:T(8,128)(2,1)S(1)}, bf16[4,128,384]{2,1,0:T(8,128)(2,1)S(1)}, bf16[4,128,384]{2,1,0:T(8,128)(2,1)S(1)}) custom-call(s32[5]{0:T(128)S(1)} %stack.44.place_ref, s32[16,128]{1,0:T(8,128)S(1)} %bitcast.32, bf16[12,128,128]{2,1,0:T(8,128)(2,1)S(1)} %later_in.1.hidden_ref, ...), custom_call_target="tpu_custom_call" | custom-call | flops 2147483648 | bytes 8388608 | tf_op jit(solution)/shard_map/project_out/pallas_call | solution.py:258
  121.5 4.6 %collective-permute-done.36.one_ref = bf16[4,128,384]{2,1,0:T(8,128)(2,1)S(1)} collective-permute-done((bf16[4,128,384]{2,1,0:T(8,128)(2,1)S(1)}, bf16[4,128,384]{2,1,0:T(8,128)(2,1)S(1)}, u32[]{:S(2)}, u32[]{:S(2)}) %collective-permute-start.36) | collective-permute-done | bytes 393248 | tf_op jit(solution)/shard_map/ppermute | solution.py:287
  127.7 6.2 %collective-permute-done.38.three_ref = bf16[4,128,384]{2,1,0:T(8,128)(2,1)S(1)} collective-permute-done((bf16[4,128,384]{2,1,0:T(8,128)(2,1)S(1)}, bf16[4,128,384]{2,1,0:T(8,128)(2,1)S(1)}, u32[]{:S(2)}, u32[]{:S(2)}) %collective-permute-start.38) | collective-permute-done | bytes 393248 | tf_op jit(solution)/shard_map/ppermute | solution.py:287
  136.2 2.6 %collective-permute-done.41 = bf16[128,384]{1,0:T(8,128)(2,1)S(1)} collective-permute-done((bf16[128,384]{1,0:T(8,128)(2,1)S(1)}, bf16[128,384]{1,0:T(8,128)(2,1)S(1)}, u32[]{:S(2)}, u32[]{:S(2)}) %collective-permute-start.41) | collective-permute-done | bytes 98336 | tf_op jit(solution)/shard_map/ppermute | solution.py:287
  (115 shorter events, 54.9 us)
Async XLA Ops:
  3.0 10.3 %collective-permute-start.2 = (bf16[8,128,128]{2,1,0:T(8,128)(2,1)S(1)}, bf16[8,128,128]{2,1,0:T(8,128)(2,1)S(1)}, u32[]{:S(2)}, u32[]{:S(2)}) collective-permute-start(bf16[8,128,128]{2,1,0:T(8,128)(2,1)S(1)} %broadcast_select_fusion.3.refs_0_), channel_id=1, source_target_pairs={{0,16},{16,32},{32,48},{48,64},{64,80},{80,96},{96,112},{112,0},{1... | collective-permute-start | bytes 786440 | tf_op jit(solution)/shard_map/ppermute | solution.py:283
  5.9 10.1 %collective-permute-start.10 = (bf16[8,128,128]{2,1,0:T(8,128)(2,1)S(1)}, bf16[8,128,128]{2,1,0:T(8,128)(2,1)S(1)}, u32[]{:S(2)}, u32[]{:S(2)}) collective-permute-start(bf16[8,128,128]{2,1,0:T(8,128)(2,1)S(1)} %broadcast_select_fusion.2.refs_0_), channel_id=1, source_target_pairs={{0,16},{16,32},{32,48},{48,64},{64,80},{80,96},{96,112},{112,0},{1... | collective-permute-start | bytes 786440 | tf_op jit(solution)/shard_map/ppermute | solution.py:283
  18.7 23.5 %collective-permute-start.29 = (bf16[16,128,128]{2,1,0:T(8,128)(2,1)}, bf16[16,128,128]{2,1,0:T(8,128)(2,1)}, u32[]{:S(2)}, u32[]{:S(2)}) collective-permute-start(bf16[16,128,128]{2,1,0:T(8,128)(2,1)} %pad_maximum_fusion.refs_4_.refs_0_), channel_id=1, source_target_pairs={{0,16},{16,32},{32,48},{48,64},{64,80},{80,96},{96,112},{112,0},{1... | collective-permute-start | bytes 1572872 | tf_op jit(solution)/shard_map/ppermute | solution.py:283
  20.9 11.3 %collective-permute-start.4 = (bf16[8,128,128]{2,1,0:T(8,128)(2,1)}, bf16[8,128,128]{2,1,0:T(8,128)(2,1)}, u32[]{:S(2)}, u32[]{:S(2)}) collective-permute-start(bf16[8,128,128]{2,1,0:T(8,128)(2,1)} %collective-permute-done.3.refs_2_), channel_id=1, source_target_pairs={{0,16},{16,32},{32,48},{48,64},{64,80},{80,96},{96,112},{112,0},{1... | collective-permute-start | bytes 786440 | tf_op jit(solution)/shard_map/ppermute | solution.py:283
  21.5 10.7 %collective-permute-start.6 = (bf16[8,128,128]{2,1,0:T(8,128)(2,1)S(1)}, bf16[8,128,128]{2,1,0:T(8,128)(2,1)S(1)}, u32[]{:S(2)}, u32[]{:S(2)}) collective-permute-start(bf16[8,128,128]{2,1,0:T(8,128)(2,1)S(1)} %collective-permute-done.2.refs_1_), channel_id=1, source_target_pairs={{0,128},{16,144},{32,160},{48,176},{64,192},{80,208},{96,224},{112... | collective-permute-start | bytes 786440 | tf_op jit(solution)/shard_map/ppermute | solution.py:283
  23.6 18.1 %collective-permute-start.7 = (bf16[8,128,128]{2,1,0:T(8,128)(2,1)}, bf16[8,128,128]{2,1,0:T(8,128)(2,1)}, u32[]{:S(2)}, u32[]{:S(2)}) collective-permute-start(bf16[8,128,128]{2,1,0:T(8,128)(2,1)} %collective-permute-done.3.refs_2_), channel_id=1, source_target_pairs={{0,128},{16,144},{32,160},{48,176},{64,192},{80,208},{96,224},{112... | collective-permute-start | bytes 786440 | tf_op jit(solution)/shard_map/ppermute | solution.py:283
  23.9 18.2 %collective-permute-start.12 = (bf16[8,128,128]{2,1,0:T(8,128)(2,1)}, bf16[8,128,128]{2,1,0:T(8,128)(2,1)}, u32[]{:S(2)}, u32[]{:S(2)}) collective-permute-start(bf16[8,128,128]{2,1,0:T(8,128)(2,1)} %collective-permute-done.11.refs_2_), channel_id=1, source_target_pairs={{0,16},{16,32},{32,48},{48,64},{64,80},{80,96},{96,112},{112,0},{1... | collective-permute-start | bytes 786440 | tf_op jit(solution)/shard_map/ppermute | solution.py:283
  32.2 11.9 %collective-permute-start.5 = (bf16[8,128,128]{2,1,0:T(8,128)(2,1)}, bf16[8,128,128]{2,1,0:T(8,128)(2,1)}, u32[]{:S(2)}, u32[]{:S(2)}) collective-permute-start(bf16[8,128,128]{2,1,0:T(8,128)(2,1)} %collective-permute-done.4.refs_3_), channel_id=1, source_target_pairs={{0,16},{16,32},{32,48},{48,64},{64,80},{80,96},{96,112},{112,0},{1... | collective-permute-start | bytes 786440 | tf_op jit(solution)/shard_map/ppermute | solution.py:283
  32.9 14.7 %collective-permute-start.8 = (bf16[8,128,128]{2,1,0:T(8,128)(2,1)}, bf16[8,128,128]{2,1,0:T(8,128)(2,1)}, u32[]{:S(2)}, u32[]{:S(2)}) collective-permute-start(bf16[8,128,128]{2,1,0:T(8,128)(2,1)} %collective-permute-done.4.refs_3_), channel_id=1, source_target_pairs={{0,128},{16,144},{32,160},{48,176},{64,192},{80,208},{96,224},{112... | collective-permute-start | bytes 786440 | tf_op jit(solution)/shard_map/ppermute | solution.py:283
  35.7 13.4 %all-to-all-start = ((s32[16,1,128]{2,1,0:T(1,128)}), s32[16,1,128]{2,1,0:T(1,128)S(1)}, u32[]{:S(2)}, u32[]{:S(2)}) async-start(s32[16,1,128]{2,1,0:T(1,128)} %broadcast_in_dim.10), calls=%async_computation | async-start | bytes 16384 | tf_op jit(solution)/shard_map/all_to_all | solution.py:367
  41.7 15.6 %collective-permute-start.14 = (bf16[8,128,128]{2,1,0:T(8,128)(2,1)}, bf16[8,128,128]{2,1,0:T(8,128)(2,1)}, u32[]{:S(2)}, u32[]{:S(2)}) collective-permute-start(bf16[8,128,128]{2,1,0:T(8,128)(2,1)} %copy-done.5), channel_id=1, source_target_pairs={{0,128},{16,144},{32,160},{48,176},{64,192},{80,208},{96,224},{112... | collective-permute-start | bytes 786440 | tf_op jit(solution)/shard_map/ppermute | solution.py:283
  42.1 15.2 %collective-permute-start.15 = (bf16[8,128,128]{2,1,0:T(8,128)(2,1)}, bf16[8,128,128]{2,1,0:T(8,128)(2,1)}, u32[]{:S(2)}, u32[]{:S(2)}) collective-permute-start(bf16[8,128,128]{2,1,0:T(8,128)(2,1)} %collective-permute-done.11.refs_2_), channel_id=1, source_target_pairs={{0,128},{16,144},{32,160},{48,176},{64,192},{80,208},{96,224},{112... | collective-permute-start | bytes 786440 | tf_op jit(solution)/shard_map/ppermute | solution.py:283
  42.2 15.1 %collective-permute-start.13 = (bf16[8,128,128]{2,1,0:T(8,128)(2,1)}, bf16[8,128,128]{2,1,0:T(8,128)(2,1)}, u32[]{:S(2)}, u32[]{:S(2)}) collective-permute-start(bf16[8,128,128]{2,1,0:T(8,128)(2,1)} %collective-permute-done.12.refs_3_), channel_id=1, source_target_pairs={{0,16},{16,32},{32,48},{48,64},{64,80},{80,96},{96,112},{112,0},{1... | collective-permute-start | bytes 786440 | tf_op jit(solution)/shard_map/ppermute | solution.py:283
  44.1 13.2 %collective-permute-start.16 = (bf16[8,128,128]{2,1,0:T(8,128)(2,1)}, bf16[8,128,128]{2,1,0:T(8,128)(2,1)}, u32[]{:S(2)}, u32[]{:S(2)}) collective-permute-start(bf16[8,128,128]{2,1,0:T(8,128)(2,1)} %collective-permute-done.12.refs_3_), channel_id=1, source_target_pairs={{0,128},{16,144},{32,160},{48,176},{64,192},{80,208},{96,224},{112... | collective-permute-start | bytes 786440 | tf_op jit(solution)/shard_map/ppermute | solution.py:283
  47.6 32.2 %collective-permute-start.30 = (bf16[16,128,128]{2,1,0:T(8,128)(2,1)}, bf16[16,128,128]{2,1,0:T(8,128)(2,1)S(1)}, u32[]{:S(2)}, u32[]{:S(2)}) collective-permute-start(bf16[16,128,128]{2,1,0:T(8,128)(2,1)} %collective-permute-done.29.refs_5_.refs_1_), channel_id=1, source_target_pairs={{0,16},{16,32},{32,48},{48,64},{64,80},{80,96},{96,112},{112,0},{1... | collective-permute-start | bytes 1572872 | tf_op jit(solution)/shard_map/ppermute | solution.py:283
  63.5 12.0 %collective-permute-start.19 = (bf16[4,128,384]{2,1,0:T(8,128)(2,1)S(1)}, bf16[4,128,384]{2,1,0:T(8,128)(2,1)S(1)}, u32[]{:S(2)}, u32[]{:S(2)}) collective-permute-start(bf16[4,128,384]{2,1,0:T(8,128)(2,1)S(1)} %get-tuple-element.32), channel_id=1, source_target_pairs={{0,3},{1,0},{2,1},{3,2},{4,7},{5,4},{6,5},{7,6},{8,11},{9,8},{10,9... | collective-permute-start | bytes 1179656 | tf_op jit(solution)/shard_map/ppermute | solution.py:287
  79.8 10.7 %collective-permute-start.31 = (bf16[16,128,128]{2,1,0:T(8,128)(2,1)S(1)}, bf16[16,128,128]{2,1,0:T(8,128)(2,1)S(1)}, u32[]{:S(2)}, u32[]{:S(2)}) collective-permute-start(bf16[16,128,128]{2,1,0:T(8,128)(2,1)S(1)} %collective-permute-done.30.refs_6_.refs_2_), channel_id=1, source_target_pairs={{0,16},{16,32},{32,48},{48,64},{64,80},{80,96},{96,112},{112,0},{1... | collective-permute-start | bytes 1572872 | tf_op jit(solution)/shard_map/ppermute | solution.py:283
  80.4 16.9 %collective-permute-start.33 = (bf16[16,128,128]{2,1,0:T(8,128)(2,1)}, bf16[16,128,128]{2,1,0:T(8,128)(2,1)S(1)}, u32[]{:S(2)}, u32[]{:S(2)}) collective-permute-start(bf16[16,128,128]{2,1,0:T(8,128)(2,1)} %collective-permute-done.29.refs_5_.refs_1_), channel_id=1, source_target_pairs={{0,128},{16,144},{32,160},{48,176},{64,192},{80,208},{96,224},{112... | collective-permute-start | bytes 1572872 | tf_op jit(solution)/shard_map/ppermute | solution.py:283
  81.8 16.9 %collective-permute-start.34 = (bf16[16,128,128]{2,1,0:T(8,128)(2,1)S(1)}, bf16[16,128,128]{2,1,0:T(8,128)(2,1)S(1)}, u32[]{:S(2)}, u32[]{:S(2)}) collective-permute-start(bf16[16,128,128]{2,1,0:T(8,128)(2,1)S(1)} %collective-permute-done.30.refs_6_.refs_2_), channel_id=1, source_target_pairs={{0,128},{16,144},{32,160},{48,176},{64,192},{80,208},{96,224},{112... | collective-permute-start | bytes 1572872 | tf_op jit(solution)/shard_map/ppermute | solution.py:283
  90.5 20.2 %collective-permute-start.32 = (bf16[16,128,128]{2,1,0:T(8,128)(2,1)S(1)}, bf16[16,128,128]{2,1,0:T(8,128)(2,1)S(1)}, u32[]{:S(2)}, u32[]{:S(2)}) collective-permute-start(bf16[16,128,128]{2,1,0:T(8,128)(2,1)S(1)} %collective-permute-done.31.refs_7_.refs_3_), channel_id=1, source_target_pairs={{0,16},{16,32},{32,48},{48,64},{64,80},{80,96},{96,112},{112,0},{1... | collective-permute-start | bytes 1572872 | tf_op jit(solution)/shard_map/ppermute | solution.py:283
  92.6 18.1 %collective-permute-start.35 = (bf16[16,128,128]{2,1,0:T(8,128)(2,1)S(1)}, bf16[16,128,128]{2,1,0:T(8,128)(2,1)S(1)}, u32[]{:S(2)}, u32[]{:S(2)}) collective-permute-start(bf16[16,128,128]{2,1,0:T(8,128)(2,1)S(1)} %collective-permute-done.31.refs_7_.refs_3_), channel_id=1, source_target_pairs={{0,128},{16,144},{32,160},{48,176},{64,192},{80,208},{96,224},{112... | collective-permute-start | bytes 1572872 | tf_op jit(solution)/shard_map/ppermute | solution.py:283
  98.7 12.0 %collective-permute-start.28 = (bf16[4,128,384]{2,1,0:T(8,128)(2,1)S(1)}, bf16[4,128,384]{2,1,0:T(8,128)(2,1)S(1)}, u32[]{:S(2)}, u32[]{:S(2)}) collective-permute-start(bf16[4,128,384]{2,1,0:T(8,128)(2,1)S(1)} %pad_maximum_fusion.1.refs_0_), channel_id=1, source_target_pairs={{0,3},{1,0},{2,1},{3,2},{4,7},{5,4},{6,5},{7,6},{8,11},{9,8},{10,9... | collective-permute-start | bytes 1179656 | tf_op jit(solution)/shard_map/ppermute | solution.py:287
  118.3 9.5 %collective-permute-start.37 = (bf16[4,128,384]{2,1,0:T(8,128)(2,1)S(1)}, bf16[4,128,384]{2,1,0:T(8,128)(2,1)S(1)}, u32[]{:S(2)}, u32[]{:S(2)}) collective-permute-start(bf16[4,128,384]{2,1,0:T(8,128)(2,1)S(1)} %get-tuple-element.43), channel_id=1, source_target_pairs={{0,2},{1,3},{2,0},{3,1},{4,6},{5,7},{6,4},{7,5},{8,10},{9,11},{10,... | collective-permute-start | bytes 1179656 | tf_op jit(solution)/shard_map/ppermute | solution.py:287
  119.8 14.1 %collective-permute-start.38 = (bf16[4,128,384]{2,1,0:T(8,128)(2,1)S(1)}, bf16[4,128,384]{2,1,0:T(8,128)(2,1)S(1)}, u32[]{:S(2)}, u32[]{:S(2)}) collective-permute-start(bf16[4,128,384]{2,1,0:T(8,128)(2,1)S(1)} %get-tuple-element.44), channel_id=1, source_target_pairs={{0,3},{1,0},{2,1},{3,2},{4,7},{5,4},{6,5},{7,6},{8,11},{9,8},{10,9... | collective-permute-start | bytes 1179656 | tf_op jit(solution)/shard_map/ppermute | solution.py:287
  (35 other events, 285.8 us)
where the time goes:
time: 145 us; the launch traced here: 144 us
  waiting for transfers between devices  70.6 us (49%)
  starting transfers between devices  41.7 us (29%)
  Pallas kernels  16.4 us (11%)
  local copies, waits for them, and re-layouts  8.33 us (6%)
  other arithmetic  4.98 us (3%)
  between operations  1.6 us (1%)
    ppermute x18, waiting for transfers between devices, on_cols(): return lax.ppermute(value, ('section', 'col'), perm)  50.4 us
    ppermute x18, starting transfers between devices, on_cols(): return lax.ppermute(value, ('section', 'col'), perm)  20.6 us
    ppermute x25, waiting for transfers between devices, on_rows(): return lax.ppermute(value, ('section', 'row'), perm)  19.2 us
    ppermute x25, starting transfers between devices, on_rows(): return lax.ppermute(value, ('section', 'row'), perm)  15.3 us
    unnamed x30, local copies, waits for them, and re-layouts  7.55 us
    pallas_call x2, Pallas kernels, project_out(): pl.pallas_call(functools.partial(out_kernel, phase), in_specs=[smem(), sm...  7.09 us
    all_to_all x1, starting transfers between devices, shards(): lax.all_to_all(jnp.broadcast_to(own_meta, (2 * GRID_ROWS, 1, BLK)), ('sec...  5.84 us
    pallas_call x1, Pallas kernels, first_in(): pl.pallas_call(first_in_kernel, in_specs=[smem(), smem(), vmem()] + [anyw...  3.94 us
  transfers between devices with their start and end apart: 44, of which 26 were waited for; matrix products, arithmetic and copies ran while one was open for 3% of the time, Pallas kernels for 6%

commit v1 on v0

--- a/solution.py
+++ b/solution.py
@@ -45,9 +45,10 @@
 
 
 def fetch(cells, offset, weights, sems):
+    size = SLOTS * BLK
     copies = [
         pltpu.make_async_copy(
-            cell.at[pl.ds(offset, SLOTS)], weights.at[pl.ds(i * SLOTS, SLOTS)], sems.at[i]
+            cell.at[pl.ds(offset, size)], weights.at[pl.ds(i * size, size)], sems.at[i]
         )
         for i, cell in enumerate(cells)
     ]
@@ -58,11 +59,11 @@
 
 def list_blocks(place_ref, meta_ref, phase, inward, blocks):
     sign = 1 - 2 * place_ref[0]
+    start = 0 if inward else SLOTS + 1
     used = 0
     for i, offset in enumerate(OFFSETS):
         row = lax.rem(place_ref[4] + sign * offset + 2 * GRID_ROWS, GRID_ROWS)
         base = phase * GRID_ROWS + row
-        start = 0 if inward else SLOTS + 1
         for n in range(SLOTS):
             slot = meta_ref[base, start + n]
             model, hid = row * DBL + slot // FBL, lax.rem(slot, FBL)
@@ -83,7 +84,7 @@
         products = [
             jnp.dot(
                 dense[blocks[1, at + u]],
-                weights[blocks[0, at + u]],
+                weights[pl.ds(pl.multiple_of(blocks[0, at + u] * BLK, BLK), BLK), :],
                 preferred_element_type=F32,
             )
             for u in range(UNROLL)
@@ -110,8 +111,9 @@
     for k in range(BLOCKS):
         part = x_ref[0, :, k * BLK : (k + 1) * BLK].astype(F32)
         normed_ref[k] = (part * scale * gain_ref[k]).astype(BF16)
-    start = pl.multiple_of(place_ref[1] * WIDTH, BLK)
-    own_ref[...] = x_ref[0, :, pl.ds(start, WIDTH)]
+    for e in range(SIDE):
+        start = pl.multiple_of(chunk_of(place_ref, place_ref[2], e) * WIDTH, BLK)
+        own_ref[e] = x_ref[0, :, pl.ds(start, WIDTH)]
 
 
 def first_in_kernel(place_ref, meta_ref, normed_ref, *refs):
@@ -142,7 +144,7 @@
     scale = lax.rsqrt(mean + EPSILON)
     for d in range(SIDE):
         for e in range(SIDE):
-            chunk = chunk_of(place_ref, digit(place_ref[2] - d), digit(place_ref[3] - e))
+            chunk = chunk_of(place_ref, digit(place_ref[2] - d), e)
             for q in range(CHUNK):
                 k = chunk * CHUNK + q
                 part = bundles[d][e, :, q * BLK : (q + 1) * BLK].astype(F32)
@@ -158,7 +160,7 @@
     cells = refs[:GRID_ROWS]
     sends = refs[GRID_ROWS : GRID_ROWS + SIDE]
     total, weights, blocks, sems = refs[GRID_ROWS + SIDE :]
-    copies = fetch(cells, phase * SLOTS, weights, sems)
+    copies = fetch(cells, phase * SLOTS * BLK, weights, sems)
     used = list_blocks(place_ref, meta_ref, phase, False, blocks)
     total[...] = jnp.zeros_like(total)
     for copy in copies:
@@ -166,20 +168,33 @@
     block_sum(hidden_ref, weights, blocks, used, total)
     for d in range(SIDE):
         for e in range(SIDE):
-            chunk = chunk_of(place_ref, digit(place_ref[2] + d), digit(place_ref[3] + e))
+            chunk = chunk_of(place_ref, digit(place_ref[2] + d), e)
             for q in range(CHUNK):
                 sends[d][e, :, q * BLK : (q + 1) * BLK] = total[chunk * CHUNK + q].astype(BF16)
 
 
-def sum_kernel(own_ref, one_ref, two_ref, three_ref, *sums):
+def sum_of(refs, index):
+    value = refs[0][index].astype(F32)
+    for ref in refs[1:]:
+        value = value + ref[index].astype(F32)
+    return value
+
+
+def whole_sum_kernel(*refs):
     for e in range(SIDE):
-        value = (
-            own_ref[e].astype(F32)
-            + one_ref[e].astype(F32)
-            + two_ref[e].astype(F32)
-            + three_ref[e].astype(F32)
-        )
-        sums[e][...] = value.astype(sums[e].dtype)
+        refs[-1][e] = sum_of(refs[:-1], e).astype(BF16)
+
+
+def merge_kernel(place_ref, *refs):
+    bundle_ref, piece_ref = refs[-2:]
+    for e in range(SIDE):
+        bundle_ref[e] = sum_of(refs[:-2], e).astype(BF16)
+    piece_ref[...] = bundle_ref[place_ref[3]]
+
+
+def piece_sum_kernel(place_ref, *refs):
+    for e, piece in enumerate(refs[SIDE:]):
+        piece[...] = sum_of(refs[:SIDE], digit(place_ref[3] + e)).astype(piece.dtype)
 
 
 def cost(blocks, moved):
@@ -187,7 +202,7 @@
 
 
 WORK = [
-    pltpu.VMEM((GRID_ROWS * SLOTS, BLK, BLK), BF16),
+    pltpu.VMEM((GRID_ROWS * SLOTS * BLK, BLK), BF16),
     pltpu.SMEM((3, GRID_ROWS * SLOTS + 2 * SLOTS), jnp.int32),
     pltpu.SemaphoreType.DMA((GRID_ROWS,)),
 ]
@@ -210,10 +225,10 @@
             ],
             out_specs=[
                 pl.BlockSpec((BLOCKS, TOK, BLK), lambda i, micro, place: (0, 0, 0)),
-                pl.BlockSpec((TOK, WIDTH), lambda i, micro, place: (0, 0)),
+                pl.BlockSpec((SIDE, TOK, WIDTH), lambda i, micro, place: (0, 0, 0)),
             ],
         ),
-        out_shape=[NORMED, PIECE],
+        out_shape=[NORMED, BUNDLE],
         cost_estimate=cost(1, 6 << 20),
         compiler_params=PARAMS,
         name="first_norm",
@@ -267,16 +282,15 @@
     )(place, meta, hidden, *cells)
 
 
-def sum_bundles(bundles):
+def add_up(kernel, place, bundles, outs):
     return pl.pallas_call(
-        sum_kernel,
-        in_specs=[vmem()] * SIDE,
-        out_specs=[vmem()] * SIDE,
-        out_shape=[jax.ShapeDtypeStruct((TOK, WIDTH), F32)] + [PIECE] * (SIDE - 1),
+        kernel,
+        in_specs=([smem()] if place is not None else []) + [vmem()] * len(bundles),
+        out_specs=[vmem()] * len(outs),
+        out_shape=outs,
         cost_estimate=cost(0, 2 << 20),
         compiler_params=PARAMS,
-        name="sum_bundles",
-    )(*bundles)
+    )(*([place] if place is not None else []), *bundles)
 
 
 def on_rows(value, perm):
@@ -316,33 +330,12 @@
     return ring + other
 
 
-def reduce_columns(bundles):
+def spread(values, first):
     landed = []
     for d in range(1, SIDE):
-        landed.append(on_cols(bundles[d], column_shift(True, d)))
-    sums = sum_bundles([bundles[0]] + landed)
-    last = []
-    for e in range(1, SIDE):
-        last.append(on_cols(sums[e], column_shift(False, e)))
-    return sums[0], last
-
-
-def gather_columns(piece):
-    pieces = [piece]
-    for e in range(1, SIDE):
-        pieces.append(on_cols(piece, column_shift(False, e)))
-    bundle = jnp.stack(pieces)
-    bundles = [bundle]
-    for d in range(1, SIDE):
-        bundles.append(on_cols(bundle, column_shift(True, d)))
-    return bundles
-
-
-def add_branch(piece, own_sum, last):
-    total = own_sum
-    for value in last:
-        total = total + value.astype(F32)
-    return (piece.astype(F32) + total).astype(BF16)
+        value = values[d] if isinstance(values, (list, tuple)) else values
+        landed.append(on_cols(value, column_shift(first, d)))
+    return landed
 
 
 def shards(inputs, norm_gain, w_in, w_in_slot, w_in_count, w_out, w_out_slot, w_out_count):
@@ -371,40 +364,50 @@
         0,
         tiled=True,
     ).reshape(2 * GRID_ROWS, BLK)
-    own_in = w_in.reshape(SLOTS, BLK, BLK)
-    own_out = w_out.reshape(SLOTS, BLK, BLK)
+    own_in = w_in.reshape(SLOTS * BLK, BLK)
+    own_out = w_out.reshape(SLOTS * BLK, BLK)
+    own_gain = norm_gain.reshape(BLOCKS, 1, BLK)
     other_in = on_rows(own_in, SWAP)
     other_out = on_rows(own_out, SWAP)
+    other_gain = on_rows(own_gain, SWAP)
     mine = core == 0
     cells_in = ring_gather(jnp.where(mine, own_in, other_in))
     cells_out = ring_gather(jnp.where(mine, own_out, other_out))
     own_in, own_out, other_in, other_out, _ = lax.optimization_barrier(
-        (own_in, own_out, other_in, other_out, cells_in[1])
+        (own_in, own_out, other_in, other_out, cells_in[2])
     )
     later_cells = ring_gather(
         jnp.concatenate(
             [jnp.where(mine, other_in, own_in), jnp.where(mine, other_out, own_out)]
         ),
     )
-
-    own_gain = norm_gain.reshape(BLOCKS, 1, BLK)
-    other_gain = on_rows(own_gain, SWAP)
     gains = [jnp.where(mine, own_gain, other_gain), jnp.where(mine, other_gain, own_gain)]
 
-    normed, piece = first_norm(micro, place, inputs, gains[0])
+    normed, own_x = first_norm(micro, place, inputs, gains[0])
     hidden = first_in(place, meta, normed, cells_in)
     bundles = project_out(0, place, meta, hidden, cells_out)
-    own_sum, last = reduce_columns(bundles)
-    middle = add_branch(piece, own_sum, last)
-
-    bundles = gather_columns(middle)
+    landed = spread(bundles, True)
+    sums = add_up(whole_sum_kernel, None, [bundles[0]] + landed, [BUNDLE])[0]
+    landed = spread(sums, False)
+    middle, piece = add_up(merge_kernel, place, [own_x, sums] + landed, [BUNDLE, PIECE])
+
+    bundles = [middle] + spread(middle, True)
     hidden = later_in(place, meta, gains[1], bundles, later_cells)
     bundles = project_out(1, place, meta, hidden, later_cells)
-    own_sum, last = reduce_columns(bundles)
-    final = add_branch(middle, own_sum, last)
-
-    other = on_rows(jnp.where(mine, final, middle), SWAP)
-    return jnp.stack([jnp.where(mine, middle, other), jnp.where(mine, other, final)])[None]
+    landed = spread(bundles, True)
+    sums = add_up(
+        piece_sum_kernel,
+        place,
+        [bundles[0]] + landed,
+        [jax.ShapeDtypeStruct((TOK, WIDTH), F32)] + [PIECE] * (SIDE - 1),
+    )
+    total = sums[0]
+    for value in spread(sums, False):
+        total = total + value.astype(F32)
+    final = (piece.astype(F32) + total).astype(BF16)
+
+    other = on_rows(jnp.where(mine, final, piece), SWAP)
+    return jnp.stack([jnp.where(mine, piece, other), jnp.where(mine, other, final)])[None]
 
 
 def solution(mesh):

time: 145 us -> 145 us (level)
  waiting for transfers between devices: 70.6 us -> 62 us
  local copies, waits for them, and re-layouts: 8.33 us -> 14 us
  starting transfers between devices: 41.7 us -> 43.2 us
    ppermute x18 -> x15, waiting for transfers between devices: 50.4 us -> 44.1 us  [on_cols(): return lax.ppermute(value, ('section', 'col'), perm)]
    unnamed x30 -> x40, local copies, waits for them, and re-layouts: 7.55 us -> 12.5 us
    ppermute x18 -> x15, starting transfers between devices: 20.6 us -> 22.7 us  [on_cols(): return lax.ppermute(value, ('section', 'col'), perm)]
  transfers between devices with their start and end apart: 44 -> 41, of which waited for: 26 -> 22; matrix products, arithmetic and copies ran while one was open for 3% -> 4% of each run, Pallas kernels for 6% -> 7%
where the time goes in v1:
time: 145 us; the launch traced here: 144 us
  waiting for transfers between devices  62 us (43%)
  starting transfers between devices  43.2 us (30%)
  Pallas kernels  17.7 us (12%)
  local copies, waits for them, and re-layouts  14 us (10%)
  other arithmetic  5.36 us (4%)
  between operations  1.55 us (1%)
    ppermute x15, waiting for transfers between devices, on_cols(): return lax.ppermute(value, ('section', 'col'), perm)  44.1 us
    ppermute x15, starting transfers between devices, on_cols(): return lax.ppermute(value, ('section', 'col'), perm)  22.7 us
    ppermute x25, waiting for transfers between devices, on_rows(): return lax.ppermute(value, ('section', 'row'), perm)  17.9 us
    ppermute x25, starting transfers between devices, on_rows(): return lax.ppermute(value, ('section', 'row'), perm)  14.7 us
    unnamed x40, local copies, waits for them, and re-layouts  12.5 us
    pallas_call x2, Pallas kernels, project_out(): pl.pallas_call(functools.partial(out_kernel, phase), in_specs=[smem(), sm...  7.17 us
    all_to_all x1, starting transfers between devices, shards(): lax.all_to_all(jnp.broadcast_to(own_meta, (2 * GRID_ROWS, 1, BLK)), ('sec...  5.84 us
    pallas_call x1, Pallas kernels, later_in(): pl.pallas_call(later_in_kernel, in_specs=[smem(), smem()] + [vmem()] * (1...  3.81 us
  transfers between devices with their start and end apart: 41, of which 22 were waited for; matrix products, arithmetic and copies ran while one was open for 4% of the time, Pallas kernels for 7%

profile of v1, /device:TPU:2, one launch (start us, length us, event | category | flops | bytes accessed | tf_op | source)
XLA Modules:
  0.0 143.8 jit_solution(14991730011765386385)
XLA Ops:
  9.1 4.6 %collective-permute-done.2.refs_1_ = bf16[1024,128]{1,0:T(8,128)(2,1)S(1)} collective-permute-done((bf16[1024,128]{1,0:T(8,128)(2,1)S(1)}, bf16[1024,128]{1,0:T(8,128)(2,1)S(1)}, u32[]{:S(2)}, u32[]{:S(2)}) %collective-permute-start.2) | collective-permute-done | bytes 262176 | tf_op jit(solution)/shard_map/ppermute | solution.py:297
  13.7 2.9 %collective-permute-done.10.refs_1_ = bf16[1024,128]{1,0:T(8,128)(2,1)} collective-permute-done((bf16[1024,128]{1,0:T(8,128)(2,1)S(1)}, bf16[1024,128]{1,0:T(8,128)(2,1)}, u32[]{:S(2)}, u32[]{:S(2)}) %collective-permute-start.10) | collective-permute-done | bytes 262176 | tf_op jit(solution)/shard_map/ppermute | solution.py:297
  16.7 4.8 %collective-permute-done.3.refs_2_ = bf16[1024,128]{1,0:T(8,128)(2,1)} collective-permute-done((bf16[1024,128]{1,0:T(8,128)(2,1)S(1)}, bf16[1024,128]{1,0:T(8,128)(2,1)}, u32[]{:S(2)}, u32[]{:S(2)}) %collective-permute-start.3) | collective-permute-done | bytes 262176 | tf_op jit(solution)/shard_map/ppermute | solution.py:297
  24.9 5.8 %all-to-all-start = ((s32[16,1,128]{2,1,0:T(1,128)}), s32[16,1,128]{2,1,0:T(1,128)S(1)}, u32[]{:S(2)}, u32[]{:S(2)}) async-start(s32[16,1,128]{2,1,0:T(1,128)} %broadcast_in_dim.10), calls=%async_computation | async-start | bytes 16384 | tf_op jit(solution)/shard_map/all_to_all | solution.py:360
  55.4 3.7 %first_in.1.hidden_ref = bf16[12,128,128]{2,1,0:T(8,128)(2,1)S(1)} custom-call(s32[5]{0:T(128)S(1)} %stack.32.place_ref, s32[16,128]{1,0:T(8,128)S(1)} %bitcast.25, bf16[48,128,128]{2,1,0:T(8,128)(2,1)S(1)} %copy-done.7, bf16[1024,128]{1,0:T(8,128)(2,1)S(1)} %copy-done.4, bf16[1024,128]{1,0:T(8,128)(2,1)S(1)} %copy-done.9, ...), custom_call_target="tpu_custom_call" | custom-call | flops 2147483648 | bytes 8388608 | tf_op jit(solution)/shard_map/first_in/pallas_call | solution.py:243
  59.2 3.5 %project_out.2 = (bf16[4,128,384]{2,1,0:T(8,128)(2,1)S(1)}, bf16[4,128,384]{2,1,0:T(8,128)(2,1)S(1)}, bf16[4,128,384]{2,1,0:T(8,128)(2,1)S(1)}, bf16[4,128,384]{2,1,0:T(8,128)(2,1)S(1)}) custom-call(s32[5]{0:T(128)S(1)} %stack.32.place_ref, s32[16,128]{1,0:T(8,128)S(1)} %bitcast.26, bf16[12,128,128]{2,1,0:T(8,128)(2,1)S(1)} %first_in.1.hidden_ref, ...), custom_call_target="tpu_custom_call" | custom-call | flops 2147483648 | bytes 8388608 | tf_op jit(solution)/shard_map/project_out/pallas_call | solution.py:273
  65.4 2.5 %collective-permute-start.19 = (bf16[4,128,384]{2,1,0:T(8,128)(2,1)S(1)}, bf16[4,128,384]{2,1,0:T(8,128)(2,1)S(1)}, u32[]{:S(2)}, u32[]{:S(2)}) collective-permute-start(bf16[4,128,384]{2,1,0:T(8,128)(2,1)S(1)} %get-tuple-element.30), channel_id=1, source_target_pairs={{0,3},{1,0},{2,1},{3,2},{4,7},{5,4},{6,5},{7,6},{8,11},{9,8},{10,9... | collective-permute-start | bytes 1179656 | tf_op jit(solution)/shard_map/ppermute | solution.py:301
  68.3 2.3 %collective-permute-done.17.refs_1_ = bf16[4,128,384]{2,1,0:T(8,128)(2,1)S(1)} collective-permute-done((bf16[4,128,384]{2,1,0:T(8,128)(2,1)S(1)}, bf16[4,128,384]{2,1,0:T(8,128)(2,1)S(1)}, u32[]{:S(2)}, u32[]{:S(2)}) %collective-permute-start.17) | collective-permute-done | bytes 393248 | tf_op jit(solution)/shard_map/ppermute | solution.py:301
  70.6 2.9 %collective-permute-done.18.refs_2_ = bf16[4,128,384]{2,1,0:T(8,128)(2,1)S(1)} collective-permute-done((bf16[4,128,384]{2,1,0:T(8,128)(2,1)S(1)}, bf16[4,128,384]{2,1,0:T(8,128)(2,1)S(1)}, u32[]{:S(2)}, u32[]{:S(2)}) %collective-permute-start.18) | collective-permute-done | bytes 393248 | tf_op jit(solution)/shard_map/ppermute | solution.py:301
  73.5 3.9 %collective-permute-done.19.refs_3_ = bf16[4,128,384]{2,1,0:T(8,128)(2,1)S(1)} collective-permute-done((bf16[4,128,384]{2,1,0:T(8,128)(2,1)S(1)}, bf16[4,128,384]{2,1,0:T(8,128)(2,1)S(1)}, u32[]{:S(2)}, u32[]{:S(2)}) %collective-permute-start.19) | collective-permute-done | bytes 393248 | tf_op jit(solution)/shard_map/ppermute | solution.py:301
  80.3 2.5 %collective-permute-start.21 = (bf16[4,128,384]{2,1,0:T(8,128)(2,1)S(1)}, bf16[4,128,384]{2,1,0:T(8,128)(2,1)S(1)}, u32[]{:S(2)}, u32[]{:S(2)}) collective-permute-start(bf16[4,128,384]{2,1,0:T(8,128)(2,1)S(1)} %shard_map.82.refs_1_), channel_id=1, source_target_pairs={{0,8},{1,9},{2,10},{3,11},{4,12},{5,13},{6,14},{7,15},{8,0},{9,1},... | collective-permute-start | bytes 1179656 | tf_op jit(solution)/shard_map/ppermute | solution.py:301
  82.8 3.8 %collective-permute-done.20.refs_2_ = bf16[4,128,384]{2,1,0:T(8,128)(2,1)S(1)} collective-permute-done((bf16[4,128,384]{2,1,0:T(8,128)(2,1)S(1)}, bf16[4,128,384]{2,1,0:T(8,128)(2,1)S(1)}, u32[]{:S(2)}, u32[]{:S(2)}) %collective-permute-start.20) | collective-permute-done | bytes 393248 | tf_op jit(solution)/shard_map/ppermute | solution.py:301
  89.8 2.1 %collective-permute-done.21.refs_3_ = bf16[4,128,384]{2,1,0:T(8,128)(2,1)S(1)} collective-permute-done((bf16[4,128,384]{2,1,0:T(8,128)(2,1)S(1)}, bf16[4,128,384]{2,1,0:T(8,128)(2,1)S(1)}, u32[]{:S(2)}, u32[]{:S(2)}) %collective-permute-start.21) | collective-permute-done | bytes 393248 | tf_op jit(solution)/shard_map/ppermute | solution.py:301
  91.9 2.5 %collective-permute-done.22.refs_4_ = bf16[4,128,384]{2,1,0:T(8,128)(2,1)S(1)} collective-permute-done((bf16[4,128,384]{2,1,0:T(8,128)(2,1)S(1)}, bf16[4,128,384]{2,1,0:T(8,128)(2,1)S(1)}, u32[]{:S(2)}, u32[]{:S(2)}) %collective-permute-start.22) | collective-permute-done | bytes 393248 | tf_op jit(solution)/shard_map/ppermute | solution.py:301
  99.7 3.6 %collective-permute-done.23.refs_1_ = bf16[4,128,384]{2,1,0:T(8,128)(2,1)S(1)} collective-permute-done((bf16[4,128,384]{2,1,0:T(8,128)(2,1)S(1)}, bf16[4,128,384]{2,1,0:T(8,128)(2,1)S(1)}, u32[]{:S(2)}, u32[]{:S(2)}) %collective-permute-start.23) | collective-permute-done | bytes 393248 | tf_op jit(solution)/shard_map/ppermute | solution.py:301
  103.4 2.4 %collective-permute-done.24.refs_2_ = bf16[4,128,384]{2,1,0:T(8,128)(2,1)S(1)} collective-permute-done((bf16[4,128,384]{2,1,0:T(8,128)(2,1)S(1)}, bf16[4,128,384]{2,1,0:T(8,128)(2,1)S(1)}, u32[]{:S(2)}, u32[]{:S(2)}) %collective-permute-start.24) | collective-permute-done | bytes 393248 | tf_op jit(solution)/shard_map/ppermute | solution.py:301
  105.8 4.1 %collective-permute-done.25.refs_3_ = bf16[4,128,384]{2,1,0:T(8,128)(2,1)S(1)} collective-permute-done((bf16[4,128,384]{2,1,0:T(8,128)(2,1)S(1)}, bf16[4,128,384]{2,1,0:T(8,128)(2,1)S(1)}, u32[]{:S(2)}, u32[]{:S(2)}) %collective-permute-start.25) | collective-permute-done | bytes 393248 | tf_op jit(solution)/shard_map/ppermute | solution.py:301
  109.9 3.8 %later_in.1.hidden_ref = bf16[12,128,128]{2,1,0:T(8,128)(2,1)S(1)} custom-call(s32[5]{0:T(128)S(1)} %stack.32.place_ref, s32[16,128]{1,0:T(8,128)S(1)} %bitcast.27, f32[48,1,128]{2,1,0:T(1,128)S(1)} %copy-done.5, bf16[4,128,384]{2,1,0:T(8,128)(2,1)S(1)} %get-tuple-element.32.refs_0_, bf16[4,128,384]{2,1,0:T(8,128)(2,1)S(1)} %collective-permute-done.23.refs_1_, ...), custom_call_target="tpu_custom_call" | custom-call | flops 2147483648 | bytes 12582912 | tf_op jit(solution)/shard_map/later_in/pallas_call | solution.py:256
  113.7 3.7 %project_out.3 = (bf16[4,128,384]{2,1,0:T(8,128)(2,1)S(1)}, bf16[4,128,384]{2,1,0:T(8,128)(2,1)S(1)}, bf16[4,128,384]{2,1,0:T(8,128)(2,1)S(1)}, bf16[4,128,384]{2,1,0:T(8,128)(2,1)S(1)}) custom-call(s32[5]{0:T(128)S(1)} %stack.32.place_ref, s32[16,128]{1,0:T(8,128)S(1)} %bitcast.28, bf16[12,128,128]{2,1,0:T(8,128)(2,1)S(1)} %later_in.1.hidden_ref, ...), custom_call_target="tpu_custom_call" | custom-call | flops 2147483648 | bytes 8388608 | tf_op jit(solution)/shard_map/project_out/pallas_call | solution.py:273
  120.9 4.3 %collective-permute-done.33.refs_1_ = bf16[4,128,384]{2,1,0:T(8,128)(2,1)S(1)} collective-permute-done((bf16[4,128,384]{2,1,0:T(8,128)(2,1)S(1)}, bf16[4,128,384]{2,1,0:T(8,128)(2,1)S(1)}, u32[]{:S(2)}, u32[]{:S(2)}) %collective-permute-start.33) | collective-permute-done | bytes 393248 | tf_op jit(solution)/shard_map/ppermute | solution.py:301
  127.0 4.2 %collective-permute-done.35.refs_3_ = bf16[4,128,384]{2,1,0:T(8,128)(2,1)S(1)} collective-permute-done((bf16[4,128,384]{2,1,0:T(8,128)(2,1)S(1)}, bf16[4,128,384]{2,1,0:T(8,128)(2,1)S(1)}, u32[]{:S(2)}, u32[]{:S(2)}) %collective-permute-start.35) | collective-permute-done | bytes 393248 | tf_op jit(solution)/shard_map/ppermute | solution.py:301
  131.9 2.6 %collective-permute-start.38 = (bf16[128,384]{1,0:T(8,128)(2,1)S(1)}, bf16[128,384]{1,0:T(8,128)(2,1)S(1)}, u32[]{:S(2)}, u32[]{:S(2)}) collective-permute-start(bf16[128,384]{1,0:T(8,128)(2,1)S(1)} %get-tuple-element.44), channel_id=1, source_target_pairs={{0,12},{1,13},{2,14},{3,15},{4,0},{5,1},{6,2},{7,3},{8,4},{9,5},{1... | collective-permute-start | bytes 294920 | tf_op jit(solution)/shard_map/ppermute | solution.py:301
  135.4 2.3 %collective-permute-done.38 = bf16[128,384]{1,0:T(8,128)(2,1)S(1)} collective-permute-done((bf16[128,384]{1,0:T(8,128)(2,1)S(1)}, bf16[128,384]{1,0:T(8,128)(2,1)S(1)}, u32[]{:S(2)}, u32[]{:S(2)}) %collective-permute-start.38) | collective-permute-done | bytes 98336 | tf_op jit(solution)/shard_map/ppermute | solution.py:301
  137.7 3.0 %collective-permute-done.37 = bf16[128,384]{1,0:T(8,128)(2,1)S(1)} collective-permute-done((bf16[128,384]{1,0:T(8,128)(2,1)S(1)}, bf16[128,384]{1,0:T(8,128)(2,1)S(1)}, u32[]{:S(2)}, u32[]{:S(2)}) %collective-permute-start.37) | collective-permute-done | bytes 98336 | tf_op jit(solution)/shard_map/ppermute | solution.py:301
  (118 shorter events, 60.4 us)
Async XLA Ops:
  3.5 10.3 %collective-permute-start.2 = (bf16[1024,128]{1,0:T(8,128)(2,1)S(1)}, bf16[1024,128]{1,0:T(8,128)(2,1)S(1)}, u32[]{:S(2)}, u32[]{:S(2)}) collective-permute-start(bf16[1024,128]{1,0:T(8,128)(2,1)S(1)} %broadcast_select_fusion.3.refs_0_), channel_id=1, source_target_pairs={{0,16},{16,32},{32,48},{48,64},{64,80},{80,96},{96,112},{112,0},{1... | collective-permute-start | bytes 786440 | tf_op jit(solution)/shard_map/ppermute | solution.py:297
  6.4 10.2 %collective-permute-start.10 = (bf16[1024,128]{1,0:T(8,128)(2,1)S(1)}, bf16[1024,128]{1,0:T(8,128)(2,1)}, u32[]{:S(2)}, u32[]{:S(2)}) collective-permute-start(bf16[1024,128]{1,0:T(8,128)(2,1)S(1)} %broadcast_select_fusion.2.refs_0_), channel_id=1, source_target_pairs={{0,16},{16,32},{32,48},{48,64},{64,80},{80,96},{96,112},{112,0},{1... | collective-permute-start | bytes 786440 | tf_op jit(solution)/shard_map/ppermute | solution.py:297
  16.7 14.7 %collective-permute-start.11 = (bf16[1024,128]{1,0:T(8,128)(2,1)}, bf16[1024,128]{1,0:T(8,128)(2,1)}, u32[]{:S(2)}, u32[]{:S(2)}) collective-permute-start(bf16[1024,128]{1,0:T(8,128)(2,1)} %collective-permute-done.10.refs_1_), channel_id=1, source_target_pairs={{0,16},{16,32},{32,48},{48,64},{64,80},{80,96},{96,112},{112,0},{1... | collective-permute-start | bytes 786440 | tf_op jit(solution)/shard_map/ppermute | solution.py:297
  21.4 11.9 %collective-permute-start.4 = (bf16[1024,128]{1,0:T(8,128)(2,1)}, bf16[1024,128]{1,0:T(8,128)(2,1)}, u32[]{:S(2)}, u32[]{:S(2)}) collective-permute-start(bf16[1024,128]{1,0:T(8,128)(2,1)} %collective-permute-done.3.refs_2_), channel_id=1, source_target_pairs={{0,16},{16,32},{32,48},{48,64},{64,80},{80,96},{96,112},{112,0},{1... | collective-permute-start | bytes 786440 | tf_op jit(solution)/shard_map/ppermute | solution.py:297
  21.4 13.3 %collective-permute-start = (f32[48,1,128]{2,1,0:T(1,128)}, f32[48,1,128]{2,1,0:T(1,128)S(1)}, u32[]{:S(2)}, u32[]{:S(2)}) collective-permute-start(f32[48,1,128]{2,1,0:T(1,128)} %bitcast.33), channel_id=1, source_target_pairs={{0,128},{16,144},{32,160},{48,176},{64,192},{80,208},{96,224},{112... | collective-permute-start | bytes 73736 | tf_op jit(solution)/shard_map/ppermute | solution.py:297
  24.9 23.4 %all-to-all-start = ((s32[16,1,128]{2,1,0:T(1,128)}), s32[16,1,128]{2,1,0:T(1,128)S(1)}, u32[]{:S(2)}, u32[]{:S(2)}) async-start(s32[16,1,128]{2,1,0:T(1,128)} %broadcast_in_dim.10), calls=%async_computation | async-start | bytes 16384 | tf_op jit(solution)/shard_map/all_to_all | solution.py:360
  38.2 21.0 %collective-permute-start.14 = (bf16[1024,128]{1,0:T(8,128)(2,1)}, bf16[1024,128]{1,0:T(8,128)(2,1)}, u32[]{:S(2)}, u32[]{:S(2)}) collective-permute-start(bf16[1024,128]{1,0:T(8,128)(2,1)} %collective-permute-done.10.refs_1_), channel_id=1, source_target_pairs={{0,128},{16,144},{32,160},{48,176},{64,192},{80,208},{96,224},{112... | collective-permute-start | bytes 786440 | tf_op jit(solution)/shard_map/ppermute | solution.py:297
  38.9 29.0 %collective-permute-start.26 = (bf16[2048,128]{1,0:T(8,128)(2,1)}, bf16[2048,128]{1,0:T(8,128)(2,1)}, u32[]{:S(2)}, u32[]{:S(2)}) collective-permute-start(bf16[2048,128]{1,0:T(8,128)(2,1)} %pad_maximum_fusion.refs_4_.refs_0_), channel_id=1, source_target_pairs={{0,16},{16,32},{32,48},{48,64},{64,80},{80,96},{96,112},{112,0},{1... | collective-permute-start | bytes 1572872 | tf_op jit(solution)/shard_map/ppermute | solution.py:297
  40.1 19.1 %collective-permute-start.15 = (bf16[1024,128]{1,0:T(8,128)(2,1)}, bf16[1024,128]{1,0:T(8,128)(2,1)}, u32[]{:S(2)}, u32[]{:S(2)}) collective-permute-start(bf16[1024,128]{1,0:T(8,128)(2,1)} %collective-permute-done.11.refs_2_), channel_id=1, source_target_pairs={{0,128},{16,144},{32,160},{48,176},{64,192},{80,208},{96,224},{112... | collective-permute-start | bytes 786440 | tf_op jit(solution)/shard_map/ppermute | solution.py:297
  42.8 16.4 %collective-permute-start.13 = (bf16[1024,128]{1,0:T(8,128)(2,1)}, bf16[1024,128]{1,0:T(8,128)(2,1)}, u32[]{:S(2)}, u32[]{:S(2)}) collective-permute-start(bf16[1024,128]{1,0:T(8,128)(2,1)} %collective-permute-done.12.refs_3_), channel_id=1, source_target_pairs={{0,16},{16,32},{32,48},{48,64},{64,80},{80,96},{96,112},{112,0},{1... | collective-permute-start | bytes 786440 | tf_op jit(solution)/shard_map/ppermute | solution.py:297
  44.2 15.0 %collective-permute-start.16 = (bf16[1024,128]{1,0:T(8,128)(2,1)}, bf16[1024,128]{1,0:T(8,128)(2,1)}, u32[]{:S(2)}, u32[]{:S(2)}) collective-permute-start(bf16[1024,128]{1,0:T(8,128)(2,1)} %collective-permute-done.12.refs_3_), channel_id=1, source_target_pairs={{0,128},{16,144},{32,160},{48,176},{64,192},{80,208},{96,224},{112... | collective-permute-start | bytes 786440 | tf_op jit(solution)/shard_map/ppermute | solution.py:297
  64.1 9.4 %collective-permute-start.18 = (bf16[4,128,384]{2,1,0:T(8,128)(2,1)S(1)}, bf16[4,128,384]{2,1,0:T(8,128)(2,1)S(1)}, u32[]{:S(2)}, u32[]{:S(2)}) collective-permute-start(bf16[4,128,384]{2,1,0:T(8,128)(2,1)S(1)} %get-tuple-element.29), channel_id=1, source_target_pairs={{0,2},{1,3},{2,0},{3,1},{4,6},{5,7},{6,4},{7,5},{8,10},{9,11},{10,... | collective-permute-start | bytes 1179656 | tf_op jit(solution)/shard_map/ppermute | solution.py:301
  65.4 12.0 %collective-permute-start.19 = (bf16[4,128,384]{2,1,0:T(8,128)(2,1)S(1)}, bf16[4,128,384]{2,1,0:T(8,128)(2,1)S(1)}, u32[]{:S(2)}, u32[]{:S(2)}) collective-permute-start(bf16[4,128,384]{2,1,0:T(8,128)(2,1)S(1)} %get-tuple-element.30), channel_id=1, source_target_pairs={{0,3},{1,0},{2,1},{3,2},{4,7},{5,4},{6,5},{7,6},{8,11},{9,8},{10,9... | collective-permute-start | bytes 1179656 | tf_op jit(solution)/shard_map/ppermute | solution.py:301
  67.9 11.5 %collective-permute-start.27 = (bf16[2048,128]{1,0:T(8,128)(2,1)}, bf16[2048,128]{1,0:T(8,128)(2,1)S(1)}, u32[]{:S(2)}, u32[]{:S(2)}) collective-permute-start(bf16[2048,128]{1,0:T(8,128)(2,1)} %collective-permute-done.26.refs_5_.refs_1_), channel_id=1, source_target_pairs={{0,16},{16,32},{32,48},{48,64},{64,80},{80,96},{96,112},{112,0},{1... | collective-permute-start | bytes 1572872 | tf_op jit(solution)/shard_map/ppermute | solution.py:297
  79.4 10.4 %collective-permute-start.28 = (bf16[2048,128]{1,0:T(8,128)(2,1)S(1)}, bf16[2048,128]{1,0:T(8,128)(2,1)S(1)}, u32[]{:S(2)}, u32[]{:S(2)}) collective-permute-start(bf16[2048,128]{1,0:T(8,128)(2,1)S(1)} %collective-permute-done.27.refs_6_.refs_2_), channel_id=1, source_target_pairs={{0,16},{16,32},{32,48},{48,64},{64,80},{80,96},{96,112},{112,0},{1... | collective-permute-start | bytes 1572872 | tf_op jit(solution)/shard_map/ppermute | solution.py:297
  79.8 16.6 %collective-permute-start.30 = (bf16[2048,128]{1,0:T(8,128)(2,1)}, bf16[2048,128]{1,0:T(8,128)(2,1)S(1)}, u32[]{:S(2)}, u32[]{:S(2)}) collective-permute-start(bf16[2048,128]{1,0:T(8,128)(2,1)} %collective-permute-done.26.refs_5_.refs_1_), channel_id=1, source_target_pairs={{0,128},{16,144},{32,160},{48,176},{64,192},{80,208},{96,224},{112... | collective-permute-start | bytes 1572872 | tf_op jit(solution)/shard_map/ppermute | solution.py:297
  79.8 18.4 %collective-permute-start.31 = (bf16[2048,128]{1,0:T(8,128)(2,1)S(1)}, bf16[2048,128]{1,0:T(8,128)(2,1)S(1)}, u32[]{:S(2)}, u32[]{:S(2)}) collective-permute-start(bf16[2048,128]{1,0:T(8,128)(2,1)S(1)} %collective-permute-done.27.refs_6_.refs_2_), channel_id=1, source_target_pairs={{0,128},{16,144},{32,160},{48,176},{64,192},{80,208},{96,224},{112... | collective-permute-start | bytes 1572872 | tf_op jit(solution)/shard_map/ppermute | solution.py:297
  80.3 11.6 %collective-permute-start.21 = (bf16[4,128,384]{2,1,0:T(8,128)(2,1)S(1)}, bf16[4,128,384]{2,1,0:T(8,128)(2,1)S(1)}, u32[]{:S(2)}, u32[]{:S(2)}) collective-permute-start(bf16[4,128,384]{2,1,0:T(8,128)(2,1)S(1)} %shard_map.82.refs_1_), channel_id=1, source_target_pairs={{0,8},{1,9},{2,10},{3,11},{4,12},{5,13},{6,14},{7,15},{8,0},{9,1},... | collective-permute-start | bytes 1179656 | tf_op jit(solution)/shard_map/ppermute | solution.py:301
  89.8 20.1 %collective-permute-start.29 = (bf16[2048,128]{1,0:T(8,128)(2,1)S(1)}, bf16[2048,128]{1,0:T(8,128)(2,1)S(1)}, u32[]{:S(2)}, u32[]{:S(2)}) collective-permute-start(bf16[2048,128]{1,0:T(8,128)(2,1)S(1)} %collective-permute-done.28.refs_7_.refs_3_), channel_id=1, source_target_pairs={{0,16},{16,32},{32,48},{48,64},{64,80},{80,96},{96,112},{112,0},{1... | collective-permute-start | bytes 1572872 | tf_op jit(solution)/shard_map/ppermute | solution.py:297
  91.9 18.0 %collective-permute-start.32 = (bf16[2048,128]{1,0:T(8,128)(2,1)S(1)}, bf16[2048,128]{1,0:T(8,128)(2,1)S(1)}, u32[]{:S(2)}, u32[]{:S(2)}) collective-permute-start(bf16[2048,128]{1,0:T(8,128)(2,1)S(1)} %collective-permute-done.28.refs_7_.refs_3_), channel_id=1, source_target_pairs={{0,128},{16,144},{32,160},{48,176},{64,192},{80,208},{96,224},{112... | collective-permute-start | bytes 1572872 | tf_op jit(solution)/shard_map/ppermute | solution.py:297
  96.4 9.4 %collective-permute-start.24 = (bf16[4,128,384]{2,1,0:T(8,128)(2,1)S(1)}, bf16[4,128,384]{2,1,0:T(8,128)(2,1)S(1)}, u32[]{:S(2)}, u32[]{:S(2)}) collective-permute-start(bf16[4,128,384]{2,1,0:T(8,128)(2,1)S(1)} %get-tuple-element.32.refs_0_), channel_id=1, source_target_pairs={{0,2},{1,3},{2,0},{3,1},{4,6},{5,7},{6,4},{7,5},{8,10},{9,11},{10,... | collective-permute-start | bytes 1179656 | tf_op jit(solution)/shard_map/ppermute | solution.py:301
  98.2 11.7 %collective-permute-start.25 = (bf16[4,128,384]{2,1,0:T(8,128)(2,1)S(1)}, bf16[4,128,384]{2,1,0:T(8,128)(2,1)S(1)}, u32[]{:S(2)}, u32[]{:S(2)}) collective-permute-start(bf16[4,128,384]{2,1,0:T(8,128)(2,1)S(1)} %get-tuple-element.32.refs_0_), channel_id=1, source_target_pairs={{0,3},{1,0},{2,1},{3,2},{4,7},{5,4},{6,5},{7,6},{8,11},{9,8},{10,9... | collective-permute-start | bytes 1179656 | tf_op jit(solution)/shard_map/ppermute | solution.py:301
  117.5 9.5 %collective-permute-start.34 = (bf16[4,128,384]{2,1,0:T(8,128)(2,1)S(1)}, bf16[4,128,384]{2,1,0:T(8,128)(2,1)S(1)}, u32[]{:S(2)}, u32[]{:S(2)}) collective-permute-start(bf16[4,128,384]{2,1,0:T(8,128)(2,1)S(1)} %get-tuple-element.39), channel_id=1, source_target_pairs={{0,2},{1,3},{2,0},{3,1},{4,6},{5,7},{6,4},{7,5},{8,10},{9,11},{10,... | collective-permute-start | bytes 1179656 | tf_op jit(solution)/shard_map/ppermute | solution.py:301
  119.3 11.8 %collective-permute-start.35 = (bf16[4,128,384]{2,1,0:T(8,128)(2,1)S(1)}, bf16[4,128,384]{2,1,0:T(8,128)(2,1)S(1)}, u32[]{:S(2)}, u32[]{:S(2)}) collective-permute-start(bf16[4,128,384]{2,1,0:T(8,128)(2,1)S(1)} %get-tuple-element.40), channel_id=1, source_target_pairs={{0,3},{1,0},{2,1},{3,2},{4,7},{5,4},{6,5},{7,6},{8,11},{9,8},{10,9... | collective-permute-start | bytes 1179656 | tf_op jit(solution)/shard_map/ppermute | solution.py:301
  (37 other events, 314.8 us)

commit v2 on v1

--- a/solution.py
+++ b/solution.py
@@ -192,11 +192,6 @@
     piece_ref[...] = bundle_ref[place_ref[3]]
 
 
-def piece_sum_kernel(place_ref, *refs):
-    for e, piece in enumerate(refs[SIDE:]):
-        piece[...] = sum_of(refs[:SIDE], digit(place_ref[3] + e)).astype(piece.dtype)
-
-
 def cost(blocks, moved):
     return pl.CostEstimate(flops=blocks * 2 * BLK**3, bytes_accessed=moved, transcendentals=0)
 
@@ -307,6 +302,9 @@
 ]
 
 
+DOWN = [(r, GRID_ROWS + (r - 1) % GRID_ROWS) for r in range(GRID_ROWS)]
+
+
 def column_shift(first, distance):
     pairs = []
     for core in range(2):
@@ -320,14 +318,28 @@
     return pairs
 
 
-def ring_gather(cell):
+NEAR_GROUPS = [[y * SIDE + x for y in range(SIDE)] for x in range(SIDE)] + [
+    [SIDE * SIDE + y * SIDE + x for x in range(SIDE)] for y in range(SIDE)
+]
+
+
+def ring_gather(cell, first=None):
     ring = [cell]
     other = []
     for step in range(1, GRID_ROWS // 2 + 1):
-        ring.append(on_rows(ring[-1], AROUND))
+        if step == 1 and first is not None:
+            ring.append(first)
+        else:
+            ring.append(on_rows(ring[-1], AROUND))
         if step < GRID_ROWS // 2:
             other.append(on_rows(ring[-1], SWAP))
     return ring + other
+
+
+def first_step(mine, own):
+    up = on_rows(own, AROUND[:GRID_ROWS])
+    down = on_rows(own, DOWN)
+    return jnp.where(mine, up, down)
 
 
 def spread(values, first):
@@ -371,8 +383,10 @@
     other_out = on_rows(own_out, SWAP)
     other_gain = on_rows(own_gain, SWAP)
     mine = core == 0
-    cells_in = ring_gather(jnp.where(mine, own_in, other_in))
-    cells_out = ring_gather(jnp.where(mine, own_out, other_out))
+    first_ins = first_step(mine, own_in)
+    first_outs = first_step(mine, own_out)
+    cells_in = ring_gather(jnp.where(mine, own_in, other_in), first_ins)
+    cells_out = ring_gather(jnp.where(mine, own_out, other_out), first_outs)
     own_in, own_out, other_in, other_out, _ = lax.optimization_barrier(
         (own_in, own_out, other_in, other_out, cells_in[2])
     )
@@ -395,16 +409,11 @@
     hidden = later_in(place, meta, gains[1], bundles, later_cells)
     bundles = project_out(1, place, meta, hidden, later_cells)
     landed = spread(bundles, True)
-    sums = add_up(
-        piece_sum_kernel,
-        place,
-        [bundles[0]] + landed,
-        [jax.ShapeDtypeStruct((TOK, WIDTH), F32)] + [PIECE] * (SIDE - 1),
-    )
-    total = sums[0]
-    for value in spread(sums, False):
-        total = total + value.astype(F32)
-    final = (piece.astype(F32) + total).astype(BF16)
+    sums = add_up(whole_sum_kernel, None, [bundles[0]] + landed, [BUNDLE])[0]
+    landed = lax.all_to_all(
+        sums, ("section", "col"), 0, 0, tiled=True, axis_index_groups=NEAR_GROUPS
+    )
+    final = (piece.astype(F32) + jnp.sum(landed.astype(F32), axis=0)).astype(BF16)
 
     other = on_rows(jnp.where(mine, final, piece), SWAP)
     return jnp.stack([jnp.where(mine, piece, other), jnp.where(mine, other, final)])[None]

time: 145 us -> 141 us (0.972)
  waiting for transfers between devices: 62 us -> 43.2 us
  blocking collectives: 0 us -> 11.3 us
  starting transfers between devices: 43.2 us -> 51.6 us
  other arithmetic: 5.36 us -> 2.82 us
  local copies, waits for them, and re-layouts: 14 us -> 12 us
    ppermute x25 -> x27, starting transfers between devices: 14.7 us -> 27.9 us  [on_rows(): return lax.ppermute(value, ('section', 'row'), perm)]
    all_to_all x0 -> x1, blocking collectives: none -> 11.3 us  [shards(): lax.all_to_all(sums, ('section', 'col'), 0, 0, tiled=True, axis_index_gro...]
    ppermute x15 -> x12, waiting for transfers between devices: 44.1 us -> 34.6 us  [on_cols(): return lax.ppermute(value, ('section', 'col'), perm)]
    ppermute x25 -> x27, waiting for transfers between devices: 17.9 us -> 8.52 us  [on_rows(): return lax.ppermute(value, ('section', 'row'), perm)]
    ppermute x15 -> x12, starting transfers between devices: 22.7 us -> 18.7 us  [on_cols(): return lax.ppermute(value, ('section', 'col'), perm)]
    unnamed x40 -> x32, local copies, waits for them, and re-layouts: 12.5 us -> 10.5 us
    select_n x2 -> x4, other arithmetic: 1.98 us -> 0.15 us  [the longest x2 0.06 us: first_step(): return jnp.where(mine, up, down)]
  transfers between devices with their start and end apart: 41 -> 40, of which waited for: 22 -> 18; matrix products, arithmetic and copies ran while one was open for 4% -> 2% of each run, Pallas kernels for 7% -> 7%
where the time goes in v2:
time: 141 us; the launch traced here: 139 us
  starting transfers between devices  51.6 us (37%)
  waiting for transfers between devices  43.2 us (31%)
  Pallas kernels  16.6 us (12%)
  local copies, waits for them, and re-layouts  12 us (9%)
  blocking collectives  11.3 us (8%)
  other arithmetic  2.82 us (2%)
  between operations  1.63 us (1%)
    ppermute x12, waiting for transfers between devices, on_cols(): return lax.ppermute(value, ('section', 'col'), perm)  34.6 us
    ppermute x27, starting transfers between devices, on_rows(): return lax.ppermute(value, ('section', 'row'), perm)  27.9 us
    ppermute x12, starting transfers between devices, on_cols(): return lax.ppermute(value, ('section', 'col'), perm)  18.7 us
    all_to_all x1, blocking collectives, shards(): lax.all_to_all(sums, ('section', 'col'), 0, 0, tiled=True, axis_index_gro...  11.3 us
    unnamed x32, local copies, waits for them, and re-layouts  10.5 us
    ppermute x27, waiting for transfers between devices, on_rows(): return lax.ppermute(value, ('section', 'row'), perm)  8.52 us
    pallas_call x2, Pallas kernels, project_out(): pl.pallas_call(functools.partial(out_kernel, phase), in_specs=[smem(), sm...  6.77 us
    all_to_all x1, starting transfers between devices, shards(): lax.all_to_all(jnp.broadcast_to(own_meta, (2 * GRID_ROWS, 1, BLK)), ('sec...  5.02 us
  transfers between devices with their start and end apart: 40, of which 18 were waited for; matrix products, arithmetic and copies ran while one was open for 2% of the time, Pallas kernels for 7%

profile of v2, /device:TPU:2, one launch (start us, length us, event | category | flops | bytes accessed | tf_op | source)
XLA Modules:
  0.0 139.1 jit_solution(6147725917124908945)
XLA Ops:
  0.0 3.9 %collective-permute-start.2 = (bf16[1024,128]{1,0:T(8,128)(2,1)}, bf16[1024,128]{1,0:T(8,128)(2,1)S(1)}, u32[]{:S(2)}, u32[]{:S(2)}) collective-permute-start(bf16[1024,128]{1,0:T(8,128)(2,1)} %bitcast.29), channel_id=1, source_target_pairs={{0,16},{16,32},{32,48},{48,64},{64,80},{80,96},{96,112},{112,0},{1... | collective-permute-start | bytes 786440 | tf_op jit(solution)/shard_map/ppermute | solution.py:292
  4.0 4.1 %collective-permute-start.3 = (bf16[1024,128]{1,0:T(8,128)(2,1)}, bf16[1024,128]{1,0:T(8,128)(2,1)S(1)}, u32[]{:S(2)}, u32[]{:S(2)}) collective-permute-start(bf16[1024,128]{1,0:T(8,128)(2,1)} %bitcast.30), channel_id=1, source_target_pairs={{0,240},{16,128},{32,144},{48,160},{64,176},{80,192},{96,208},{112... | collective-permute-start | bytes 786440 | tf_op jit(solution)/shard_map/ppermute | solution.py:292
  8.0 1.9 %collective-permute-start.11 = (bf16[1024,128]{1,0:T(8,128)(2,1)}, bf16[1024,128]{1,0:T(8,128)(2,1)S(1)}, u32[]{:S(2)}, u32[]{:S(2)}) collective-permute-start(bf16[1024,128]{1,0:T(8,128)(2,1)} %bitcast.33), channel_id=1, source_target_pairs={{0,16},{16,32},{32,48},{48,64},{64,80},{80,96},{96,112},{112,0},{1... | collective-permute-start | bytes 786440 | tf_op jit(solution)/shard_map/ppermute | solution.py:292
  12.6 2.9 %collective-permute-start.1 = (bf16[1024,128]{1,0:T(8,128)(2,1)}, bf16[1024,128]{1,0:T(8,128)(2,1)S(1)}, u32[]{:S(2)}, u32[]{:S(2)}) collective-permute-start(bf16[1024,128]{1,0:T(8,128)(2,1)} %bitcast.31), channel_id=1, source_target_pairs={{0,128},{16,144},{32,160},{48,176},{64,192},{80,208},{96,224},{112... | collective-permute-start | bytes 786440 | tf_op jit(solution)/shard_map/ppermute | solution.py:292
  18.1 5.0 %all-to-all-start = ((s32[16,1,128]{2,1,0:T(1,128)}), s32[16,1,128]{2,1,0:T(1,128)S(1)}, u32[]{:S(2)}, u32[]{:S(2)}) async-start(s32[16,1,128]{2,1,0:T(1,128)} %broadcast_in_dim.10), calls=%async_computation | async-start | bytes 16384 | tf_op jit(solution)/shard_map/all_to_all | solution.py:372
  27.7 1.9 %copy-done = bf16[2,128,6144]{2,1,0:T(8,128)(2,1)S(1)} copy-done((bf16[2,128,6144]{2,1,0:T(8,128)(2,1)S(1)}, bf16[2,128,6144]{2,1,0:T(8,128)(2,1)}, u32[]{:S(2)}) %copy-start) | copy-done | bytes 3145752
  34.3 2.0 %collective-permute-start.6 = (bf16[1024,128]{1,0:T(8,128)(2,1)S(1)}, bf16[1024,128]{1,0:T(8,128)(2,1)S(1)}, u32[]{:S(2)}, u32[]{:S(2)}) collective-permute-start(bf16[1024,128]{1,0:T(8,128)(2,1)S(1)} %collective-permute-done.5.refs_3_), channel_id=1, source_target_pairs={{0,16},{16,32},{32,48},{48,64},{64,80},{80,96},{96,112},{112,0},{1... | collective-permute-start | bytes 786440 | tf_op jit(solution)/shard_map/ppermute | solution.py:292
  40.6 2.7 %collective-permute-done.6.refs_4_ = bf16[1024,128]{1,0:T(8,128)(2,1)S(1)} collective-permute-done((bf16[1024,128]{1,0:T(8,128)(2,1)S(1)}, bf16[1024,128]{1,0:T(8,128)(2,1)S(1)}, u32[]{:S(2)}, u32[]{:S(2)}) %collective-permute-start.6) | collective-permute-done | bytes 262176 | tf_op jit(solution)/shard_map/ppermute | solution.py:292
  50.3 3.4 %first_in.1.hidden_ref = bf16[12,128,128]{2,1,0:T(8,128)(2,1)S(1)} custom-call(s32[5]{0:T(128)S(1)} %stack.32.place_ref, s32[16,128]{1,0:T(8,128)S(1)} %bitcast.25, bf16[48,128,128]{2,1,0:T(8,128)(2,1)S(1)} %copy-done.2, bf16[1024,128]{1,0:T(8,128)(2,1)S(1)} %broadcast_select_fusion.5.refs_0_, bf16[1024,128]{1,0:T(8,128)(2,1)S(1)} %broadcast_select_fusion.4.refs_1_, ...), custom_call_target="tpu_custom_call" | custom-call | flops 2147483648 | bytes 8388608 | tf_op jit(solution)/shard_map/first_in/pallas_call | solution.py:238
  53.8 3.4 %project_out.2 = (bf16[4,128,384]{2,1,0:T(8,128)(2,1)S(1)}, bf16[4,128,384]{2,1,0:T(8,128)(2,1)S(1)}, bf16[4,128,384]{2,1,0:T(8,128)(2,1)S(1)}, bf16[4,128,384]{2,1,0:T(8,128)(2,1)S(1)}) custom-call(s32[5]{0:T(128)S(1)} %stack.32.place_ref, s32[16,128]{1,0:T(8,128)S(1)} %bitcast.26, bf16[12,128,128]{2,1,0:T(8,128)(2,1)S(1)} %first_in.1.hidden_ref, ...), custom_call_target="tpu_custom_call" | custom-call | flops 2147483648 | bytes 8388608 | tf_op jit(solution)/shard_map/project_out/pallas_call | solution.py:268
  59.8 2.5 %collective-permute-start.21 = (bf16[4,128,384]{2,1,0:T(8,128)(2,1)S(1)}, bf16[4,128,384]{2,1,0:T(8,128)(2,1)S(1)}, u32[]{:S(2)}, u32[]{:S(2)}) collective-permute-start(bf16[4,128,384]{2,1,0:T(8,128)(2,1)S(1)} %get-tuple-element.26), channel_id=1, source_target_pairs={{0,3},{1,0},{2,1},{3,2},{4,7},{5,4},{6,5},{7,6},{8,11},{9,8},{10,9... | collective-permute-start | bytes 1179656 | tf_op jit(solution)/shard_map/ppermute | solution.py:296
  65.0 2.9 %collective-permute-done.20.refs_2_ = bf16[4,128,384]{2,1,0:T(8,128)(2,1)S(1)} collective-permute-done((bf16[4,128,384]{2,1,0:T(8,128)(2,1)S(1)}, bf16[4,128,384]{2,1,0:T(8,128)(2,1)S(1)}, u32[]{:S(2)}, u32[]{:S(2)}) %collective-permute-start.20) | collective-permute-done | bytes 393248 | tf_op jit(solution)/shard_map/ppermute | solution.py:296
  67.9 3.9 %collective-permute-done.21.refs_3_ = bf16[4,128,384]{2,1,0:T(8,128)(2,1)S(1)} collective-permute-done((bf16[4,128,384]{2,1,0:T(8,128)(2,1)S(1)}, bf16[4,128,384]{2,1,0:T(8,128)(2,1)S(1)}, u32[]{:S(2)}, u32[]{:S(2)}) %collective-permute-start.21) | collective-permute-done | bytes 393248 | tf_op jit(solution)/shard_map/ppermute | solution.py:296
  76.3 2.5 %collective-permute-start.23 = (bf16[4,128,384]{2,1,0:T(8,128)(2,1)S(1)}, bf16[4,128,384]{2,1,0:T(8,128)(2,1)S(1)}, u32[]{:S(2)}, u32[]{:S(2)}) collective-permute-start(bf16[4,128,384]{2,1,0:T(8,128)(2,1)S(1)} %shard_map.82.refs_1_), channel_id=1, source_target_pairs={{0,8},{1,9},{2,10},{3,11},{4,12},{5,13},{6,14},{7,15},{8,0},{9,1},... | collective-permute-start | bytes 1179656 | tf_op jit(solution)/shard_map/ppermute | solution.py:296
  78.8 2.3 %collective-permute-done.22.refs_2_ = bf16[4,128,384]{2,1,0:T(8,128)(2,1)S(1)} collective-permute-done((bf16[4,128,384]{2,1,0:T(8,128)(2,1)S(1)}, bf16[4,128,384]{2,1,0:T(8,128)(2,1)S(1)}, u32[]{:S(2)}, u32[]{:S(2)}) %collective-permute-start.22) | collective-permute-done | bytes 393248 | tf_op jit(solution)/shard_map/ppermute | solution.py:296
  86.4 2.5 %collective-permute-done.24.refs_4_ = bf16[4,128,384]{2,1,0:T(8,128)(2,1)S(1)} collective-permute-done((bf16[4,128,384]{2,1,0:T(8,128)(2,1)S(1)}, bf16[4,128,384]{2,1,0:T(8,128)(2,1)S(1)}, u32[]{:S(2)}, u32[]{:S(2)}) %collective-permute-start.24) | collective-permute-done | bytes 393248 | tf_op jit(solution)/shard_map/ppermute | solution.py:296
  94.0 3.6 %collective-permute-done.25.refs_1_ = bf16[4,128,384]{2,1,0:T(8,128)(2,1)S(1)} collective-permute-done((bf16[4,128,384]{2,1,0:T(8,128)(2,1)S(1)}, bf16[4,128,384]{2,1,0:T(8,128)(2,1)S(1)}, u32[]{:S(2)}, u32[]{:S(2)}) %collective-permute-start.25) | collective-permute-done | bytes 393248 | tf_op jit(solution)/shard_map/ppermute | solution.py:296
  97.6 3.2 %collective-permute-done.26.refs_2_ = bf16[4,128,384]{2,1,0:T(8,128)(2,1)S(1)} collective-permute-done((bf16[4,128,384]{2,1,0:T(8,128)(2,1)S(1)}, bf16[4,128,384]{2,1,0:T(8,128)(2,1)S(1)}, u32[]{:S(2)}, u32[]{:S(2)}) %collective-permute-start.26) | collective-permute-done | bytes 393248 | tf_op jit(solution)/shard_map/ppermute | solution.py:296
  100.8 3.7 %collective-permute-done.27.refs_3_ = bf16[4,128,384]{2,1,0:T(8,128)(2,1)S(1)} collective-permute-done((bf16[4,128,384]{2,1,0:T(8,128)(2,1)S(1)}, bf16[4,128,384]{2,1,0:T(8,128)(2,1)S(1)}, u32[]{:S(2)}, u32[]{:S(2)}) %collective-permute-start.27) | collective-permute-done | bytes 393248 | tf_op jit(solution)/shard_map/ppermute | solution.py:296
  104.5 3.8 %later_in.1.hidden_ref = bf16[12,128,128]{2,1,0:T(8,128)(2,1)S(1)} custom-call(s32[5]{0:T(128)S(1)} %stack.32.place_ref, s32[16,128]{1,0:T(8,128)S(1)} %bitcast.27, f32[48,1,128]{2,1,0:T(1,128)S(1)} %get-tuple-element.39.gain_ref, bf16[4,128,384]{2,1,0:T(8,128)(2,1)S(1)} %get-tuple-element.28.refs_0_, ...), custom_call_target="tpu_custom_call" | custom-call | flops 2147483648 | bytes 12582912 | tf_op jit(solution)/shard_map/later_in/pallas_call | solution.py:251
  108.3 3.4 %project_out.3 = (bf16[4,128,384]{2,1,0:T(8,128)(2,1)S(1)}, bf16[4,128,384]{2,1,0:T(8,128)(2,1)S(1)}, bf16[4,128,384]{2,1,0:T(8,128)(2,1)S(1)}, bf16[4,128,384]{2,1,0:T(8,128)(2,1)S(1)}) custom-call(s32[5]{0:T(128)S(1)} %stack.32.place_ref, s32[16,128]{1,0:T(8,128)S(1)} %bitcast.28, bf16[12,128,128]{2,1,0:T(8,128)(2,1)S(1)} %later_in.1.hidden_ref, ...), custom_call_target="tpu_custom_call" | custom-call | flops 2147483648 | bytes 8388608 | tf_op jit(solution)/shard_map/project_out/pallas_call | solution.py:268
  115.0 4.6 %collective-permute-done.35.refs_1_ = bf16[4,128,384]{2,1,0:T(8,128)(2,1)S(1)} collective-permute-done((bf16[4,128,384]{2,1,0:T(8,128)(2,1)S(1)}, bf16[4,128,384]{2,1,0:T(8,128)(2,1)S(1)}, u32[]{:S(2)}, u32[]{:S(2)}) %collective-permute-start.35) | collective-permute-done | bytes 393248 | tf_op jit(solution)/shard_map/ppermute | solution.py:296
  121.3 4.0 %collective-permute-done.37.refs_3_ = bf16[4,128,384]{2,1,0:T(8,128)(2,1)S(1)} collective-permute-done((bf16[4,128,384]{2,1,0:T(8,128)(2,1)S(1)}, bf16[4,128,384]{2,1,0:T(8,128)(2,1)S(1)}, u32[]{:S(2)}, u32[]{:S(2)}) %collective-permute-start.37) | collective-permute-done | bytes 393248 | tf_op jit(solution)/shard_map/ppermute | solution.py:296
  125.6 11.3 %all_to_all.10 = bf16[4,128,384]{2,1,0:T(8,128)(2,1)S(1)} all-to-all(bf16[4,128,384]{2,1,0:T(8,128)(2,1)S(1)} %shard_map.84), channel_id=1, replica_groups={{0,4,8,12},{1,5,9,13},{2,6,10,14},{3,7,11,15},{128,129,130,131},{132,13..., dimensions={0} | all-to-all | bytes 786432 | tf_op jit(solution)/shard_map/all_to_all | solution.py:413
  (112 shorter events, 52.0 us)
Async XLA Ops:
  0.0 12.4 %collective-permute-start.2 = (bf16[1024,128]{1,0:T(8,128)(2,1)}, bf16[1024,128]{1,0:T(8,128)(2,1)S(1)}, u32[]{:S(2)}, u32[]{:S(2)}) collective-permute-start(bf16[1024,128]{1,0:T(8,128)(2,1)} %bitcast.29), channel_id=1, source_target_pairs={{0,16},{16,32},{32,48},{48,64},{64,80},{80,96},{96,112},{112,0},{1... | collective-permute-start | bytes 786440 | tf_op jit(solution)/shard_map/ppermute | solution.py:292
  8.0 15.2 %collective-permute-start.11 = (bf16[1024,128]{1,0:T(8,128)(2,1)}, bf16[1024,128]{1,0:T(8,128)(2,1)S(1)}, u32[]{:S(2)}, u32[]{:S(2)}) collective-permute-start(bf16[1024,128]{1,0:T(8,128)(2,1)} %bitcast.33), channel_id=1, source_target_pairs={{0,16},{16,32},{32,48},{48,64},{64,80},{80,96},{96,112},{112,0},{1... | collective-permute-start | bytes 786440 | tf_op jit(solution)/shard_map/ppermute | solution.py:292
  10.0 13.7 %collective-permute-start.12 = (bf16[1024,128]{1,0:T(8,128)(2,1)}, bf16[1024,128]{1,0:T(8,128)(2,1)S(1)}, u32[]{:S(2)}, u32[]{:S(2)}) collective-permute-start(bf16[1024,128]{1,0:T(8,128)(2,1)} %bitcast.34), channel_id=1, source_target_pairs={{0,240},{16,128},{32,144},{48,160},{64,176},{80,192},{96,208},{112... | collective-permute-start | bytes 786440 | tf_op jit(solution)/shard_map/ppermute | solution.py:292
  12.5 12.9 %collective-permute-start.4 = (bf16[1024,128]{1,0:T(8,128)(2,1)S(1)}, bf16[1024,128]{1,0:T(8,128)(2,1)S(1)}, u32[]{:S(2)}, u32[]{:S(2)}) collective-permute-start(bf16[1024,128]{1,0:T(8,128)(2,1)S(1)} %broadcast_select_fusion.4.refs_1_), channel_id=1, source_target_pairs={{0,16},{16,32},{32,48},{48,64},{64,80},{80,96},{96,112},{112,0},{1... | collective-permute-start | bytes 786440 | tf_op jit(solution)/shard_map/ppermute | solution.py:292
  12.6 19.4 %collective-permute-start.1 = (bf16[1024,128]{1,0:T(8,128)(2,1)}, bf16[1024,128]{1,0:T(8,128)(2,1)S(1)}, u32[]{:S(2)}, u32[]{:S(2)}) collective-permute-start(bf16[1024,128]{1,0:T(8,128)(2,1)} %bitcast.31), channel_id=1, source_target_pairs={{0,128},{16,144},{32,160},{48,176},{64,192},{80,208},{96,224},{112... | collective-permute-start | bytes 786440 | tf_op jit(solution)/shard_map/ppermute | solution.py:292
  15.4 17.2 %collective-permute-start.10 = (bf16[1024,128]{1,0:T(8,128)(2,1)}, bf16[1024,128]{1,0:T(8,128)(2,1)S(1)}, u32[]{:S(2)}, u32[]{:S(2)}) collective-permute-start(bf16[1024,128]{1,0:T(8,128)(2,1)} %bitcast.35), channel_id=1, source_target_pairs={{0,128},{16,144},{32,160},{48,176},{64,192},{80,208},{96,224},{112... | collective-permute-start | bytes 786440 | tf_op jit(solution)/shard_map/ppermute | solution.py:292
  18.1 27.0 %all-to-all-start = ((s32[16,1,128]{2,1,0:T(1,128)}), s32[16,1,128]{2,1,0:T(1,128)S(1)}, u32[]{:S(2)}, u32[]{:S(2)}) async-start(s32[16,1,128]{2,1,0:T(1,128)} %broadcast_in_dim.10), calls=%async_computation | async-start | bytes 16384 | tf_op jit(solution)/shard_map/all_to_all | solution.py:372
  38.1 15.7 %collective-permute-start.16 = (bf16[1024,128]{1,0:T(8,128)(2,1)S(1)}, bf16[1024,128]{1,0:T(8,128)(2,1)}, u32[]{:S(2)}, u32[]{:S(2)}) collective-permute-start(bf16[1024,128]{1,0:T(8,128)(2,1)S(1)} %broadcast_select_fusion.2.refs_1_), channel_id=1, source_target_pairs={{0,128},{16,144},{32,160},{48,176},{64,192},{80,208},{96,224},{112... | collective-permute-start | bytes 786440 | tf_op jit(solution)/shard_map/ppermute | solution.py:292
  38.8 23.6 %collective-permute-start.28 = (bf16[2048,128]{1,0:T(8,128)(2,1)S(1)}, bf16[2048,128]{1,0:T(8,128)(2,1)S(1)}, u32[]{:S(2)}, u32[]{:S(2)}) collective-permute-start(bf16[2048,128]{1,0:T(8,128)(2,1)S(1)} %pad_maximum_fusion.refs_4_.refs_0_), channel_id=1, source_target_pairs={{0,16},{16,32},{32,48},{48,64},{64,80},{80,96},{96,112},{112,0},{1... | collective-permute-start | bytes 1572872 | tf_op jit(solution)/shard_map/ppermute | solution.py:292
  40.6 13.2 %collective-permute-start.17 = (bf16[1024,128]{1,0:T(8,128)(2,1)S(1)}, bf16[1024,128]{1,0:T(8,128)(2,1)}, u32[]{:S(2)}, u32[]{:S(2)}) collective-permute-start(bf16[1024,128]{1,0:T(8,128)(2,1)S(1)} %collective-permute-done.13.refs_2_), channel_id=1, source_target_pairs={{0,128},{16,144},{32,160},{48,176},{64,192},{80,208},{96,224},{112... | collective-permute-start | bytes 786440 | tf_op jit(solution)/shard_map/ppermute | solution.py:292
  44.0 9.8 %collective-permute-start.15 = (bf16[1024,128]{1,0:T(8,128)(2,1)}, bf16[1024,128]{1,0:T(8,128)(2,1)}, u32[]{:S(2)}, u32[]{:S(2)}) collective-permute-start(bf16[1024,128]{1,0:T(8,128)(2,1)} %collective-permute-done.14.refs_3_), channel_id=1, source_target_pairs={{0,16},{16,32},{32,48},{48,64},{64,80},{80,96},{96,112},{112,0},{1... | collective-permute-start | bytes 786440 | tf_op jit(solution)/shard_map/ppermute | solution.py:292
  58.6 9.4 %collective-permute-start.20 = (bf16[4,128,384]{2,1,0:T(8,128)(2,1)S(1)}, bf16[4,128,384]{2,1,0:T(8,128)(2,1)S(1)}, u32[]{:S(2)}, u32[]{:S(2)}) collective-permute-start(bf16[4,128,384]{2,1,0:T(8,128)(2,1)S(1)} %get-tuple-element.25), channel_id=1, source_target_pairs={{0,2},{1,3},{2,0},{3,1},{4,6},{5,7},{6,4},{7,5},{8,10},{9,11},{10,... | collective-permute-start | bytes 1179656 | tf_op jit(solution)/shard_map/ppermute | solution.py:296
  59.8 12.0 %collective-permute-start.21 = (bf16[4,128,384]{2,1,0:T(8,128)(2,1)S(1)}, bf16[4,128,384]{2,1,0:T(8,128)(2,1)S(1)}, u32[]{:S(2)}, u32[]{:S(2)}) collective-permute-start(bf16[4,128,384]{2,1,0:T(8,128)(2,1)S(1)} %get-tuple-element.26), channel_id=1, source_target_pairs={{0,3},{1,0},{2,1},{3,2},{4,7},{5,4},{6,5},{7,6},{8,11},{9,8},{10,9... | collective-permute-start | bytes 1179656 | tf_op jit(solution)/shard_map/ppermute | solution.py:296
  62.4 11.5 %collective-permute-start.29 = (bf16[2048,128]{1,0:T(8,128)(2,1)S(1)}, bf16[2048,128]{1,0:T(8,128)(2,1)S(1)}, u32[]{:S(2)}, u32[]{:S(2)}) collective-permute-start(bf16[2048,128]{1,0:T(8,128)(2,1)S(1)} %collective-permute-done.28.refs_5_.refs_1_), channel_id=1, source_target_pairs={{0,16},{16,32},{32,48},{48,64},{64,80},{80,96},{96,112},{112,0},{1... | collective-permute-start | bytes 1572872 | tf_op jit(solution)/shard_map/ppermute | solution.py:292
  73.9 10.4 %collective-permute-start.30 = (bf16[2048,128]{1,0:T(8,128)(2,1)S(1)}, bf16[2048,128]{1,0:T(8,128)(2,1)S(1)}, u32[]{:S(2)}, u32[]{:S(2)}) collective-permute-start(bf16[2048,128]{1,0:T(8,128)(2,1)S(1)} %collective-permute-done.29.refs_6_.refs_2_), channel_id=1, source_target_pairs={{0,16},{16,32},{32,48},{48,64},{64,80},{80,96},{96,112},{112,0},{1... | collective-permute-start | bytes 1572872 | tf_op jit(solution)/shard_map/ppermute | solution.py:292
  75.8 15.7 %collective-permute-start.32 = (bf16[2048,128]{1,0:T(8,128)(2,1)S(1)}, bf16[2048,128]{1,0:T(8,128)(2,1)S(1)}, u32[]{:S(2)}, u32[]{:S(2)}) collective-permute-start(bf16[2048,128]{1,0:T(8,128)(2,1)S(1)} %collective-permute-done.28.refs_5_.refs_1_), channel_id=1, source_target_pairs={{0,128},{16,144},{32,160},{48,176},{64,192},{80,208},{96,224},{112... | collective-permute-start | bytes 1572872 | tf_op jit(solution)/shard_map/ppermute | solution.py:292
  75.8 16.7 %collective-permute-start.33 = (bf16[2048,128]{1,0:T(8,128)(2,1)S(1)}, bf16[2048,128]{1,0:T(8,128)(2,1)S(1)}, u32[]{:S(2)}, u32[]{:S(2)}) collective-permute-start(bf16[2048,128]{1,0:T(8,128)(2,1)S(1)} %collective-permute-done.29.refs_6_.refs_2_), channel_id=1, source_target_pairs={{0,128},{16,144},{32,160},{48,176},{64,192},{80,208},{96,224},{112... | collective-permute-start | bytes 1572872 | tf_op jit(solution)/shard_map/ppermute | solution.py:292
  76.3 10.1 %collective-permute-start.23 = (bf16[4,128,384]{2,1,0:T(8,128)(2,1)S(1)}, bf16[4,128,384]{2,1,0:T(8,128)(2,1)S(1)}, u32[]{:S(2)}, u32[]{:S(2)}) collective-permute-start(bf16[4,128,384]{2,1,0:T(8,128)(2,1)S(1)} %shard_map.82.refs_1_), channel_id=1, source_target_pairs={{0,8},{1,9},{2,10},{3,11},{4,12},{5,13},{6,14},{7,15},{8,0},{9,1},... | collective-permute-start | bytes 1179656 | tf_op jit(solution)/shard_map/ppermute | solution.py:296
  84.3 20.2 %collective-permute-start.31 = (bf16[2048,128]{1,0:T(8,128)(2,1)S(1)}, bf16[2048,128]{1,0:T(8,128)(2,1)S(1)}, u32[]{:S(2)}, u32[]{:S(2)}) collective-permute-start(bf16[2048,128]{1,0:T(8,128)(2,1)S(1)} %collective-permute-done.30.refs_7_.refs_3_), channel_id=1, source_target_pairs={{0,16},{16,32},{32,48},{48,64},{64,80},{80,96},{96,112},{112,0},{1... | collective-permute-start | bytes 1572872 | tf_op jit(solution)/shard_map/ppermute | solution.py:292
  86.4 18.1 %collective-permute-start.34 = (bf16[2048,128]{1,0:T(8,128)(2,1)S(1)}, bf16[2048,128]{1,0:T(8,128)(2,1)S(1)}, u32[]{:S(2)}, u32[]{:S(2)}) collective-permute-start(bf16[2048,128]{1,0:T(8,128)(2,1)S(1)} %collective-permute-done.30.refs_7_.refs_3_), channel_id=1, source_target_pairs={{0,128},{16,144},{32,160},{48,176},{64,192},{80,208},{96,224},{112... | collective-permute-start | bytes 1572872 | tf_op jit(solution)/shard_map/ppermute | solution.py:292
  91.4 9.4 %collective-permute-start.26 = (bf16[4,128,384]{2,1,0:T(8,128)(2,1)S(1)}, bf16[4,128,384]{2,1,0:T(8,128)(2,1)S(1)}, u32[]{:S(2)}, u32[]{:S(2)}) collective-permute-start(bf16[4,128,384]{2,1,0:T(8,128)(2,1)S(1)} %get-tuple-element.28.refs_0_), channel_id=1, source_target_pairs={{0,2},{1,3},{2,0},{3,1},{4,6},{5,7},{6,4},{7,5},{8,10},{9,11},{10,... | collective-permute-start | bytes 1179656 | tf_op jit(solution)/shard_map/ppermute | solution.py:296
  92.5 12.0 %collective-permute-start.27 = (bf16[4,128,384]{2,1,0:T(8,128)(2,1)S(1)}, bf16[4,128,384]{2,1,0:T(8,128)(2,1)S(1)}, u32[]{:S(2)}, u32[]{:S(2)}) collective-permute-start(bf16[4,128,384]{2,1,0:T(8,128)(2,1)S(1)} %get-tuple-element.28.refs_0_), channel_id=1, source_target_pairs={{0,3},{1,0},{2,1},{3,2},{4,7},{5,4},{6,5},{7,6},{8,11},{9,8},{10,9... | collective-permute-start | bytes 1179656 | tf_op jit(solution)/shard_map/ppermute | solution.py:296
  111.9 9.4 %collective-permute-start.36 = (bf16[4,128,384]{2,1,0:T(8,128)(2,1)S(1)}, bf16[4,128,384]{2,1,0:T(8,128)(2,1)S(1)}, u32[]{:S(2)}, u32[]{:S(2)}) collective-permute-start(bf16[4,128,384]{2,1,0:T(8,128)(2,1)S(1)} %get-tuple-element.35), channel_id=1, source_target_pairs={{0,2},{1,3},{2,0},{3,1},{4,6},{5,7},{6,4},{7,5},{8,10},{9,11},{10,... | collective-permute-start | bytes 1179656 | tf_op jit(solution)/shard_map/ppermute | solution.py:296
  113.4 12.0 %collective-permute-start.37 = (bf16[4,128,384]{2,1,0:T(8,128)(2,1)S(1)}, bf16[4,128,384]{2,1,0:T(8,128)(2,1)S(1)}, u32[]{:S(2)}, u32[]{:S(2)}) collective-permute-start(bf16[4,128,384]{2,1,0:T(8,128)(2,1)S(1)} %get-tuple-element.36), channel_id=1, source_target_pairs={{0,3},{1,0},{2,1},{3,2},{4,7},{5,4},{6,5},{7,6},{8,11},{9,8},{10,9... | collective-permute-start | bytes 1179656 | tf_op jit(solution)/shard_map/ppermute | solution.py:296
  (32 other events, 237.2 us)

commit v3 on v1

--- a/solution.py
+++ b/solution.py
@@ -12,8 +12,9 @@
 BLK = 128
 SLOTS = 8
 UNROLL = 4
+TAIL = 16
+SPAN = 1024 + TAIL
 GRID_ROWS = 8
-OFFSETS = (0, -1, -2, -3, -4, 1, 2, 3)
 SIDE = 4
 DBL = 6
 FBL = 12
@@ -44,37 +45,68 @@
     return lax.rem(value + 2 * SIDE, SIDE)
 
 
-def fetch(cells, offset, weights, sems):
+def pack_kernel(place_ref, *refs):
+    sources, outs, sems = refs[:6], refs[6:8], refs[8]
+    copies = [
+        pltpu.make_async_copy(sources[k], outs[k].at[pl.ds(0, SLOTS * BLK)], sems.at[k])
+        for k in range(2)
+    ]
+    for copy in copies:
+        copy.start()
+    lane = lax.broadcasted_iota(jnp.int32, (TAIL, BLK), 1)
+    for k, out in enumerate(outs):
+        slots, count = sources[2 + k], sources[4 + k]
+        row = jnp.where(lane == 2 * SLOTS, count[0], 0)
+        for n in range(SLOTS):
+            model, hid = place_ref[4] * DBL + slots[n] // FBL, lax.rem(slots[n], FBL)
+            row = jnp.where(lane == n, hid if k else model, row)
+            row = jnp.where(lane == SLOTS + n, model if k else hid, row)
+        out[SLOTS * BLK : SPAN, :] = row.astype(F32).astype(BF16)
+    for copy in copies:
+        copy.wait()
+
+
+def fetch(cells, offset, weights, tails, sems):
     size = SLOTS * BLK
-    copies = [
-        pltpu.make_async_copy(
-            cell.at[pl.ds(offset, size)], weights.at[pl.ds(i * size, size)], sems.at[i]
+    copies = []
+    for i, cell in enumerate(cells):
+        copies.append(
+            pltpu.make_async_copy(
+                cell.at[pl.ds(offset + size, TAIL)], tails.at[pl.ds(i * TAIL, TAIL)], sems.at[1, i]
+            )
         )
-        for i, cell in enumerate(cells)
-    ]
+    for i, cell in enumerate(cells):
+        copies.append(
+            pltpu.make_async_copy(
+                cell.at[pl.ds(offset, size)], weights.at[pl.ds(i * size, size)], sems.at[0, i]
+            )
+        )
     for copy in copies:
         copy.start()
-    return copies
-
-
-def list_blocks(place_ref, meta_ref, phase, inward, blocks):
-    sign = 1 - 2 * place_ref[0]
-    start = 0 if inward else SLOTS + 1
+    return copies[:GRID_ROWS], copies[GRID_ROWS:]
+
+
+def read_table(copies, tails, table):
+    for copy in copies:
+        copy.wait()
+    for i in range(GRID_ROWS):
+        rows = tails[i * TAIL : (i + 1) * TAIL, :].astype(F32).astype(jnp.int32)
+        table[i : i + 1, :] = rows[0:1, :]
+
+
+def list_blocks(table, small, dummy, blocks):
+    pltpu.sync_copy(table, small)
     used = 0
-    for i, offset in enumerate(OFFSETS):
-        row = lax.rem(place_ref[4] + sign * offset + 2 * GRID_ROWS, GRID_ROWS)
-        base = phase * GRID_ROWS + row
+    for i in range(GRID_ROWS):
         for n in range(SLOTS):
-            slot = meta_ref[base, start + n]
-            model, hid = row * DBL + slot // FBL, lax.rem(slot, FBL)
             blocks[0, used + n] = i * SLOTS + n
-            blocks[1, used + n] = model if inward else hid
-            blocks[2, used + n] = hid if inward else model
-        used = used + meta_ref[base, start + SLOTS]
+            blocks[1, used + n] = small[i, n]
+            blocks[2, used + n] = small[i, SLOTS + n]
+        used = used + small[i, 2 * SLOTS]
     for n in range(UNROLL):
         blocks[0, used + n] = 0
         blocks[1, used + n] = 0
-        blocks[2, used + n] = FBL if inward else BLOCKS
+        blocks[2, used + n] = dummy
     return used
 
 
@@ -116,24 +148,25 @@
         own_ref[e] = x_ref[0, :, pl.ds(start, WIDTH)]
 
 
-def first_in_kernel(place_ref, meta_ref, normed_ref, *refs):
+def first_in_kernel(normed_ref, *refs):
     cells = refs[:GRID_ROWS]
-    hidden_ref, total, weights, blocks, sems = refs[GRID_ROWS:]
-    copies = fetch(cells, 0, weights, sems)
-    used = list_blocks(place_ref, meta_ref, 0, True, blocks)
+    hidden_ref, total, weights, tails, table, small, blocks, sems = refs[GRID_ROWS:]
+    tail_copies, copies = fetch(cells, 0, weights, tails, sems)
+    read_table(tail_copies, tails, table)
     total[...] = jnp.zeros_like(total)
+    used = list_blocks(table, small, FBL, blocks)
     for copy in copies:
         copy.wait()
     block_sum(normed_ref, weights, blocks, used, total)
     gelu_into(total, hidden_ref)
 
 
-def later_in_kernel(place_ref, meta_ref, gain_ref, *refs):
+def later_in_kernel(place_ref, gain_ref, *refs):
     bundles = refs[:SIDE]
     cells = refs[SIDE : SIDE + GRID_ROWS]
-    hidden_ref, normed, total, weights, blocks, sems = refs[SIDE + GRID_ROWS :]
-    copies = fetch(cells, 0, weights, sems)
-    used = list_blocks(place_ref, meta_ref, 1, True, blocks)
+    hidden_ref, normed, total, weights, tails, table, small, blocks, sems = refs[SIDE + GRID_ROWS :]
+    tail_copies, copies = fetch(cells, 0, weights, tails, sems)
+    read_table(tail_copies, tails, table)
     squares = jnp.zeros((TOK, BLK), F32)
     for d in range(SIDE):
         for e in range(SIDE):
@@ -150,25 +183,28 @@
                 part = bundles[d][e, :, q * BLK : (q + 1) * BLK].astype(F32)
                 normed[k] = (part * scale * gain_ref[k]).astype(BF16)
     total[...] = jnp.zeros_like(total)
+    used = list_blocks(table, small, FBL, blocks)
     for copy in copies:
         copy.wait()
     block_sum(normed, weights, blocks, used, total)
     gelu_into(total, hidden_ref)
 
 
-def out_kernel(phase, place_ref, meta_ref, hidden_ref, *refs):
+def out_kernel(phase, place_ref, hidden_ref, *refs):
     cells = refs[:GRID_ROWS]
     sends = refs[GRID_ROWS : GRID_ROWS + SIDE]
-    total, weights, blocks, sems = refs[GRID_ROWS + SIDE :]
-    copies = fetch(cells, phase * SLOTS * BLK, weights, sems)
-    used = list_blocks(place_ref, meta_ref, phase, False, blocks)
+    total, weights, tails, table, small, blocks, sems = refs[GRID_ROWS + SIDE :]
+    tail_copies, copies = fetch(cells, phase * SPAN, weights, tails, sems)
+    read_table(tail_copies, tails, table)
     total[...] = jnp.zeros_like(total)
+    used = list_blocks(table, small, BLOCKS, blocks)
     for copy in copies:
         copy.wait()
     block_sum(hidden_ref, weights, blocks, used, total)
     for d in range(SIDE):
         for e in range(SIDE):
-            chunk = chunk_of(place_ref, digit(place_ref[2] + d), e)
+            second = digit(place_ref[3] + e) if phase else e
+            chunk = chunk_of(place_ref, digit(place_ref[2] + d), second)
             for q in range(CHUNK):
                 sends[d][e, :, q * BLK : (q + 1) * BLK] = total[chunk * CHUNK + q].astype(BF16)
 
@@ -192,9 +228,9 @@
     piece_ref[...] = bundle_ref[place_ref[3]]
 
 
-def piece_sum_kernel(place_ref, *refs):
+def piece_sum_kernel(*refs):
     for e, piece in enumerate(refs[SIDE:]):
-        piece[...] = sum_of(refs[:SIDE], digit(place_ref[3] + e)).astype(piece.dtype)
+        piece[...] = sum_of(refs[:SIDE], e).astype(piece.dtype)
 
 
 def cost(blocks, moved):
@@ -203,8 +239,11 @@
 
 WORK = [
     pltpu.VMEM((GRID_ROWS * SLOTS * BLK, BLK), BF16),
+    pltpu.VMEM((GRID_ROWS * TAIL, BLK), BF16),
+    pltpu.VMEM((GRID_ROWS, BLK), jnp.int32),
+    pltpu.SMEM((GRID_ROWS, BLK), jnp.int32),
     pltpu.SMEM((3, GRID_ROWS * SLOTS + 2 * SLOTS), jnp.int32),
-    pltpu.SemaphoreType.DMA((GRID_ROWS,)),
+    pltpu.SemaphoreType.DMA((2, GRID_ROWS)),
 ]
 PARAMS = pltpu.CompilerParams(vmem_limit_bytes=16 << 20)
 NORMED = jax.ShapeDtypeStruct((BLOCKS, TOK, BLK), BF16)
@@ -239,23 +278,23 @@
     return pl.BlockSpec(memory_space=pl.ANY)
 
 
-def first_in(place, meta, normed, cells):
+def first_in(normed, cells):
     return pl.pallas_call(
         first_in_kernel,
-        in_specs=[smem(), smem(), vmem()] + [anywhere()] * GRID_ROWS,
+        in_specs=[vmem()] + [anywhere()] * GRID_ROWS,
         out_specs=vmem(),
         out_shape=HIDDEN,
         scratch_shapes=[pltpu.VMEM((FBL + 1, TOK, BLK), F32)] + WORK,
         cost_estimate=cost(512, 8 << 20),
         compiler_params=PARAMS,
         name="first_in",
-    )(place, meta, normed, *cells)
-
-
-def later_in(place, meta, gain, bundles, cells):
+    )(normed, *cells)
+
+
+def later_in(place, gain, bundles, cells):
     return pl.pallas_call(
         later_in_kernel,
-        in_specs=[smem(), smem()] + [vmem()] * (1 + SIDE) + [anywhere()] * GRID_ROWS,
+        in_specs=[smem()] + [vmem()] * (1 + SIDE) + [anywhere()] * GRID_ROWS,
         out_specs=vmem(),
         out_shape=HIDDEN,
         scratch_shapes=[
@@ -266,20 +305,34 @@
         cost_estimate=cost(512, 12 << 20),
         compiler_params=PARAMS,
         name="later_in",
-    )(place, meta, gain, *bundles, *cells)
-
-
-def project_out(phase, place, meta, hidden, cells):
+    )(place, gain, *bundles, *cells)
+
+
+def project_out(phase, place, hidden, cells):
     return pl.pallas_call(
         functools.partial(out_kernel, phase),
-        in_specs=[smem(), smem(), vmem()] + [anywhere()] * GRID_ROWS,
+        in_specs=[smem(), vmem()] + [anywhere()] * GRID_ROWS,
         out_specs=[vmem()] * SIDE,
         out_shape=[BUNDLE] * SIDE,
         scratch_shapes=[pltpu.VMEM((BLOCKS + 1, TOK, BLK), F32)] + WORK,
         cost_estimate=cost(512, 8 << 20),
         compiler_params=PARAMS,
         name="project_out",
-    )(place, meta, hidden, *cells)
+    )(place, hidden, *cells)
+
+
+def pack(place, *sources):
+    shape = jax.ShapeDtypeStruct((SPAN, BLK), BF16)
+    return pl.pallas_call(
+        pack_kernel,
+        in_specs=[smem()] + [anywhere()] * 2 + [smem()] * 4,
+        out_specs=[vmem()] * 2,
+        out_shape=[shape] * 2,
+        scratch_shapes=[pltpu.SemaphoreType.DMA((2,))],
+        cost_estimate=cost(0, 1 << 20),
+        compiler_params=PARAMS,
+        name="pack",
+    )(place, *sources)
 
 
 def add_up(kernel, place, bundles, outs):
@@ -348,24 +401,15 @@
     place = jnp.stack([core, col, first, second, row]).astype(jnp.int32)
     micro = jnp.reshape(core, (1,)).astype(jnp.int32)
 
-    own_meta = jnp.concatenate(
-        [
-            w_in_slot.reshape(SLOTS),
-            w_in_count.reshape(1),
-            w_out_slot.reshape(SLOTS),
-            w_out_count.reshape(1),
-            jnp.zeros((BLK - 2 * SLOTS - 2,), jnp.int32),
-        ]
-    )
-    meta = lax.all_to_all(
-        jnp.broadcast_to(own_meta, (2 * GRID_ROWS, 1, BLK)),
-        ("section", "row"),
-        0,
-        0,
-        tiled=True,
-    ).reshape(2 * GRID_ROWS, BLK)
-    own_in = w_in.reshape(SLOTS * BLK, BLK)
-    own_out = w_out.reshape(SLOTS * BLK, BLK)
+    own_in, own_out = pack(
+        place,
+        w_in.reshape(SLOTS * BLK, BLK),
+        w_out.reshape(SLOTS * BLK, BLK),
+        w_in_slot.reshape(SLOTS),
+        w_out_slot.reshape(SLOTS),
+        w_in_count.reshape(1),
+        w_out_count.reshape(1),
+    )
     own_gain = norm_gain.reshape(BLOCKS, 1, BLK)
     other_in = on_rows(own_in, SWAP)
     other_out = on_rows(own_out, SWAP)
@@ -384,20 +428,20 @@
     gains = [jnp.where(mine, own_gain, other_gain), jnp.where(mine, other_gain, own_gain)]
 
     normed, own_x = first_norm(micro, place, inputs, gains[0])
-    hidden = first_in(place, meta, normed, cells_in)
-    bundles = project_out(0, place, meta, hidden, cells_out)
+    hidden = first_in(normed, cells_in)
+    bundles = project_out(0, place, hidden, cells_out)
     landed = spread(bundles, True)
     sums = add_up(whole_sum_kernel, None, [bundles[0]] + landed, [BUNDLE])[0]
     landed = spread(sums, False)
     middle, piece = add_up(merge_kernel, place, [own_x, sums] + landed, [BUNDLE, PIECE])
 
     bundles = [middle] + spread(middle, True)
-    hidden = later_in(place, meta, gains[1], bundles, later_cells)
-    bundles = project_out(1, place, meta, hidden, later_cells)
+    hidden = later_in(place, gains[1], bundles, later_cells)
+    bundles = project_out(1, place, hidden, later_cells)
     landed = spread(bundles, True)
     sums = add_up(
         piece_sum_kernel,
-        place,
+        None,
         [bundles[0]] + landed,
         [jax.ShapeDtypeStruct((TOK, WIDTH), F32)] + [PIECE] * (SIDE - 1),
     )

time: 145 us -> 139 us (0.959)
  waiting for transfers between devices: 62 us -> 79.3 us
  local copies, waits for them, and re-layouts: 14 us -> 3.3 us
  starting transfers between devices: 43.2 us -> 34.8 us
  other arithmetic: 5.36 us -> 1.04 us
    ppermute x25, waiting for transfers between devices: 17.9 us -> 34.6 us  [on_rows(): return lax.ppermute(value, ('section', 'row'), perm)]
    unnamed x40 -> x12, local copies, waits for them, and re-layouts: 12.5 us -> 3.22 us
    all_to_all x1 -> x0, starting transfers between devices: 5.84 us -> none  [shards(): lax.all_to_all(jnp.broadcast_to(own_meta, (2 * GRID_ROWS, 1, BLK)), ('sec...]
    ppermute x25, starting transfers between devices: 14.7 us -> 10.6 us  [on_rows(): return lax.ppermute(value, ('section', 'row'), perm)]
    ppermute x15, starting transfers between devices: 22.7 us -> 24.3 us  [on_cols(): return lax.ppermute(value, ('section', 'col'), perm)]
    pallas_call x4 -> x5, Pallas kernels: 14.7 us -> 15.3 us  [the longest x2 7.14 us: project_out(): pl.pallas_call(functools.partial(out_kernel, phase), in_specs=[smem(), vm...]
  transfers between devices with their start and end apart: 41 -> 40, of which waited for: 22 -> 27; matrix products, arithmetic and copies ran while one was open for 4% -> 0% of each run, Pallas kernels for 7% -> 6%
where the time goes in v3:
time: 139 us; the launch traced here: 138 us
  waiting for transfers between devices  79.3 us (57%)
  starting transfers between devices  34.8 us (25%)
  Pallas kernels  17.8 us (13%)
  local copies, waits for them, and re-layouts  3.3 us (2%)
  between operations  1.53 us (1%)
    ppermute x15, waiting for transfers between devices, on_cols(): return lax.ppermute(value, ('section', 'col'), perm)  44.7 us
    ppermute x25, waiting for transfers between devices, on_rows(): return lax.ppermute(value, ('section', 'row'), perm)  34.6 us
    ppermute x15, starting transfers between devices, on_cols(): return lax.ppermute(value, ('section', 'col'), perm)  24.3 us
    ppermute x25, starting transfers between devices, on_rows(): return lax.ppermute(value, ('section', 'row'), perm)  10.6 us
    pallas_call x2, Pallas kernels, project_out(): pl.pallas_call(functools.partial(out_kernel, phase), in_specs=[smem(), vm...  7.14 us
    pallas_call x1, Pallas kernels, later_in(): pl.pallas_call(later_in_kernel, in_specs=[smem()] + [vmem()] * (1 + SIDE)...  4.25 us
    unnamed x12, local copies, waits for them, and re-layouts  3.22 us
    pallas_call x1, Pallas kernels, first_in(): pl.pallas_call(first_in_kernel, in_specs=[vmem()] + [anywhere()] * GRID_R...  3.19 us
  transfers between devices with their start and end apart: 40, of which 27 were waited for; matrix products, arithmetic and copies ran while one was open for 0% of the time, Pallas kernels for 6%

profile of v3, /device:TPU:2, one launch (start us, length us, event | category | flops | bytes accessed | tf_op | source)
XLA Modules:
  0.0 137.8 jit_solution(18433379376294257266)
XLA Ops:
  11.0 6.3 %collective-permute-done.2.refs_1_ = bf16[1040,128]{1,0:T(8,128)(2,1)S(1)} collective-permute-done((bf16[1040,128]{1,0:T(8,128)(2,1)S(1)}, bf16[1040,128]{1,0:T(8,128)(2,1)S(1)}, u32[]{:S(2)}, u32[]{:S(2)}) %collective-permute-start.2) | collective-permute-done | bytes 266272 | tf_op jit(solution)/shard_map/ppermute | solution.py:350
  20.2 4.8 %collective-permute-done.3.refs_2_ = bf16[1040,128]{1,0:T(8,128)(2,1)S(1)} collective-permute-done((bf16[1040,128]{1,0:T(8,128)(2,1)S(1)}, bf16[1040,128]{1,0:T(8,128)(2,1)S(1)}, u32[]{:S(2)}, u32[]{:S(2)}) %collective-permute-start.3) | collective-permute-done | bytes 266272 | tf_op jit(solution)/shard_map/ppermute | solution.py:350
  29.1 3.6 %collective-permute-done.4.refs_3_ = bf16[1040,128]{1,0:T(8,128)(2,1)S(1)} collective-permute-done((bf16[1040,128]{1,0:T(8,128)(2,1)S(1)}, bf16[1040,128]{1,0:T(8,128)(2,1)S(1)}, u32[]{:S(2)}, u32[]{:S(2)}) %collective-permute-start.4) | collective-permute-done | bytes 266272 | tf_op jit(solution)/shard_map/ppermute | solution.py:350
  33.4 7.9 %collective-permute-done.12.refs_3_ = bf16[1040,128]{1,0:T(8,128)(2,1)S(1)} collective-permute-done((bf16[1040,128]{1,0:T(8,128)(2,1)S(1)}, bf16[1040,128]{1,0:T(8,128)(2,1)S(1)}, u32[]{:S(2)}, u32[]{:S(2)}) %collective-permute-start.12) | collective-permute-done | bytes 266272 | tf_op jit(solution)/shard_map/ppermute | solution.py:350
  41.3 2.8 %collective-permute-done.5.refs_4_ = bf16[1040,128]{1,0:T(8,128)(2,1)S(1)} collective-permute-done((bf16[1040,128]{1,0:T(8,128)(2,1)S(1)}, bf16[1040,128]{1,0:T(8,128)(2,1)S(1)}, u32[]{:S(2)}, u32[]{:S(2)}) %collective-permute-start.5) | collective-permute-done | bytes 266272 | tf_op jit(solution)/shard_map/ppermute | solution.py:350
  45.6 3.2 %first_in.1.hidden_ref = bf16[12,128,128]{2,1,0:T(8,128)(2,1)S(1)} custom-call(bf16[48,128,128]{2,1,0:T(8,128)(2,1)S(1)} %get-tuple-element.28.normed_ref, bf16[1040,128]{1,0:T(8,128)(2,1)S(1)} %broadcast_select_fusion.3.refs_0_, bf16[1040,128]{1,0:T(8,128)(2,1)S(1)} %collective-permute-done.2.refs_1_, bf16[1040,128]{1,0:T(8,128)(2,1)S(1)} %collective-permute-done.3.refs_2_, ...), custom_call_target="tpu_custom_call" | custom-call | flops 2147483648 | bytes 8388608 | tf_op jit(solution)/shard_map/first_in/pallas_call | solution.py:282
  48.8 3.0 %collective-permute-done.13.refs_4_ = bf16[1040,128]{1,0:T(8,128)(2,1)S(1)} collective-permute-done((bf16[1040,128]{1,0:T(8,128)(2,1)S(1)}, bf16[1040,128]{1,0:T(8,128)(2,1)S(1)}, u32[]{:S(2)}, u32[]{:S(2)}) %collective-permute-start.13) | collective-permute-done | bytes 266272 | tf_op jit(solution)/shard_map/ppermute | solution.py:350
  51.8 3.3 %project_out.2 = (bf16[4,128,384]{2,1,0:T(8,128)(2,1)S(1)}, bf16[4,128,384]{2,1,0:T(8,128)(2,1)S(1)}, bf16[4,128,384]{2,1,0:T(8,128)(2,1)S(1)}, bf16[4,128,384]{2,1,0:T(8,128)(2,1)S(1)}) custom-call(s32[5]{0:T(128)S(1)} %stack.32.place_ref, bf16[12,128,128]{2,1,0:T(8,128)(2,1)S(1)} %first_in.1.hidden_ref, ...), custom_call_target="tpu_custom_call" | custom-call | flops 2147483648 | bytes 8388608 | tf_op jit(solution)/shard_map/project_out/pallas_call | solution.py:312
  57.7 2.5 %collective-permute-start.19 = (bf16[4,128,384]{2,1,0:T(8,128)(2,1)S(1)}, bf16[4,128,384]{2,1,0:T(8,128)(2,1)S(1)}, u32[]{:S(2)}, u32[]{:S(2)}) collective-permute-start(bf16[4,128,384]{2,1,0:T(8,128)(2,1)S(1)} %get-tuple-element.34), channel_id=1, source_target_pairs={{0,3},{1,0},{2,1},{3,2},{4,7},{5,4},{6,5},{7,6},{8,11},{9,8},{10,9... | collective-permute-start | bytes 1179656 | tf_op jit(solution)/shard_map/ppermute | solution.py:354
  60.3 2.7 %collective-permute-done.17.refs_1_ = bf16[4,128,384]{2,1,0:T(8,128)(2,1)S(1)} collective-permute-done((bf16[4,128,384]{2,1,0:T(8,128)(2,1)S(1)}, bf16[4,128,384]{2,1,0:T(8,128)(2,1)S(1)}, u32[]{:S(2)}, u32[]{:S(2)}) %collective-permute-start.17) | collective-permute-done | bytes 393248 | tf_op jit(solution)/shard_map/ppermute | solution.py:354
  62.9 3.1 %collective-permute-done.18.refs_2_ = bf16[4,128,384]{2,1,0:T(8,128)(2,1)S(1)} collective-permute-done((bf16[4,128,384]{2,1,0:T(8,128)(2,1)S(1)}, bf16[4,128,384]{2,1,0:T(8,128)(2,1)S(1)}, u32[]{:S(2)}, u32[]{:S(2)}) %collective-permute-start.18) | collective-permute-done | bytes 393248 | tf_op jit(solution)/shard_map/ppermute | solution.py:354
  66.0 3.7 %collective-permute-done.19.refs_3_ = bf16[4,128,384]{2,1,0:T(8,128)(2,1)S(1)} collective-permute-done((bf16[4,128,384]{2,1,0:T(8,128)(2,1)S(1)}, bf16[4,128,384]{2,1,0:T(8,128)(2,1)S(1)}, u32[]{:S(2)}, u32[]{:S(2)}) %collective-permute-start.19) | collective-permute-done | bytes 393248 | tf_op jit(solution)/shard_map/ppermute | solution.py:354
  72.7 2.5 %collective-permute-start.21 = (bf16[4,128,384]{2,1,0:T(8,128)(2,1)S(1)}, bf16[4,128,384]{2,1,0:T(8,128)(2,1)S(1)}, u32[]{:S(2)}, u32[]{:S(2)}) collective-permute-start(bf16[4,128,384]{2,1,0:T(8,128)(2,1)S(1)} %shard_map.82.refs_1_), channel_id=1, source_target_pairs={{0,8},{1,9},{2,10},{3,11},{4,12},{5,13},{6,14},{7,15},{8,0},{9,1},... | collective-permute-start | bytes 1179656 | tf_op jit(solution)/shard_map/ppermute | solution.py:354
  75.2 3.8 %collective-permute-done.20.refs_2_ = bf16[4,128,384]{2,1,0:T(8,128)(2,1)S(1)} collective-permute-done((bf16[4,128,384]{2,1,0:T(8,128)(2,1)S(1)}, bf16[4,128,384]{2,1,0:T(8,128)(2,1)S(1)}, u32[]{:S(2)}, u32[]{:S(2)}) %collective-permute-start.20) | collective-permute-done | bytes 393248 | tf_op jit(solution)/shard_map/ppermute | solution.py:354
  91.9 3.6 %collective-permute-done.23.refs_1_ = bf16[4,128,384]{2,1,0:T(8,128)(2,1)S(1)} collective-permute-done((bf16[4,128,384]{2,1,0:T(8,128)(2,1)S(1)}, bf16[4,128,384]{2,1,0:T(8,128)(2,1)S(1)}, u32[]{:S(2)}, u32[]{:S(2)}) %collective-permute-start.23) | collective-permute-done | bytes 393248 | tf_op jit(solution)/shard_map/ppermute | solution.py:354
  95.5 2.6 %collective-permute-done.24.refs_2_ = bf16[4,128,384]{2,1,0:T(8,128)(2,1)S(1)} collective-permute-done((bf16[4,128,384]{2,1,0:T(8,128)(2,1)S(1)}, bf16[4,128,384]{2,1,0:T(8,128)(2,1)S(1)}, u32[]{:S(2)}, u32[]{:S(2)}) %collective-permute-start.24) | collective-permute-done | bytes 393248 | tf_op jit(solution)/shard_map/ppermute | solution.py:354
  98.1 4.1 %collective-permute-done.25.refs_3_ = bf16[4,128,384]{2,1,0:T(8,128)(2,1)S(1)} collective-permute-done((bf16[4,128,384]{2,1,0:T(8,128)(2,1)S(1)}, bf16[4,128,384]{2,1,0:T(8,128)(2,1)S(1)}, u32[]{:S(2)}, u32[]{:S(2)}) %collective-permute-start.25) | collective-permute-done | bytes 393248 | tf_op jit(solution)/shard_map/ppermute | solution.py:354
  102.2 4.2 %later_in.1.hidden_ref = bf16[12,128,128]{2,1,0:T(8,128)(2,1)S(1)} custom-call(s32[5]{0:T(128)S(1)} %stack.32.place_ref, f32[48,1,128]{2,1,0:T(1,128)S(1)} %get-tuple-element.53.gain_ref, bf16[4,128,384]{2,1,0:T(8,128)(2,1)S(1)} %get-tuple-element.36.refs_0_, bf16[4,128,384]{2,1,0:T(8,128)(2,1)S(1)} %collective-permute-done.23.refs_1_, ...), custom_call_target="tpu_custom_call" | custom-call | flops 2147483648 | bytes 12582912 | tf_op jit(solution)/shard_map/later_in/pallas_call | solution.py:295
  106.5 3.9 %project_out.3 = (bf16[4,128,384]{2,1,0:T(8,128)(2,1)S(1)}, bf16[4,128,384]{2,1,0:T(8,128)(2,1)S(1)}, bf16[4,128,384]{2,1,0:T(8,128)(2,1)S(1)}, bf16[4,128,384]{2,1,0:T(8,128)(2,1)S(1)}) custom-call(s32[5]{0:T(128)S(1)} %stack.32.place_ref, bf16[12,128,128]{2,1,0:T(8,128)(2,1)S(1)} %later_in.1.hidden_ref, ...), custom_call_target="tpu_custom_call" | custom-call | flops 2147483648 | bytes 8388608 | tf_op jit(solution)/shard_map/project_out/pallas_call | solution.py:312
  113.7 4.5 %collective-permute-done.33.refs_1_ = bf16[4,128,384]{2,1,0:T(8,128)(2,1)S(1)} collective-permute-done((bf16[4,128,384]{2,1,0:T(8,128)(2,1)S(1)}, bf16[4,128,384]{2,1,0:T(8,128)(2,1)S(1)}, u32[]{:S(2)}, u32[]{:S(2)}) %collective-permute-start.33) | collective-permute-done | bytes 393248 | tf_op jit(solution)/shard_map/ppermute | solution.py:354
  119.9 4.8 %collective-permute-done.35.refs_3_ = bf16[4,128,384]{2,1,0:T(8,128)(2,1)S(1)} collective-permute-done((bf16[4,128,384]{2,1,0:T(8,128)(2,1)S(1)}, bf16[4,128,384]{2,1,0:T(8,128)(2,1)S(1)}, u32[]{:S(2)}, u32[]{:S(2)}) %collective-permute-start.35) | collective-permute-done | bytes 393248 | tf_op jit(solution)/shard_map/ppermute | solution.py:354
  124.9 3.8 %collective-permute-start.38 = (bf16[128,384]{1,0:T(8,128)(2,1)S(1)}, bf16[128,384]{1,0:T(8,128)(2,1)S(1)}, u32[]{:S(2)}, u32[]{:S(2)}) collective-permute-start(bf16[128,384]{1,0:T(8,128)(2,1)S(1)} %get-tuple-element.48), channel_id=1, source_target_pairs={{0,12},{1,13},{2,14},{3,15},{4,0},{5,1},{6,2},{7,3},{8,4},{9,5},{1... | collective-permute-start | bytes 294920 | tf_op jit(solution)/shard_map/ppermute | solution.py:354
  129.7 2.3 %collective-permute-done.38 = bf16[128,384]{1,0:T(8,128)(2,1)S(1)} collective-permute-done((bf16[128,384]{1,0:T(8,128)(2,1)S(1)}, bf16[128,384]{1,0:T(8,128)(2,1)S(1)}, u32[]{:S(2)}, u32[]{:S(2)}) %collective-permute-start.38) | collective-permute-done | bytes 98336 | tf_op jit(solution)/shard_map/ppermute | solution.py:354
  131.9 3.0 %collective-permute-done.37 = bf16[128,384]{1,0:T(8,128)(2,1)S(1)} collective-permute-done((bf16[128,384]{1,0:T(8,128)(2,1)S(1)}, bf16[128,384]{1,0:T(8,128)(2,1)S(1)}, u32[]{:S(2)}, u32[]{:S(2)}) %collective-permute-start.37) | collective-permute-done | bytes 98336 | tf_op jit(solution)/shard_map/ppermute | solution.py:354
  (86 shorter events, 46.3 us)
Async XLA Ops:
  7.0 10.3 %collective-permute-start.2 = (bf16[1040,128]{1,0:T(8,128)(2,1)S(1)}, bf16[1040,128]{1,0:T(8,128)(2,1)S(1)}, u32[]{:S(2)}, u32[]{:S(2)}) collective-permute-start(bf16[1040,128]{1,0:T(8,128)(2,1)S(1)} %broadcast_select_fusion.3.refs_0_), channel_id=1, source_target_pairs={{0,16},{16,32},{32,48},{48,64},{64,80},{80,96},{96,112},{112,0},{1... | collective-permute-start | bytes 798728 | tf_op jit(solution)/shard_map/ppermute | solution.py:350
  9.0 11.1 %collective-permute-start.10 = (bf16[1040,128]{1,0:T(8,128)(2,1)S(1)}, bf16[1040,128]{1,0:T(8,128)(2,1)S(1)}, u32[]{:S(2)}, u32[]{:S(2)}) collective-permute-start(bf16[1040,128]{1,0:T(8,128)(2,1)S(1)} %broadcast_select_fusion.2.refs_0_), channel_id=1, source_target_pairs={{0,16},{16,32},{32,48},{48,64},{64,80},{80,96},{96,112},{112,0},{1... | collective-permute-start | bytes 798728 | tf_op jit(solution)/shard_map/ppermute | solution.py:350
  17.3 15.5 %collective-permute-start.6 = (bf16[1040,128]{1,0:T(8,128)(2,1)S(1)}, bf16[1040,128]{1,0:T(8,128)(2,1)S(1)}, u32[]{:S(2)}, u32[]{:S(2)}) collective-permute-start(bf16[1040,128]{1,0:T(8,128)(2,1)S(1)} %collective-permute-done.2.refs_1_), channel_id=1, source_target_pairs={{0,128},{16,144},{32,160},{48,176},{64,192},{80,208},{96,224},{112... | collective-permute-start | bytes 798728 | tf_op jit(solution)/shard_map/ppermute | solution.py:350
  25.2 20.3 %collective-permute-start.26 = (bf16[2080,128]{1,0:T(8,128)(2,1)S(1)}, bf16[2080,128]{1,0:T(8,128)(2,1)S(1)}, u32[]{:S(2)}, u32[]{:S(2)}) collective-permute-start(bf16[2080,128]{1,0:T(8,128)(2,1)S(1)} %pad_maximum_fusion.refs_4_.refs_0_), channel_id=1, source_target_pairs={{0,16},{16,32},{32,48},{48,64},{64,80},{80,96},{96,112},{112,0},{1... | collective-permute-start | bytes 1597448 | tf_op jit(solution)/shard_map/ppermute | solution.py:350
  27.8 13.5 %collective-permute-start.12 = (bf16[1040,128]{1,0:T(8,128)(2,1)S(1)}, bf16[1040,128]{1,0:T(8,128)(2,1)S(1)}, u32[]{:S(2)}, u32[]{:S(2)}) collective-permute-start(bf16[1040,128]{1,0:T(8,128)(2,1)S(1)} %collective-permute-done.11.refs_2_), channel_id=1, source_target_pairs={{0,16},{16,32},{32,48},{48,64},{64,80},{80,96},{96,112},{112,0},{1... | collective-permute-start | bytes 798728 | tf_op jit(solution)/shard_map/ppermute | solution.py:350
  32.7 11.4 %collective-permute-start.5 = (bf16[1040,128]{1,0:T(8,128)(2,1)S(1)}, bf16[1040,128]{1,0:T(8,128)(2,1)S(1)}, u32[]{:S(2)}, u32[]{:S(2)}) collective-permute-start(bf16[1040,128]{1,0:T(8,128)(2,1)S(1)} %collective-permute-done.4.refs_3_), channel_id=1, source_target_pairs={{0,16},{16,32},{32,48},{48,64},{64,80},{80,96},{96,112},{112,0},{1... | collective-permute-start | bytes 798728 | tf_op jit(solution)/shard_map/ppermute | solution.py:350
  32.8 11.3 %collective-permute-start.8 = (bf16[1040,128]{1,0:T(8,128)(2,1)S(1)}, bf16[1040,128]{1,0:T(8,128)(2,1)S(1)}, u32[]{:S(2)}, u32[]{:S(2)}) collective-permute-start(bf16[1040,128]{1,0:T(8,128)(2,1)S(1)} %collective-permute-done.4.refs_3_), channel_id=1, source_target_pairs={{0,128},{16,144},{32,160},{48,176},{64,192},{80,208},{96,224},{112... | collective-permute-start | bytes 798728 | tf_op jit(solution)/shard_map/ppermute | solution.py:350
  32.9 15.9 %collective-permute-start.14 = (bf16[1040,128]{1,0:T(8,128)(2,1)S(1)}, bf16[1040,128]{1,0:T(8,128)(2,1)S(1)}, u32[]{:S(2)}, u32[]{:S(2)}) collective-permute-start(bf16[1040,128]{1,0:T(8,128)(2,1)S(1)} %collective-permute-done.10.refs_1_), channel_id=1, source_target_pairs={{0,128},{16,144},{32,160},{48,176},{64,192},{80,208},{96,224},{112... | collective-permute-start | bytes 798728 | tf_op jit(solution)/shard_map/ppermute | solution.py:350
  45.5 26.7 %collective-permute-start.27 = (bf16[2080,128]{1,0:T(8,128)(2,1)S(1)}, bf16[2080,128]{1,0:T(8,128)(2,1)S(1)}, u32[]{:S(2)}, u32[]{:S(2)}) collective-permute-start(bf16[2080,128]{1,0:T(8,128)(2,1)S(1)} %collective-permute-done.26.refs_5_.refs_1_), channel_id=1, source_target_pairs={{0,16},{16,32},{32,48},{48,64},{64,80},{80,96},{96,112},{112,0},{1... | collective-permute-start | bytes 1597448 | tf_op jit(solution)/shard_map/ppermute | solution.py:350
  55.1 7.9 %collective-permute-start.17 = (bf16[4,128,384]{2,1,0:T(8,128)(2,1)S(1)}, bf16[4,128,384]{2,1,0:T(8,128)(2,1)S(1)}, u32[]{:S(2)}, u32[]{:S(2)}) collective-permute-start(bf16[4,128,384]{2,1,0:T(8,128)(2,1)S(1)} %get-tuple-element.32), channel_id=1, source_target_pairs={{0,1},{1,2},{2,3},{3,0},{4,5},{5,6},{6,7},{7,4},{8,9},{9,10},{10,1... | collective-permute-start | bytes 1179656 | tf_op jit(solution)/shard_map/ppermute | solution.py:354
  56.6 9.4 %collective-permute-start.18 = (bf16[4,128,384]{2,1,0:T(8,128)(2,1)S(1)}, bf16[4,128,384]{2,1,0:T(8,128)(2,1)S(1)}, u32[]{:S(2)}, u32[]{:S(2)}) collective-permute-start(bf16[4,128,384]{2,1,0:T(8,128)(2,1)S(1)} %get-tuple-element.33), channel_id=1, source_target_pairs={{0,2},{1,3},{2,0},{3,1},{4,6},{5,7},{6,4},{7,5},{8,10},{9,11},{10,... | collective-permute-start | bytes 1179656 | tf_op jit(solution)/shard_map/ppermute | solution.py:354
  57.7 12.0 %collective-permute-start.19 = (bf16[4,128,384]{2,1,0:T(8,128)(2,1)S(1)}, bf16[4,128,384]{2,1,0:T(8,128)(2,1)S(1)}, u32[]{:S(2)}, u32[]{:S(2)}) collective-permute-start(bf16[4,128,384]{2,1,0:T(8,128)(2,1)S(1)} %get-tuple-element.34), channel_id=1, source_target_pairs={{0,3},{1,0},{2,1},{3,2},{4,7},{5,4},{6,5},{7,6},{8,11},{9,8},{10,9... | collective-permute-start | bytes 1179656 | tf_op jit(solution)/shard_map/ppermute | solution.py:354
  69.9 9.1 %collective-permute-start.20 = (bf16[4,128,384]{2,1,0:T(8,128)(2,1)S(1)}, bf16[4,128,384]{2,1,0:T(8,128)(2,1)S(1)}, u32[]{:S(2)}, u32[]{:S(2)}) collective-permute-start(bf16[4,128,384]{2,1,0:T(8,128)(2,1)S(1)} %shard_map.82.refs_1_), channel_id=1, source_target_pairs={{0,4},{1,5},{2,6},{3,7},{4,8},{5,9},{6,10},{7,11},{8,12},{9,13},{1... | collective-permute-start | bytes 1179656 | tf_op jit(solution)/shard_map/ppermute | solution.py:354
  72.2 10.5 %collective-permute-start.28 = (bf16[2080,128]{1,0:T(8,128)(2,1)S(1)}, bf16[2080,128]{1,0:T(8,128)(2,1)S(1)}, u32[]{:S(2)}, u32[]{:S(2)}) collective-permute-start(bf16[2080,128]{1,0:T(8,128)(2,1)S(1)} %collective-permute-done.27.refs_6_.refs_2_), channel_id=1, source_target_pairs={{0,16},{16,32},{32,48},{48,64},{64,80},{80,96},{96,112},{112,0},{1... | collective-permute-start | bytes 1597448 | tf_op jit(solution)/shard_map/ppermute | solution.py:350
  72.2 16.6 %collective-permute-start.30 = (bf16[2080,128]{1,0:T(8,128)(2,1)S(1)}, bf16[2080,128]{1,0:T(8,128)(2,1)S(1)}, u32[]{:S(2)}, u32[]{:S(2)}) collective-permute-start(bf16[2080,128]{1,0:T(8,128)(2,1)S(1)} %collective-permute-done.26.refs_5_.refs_1_), channel_id=1, source_target_pairs={{0,128},{16,144},{32,160},{48,176},{64,192},{80,208},{96,224},{112... | collective-permute-start | bytes 1597448 | tf_op jit(solution)/shard_map/ppermute | solution.py:350
  72.2 18.1 %collective-permute-start.31 = (bf16[2080,128]{1,0:T(8,128)(2,1)S(1)}, bf16[2080,128]{1,0:T(8,128)(2,1)S(1)}, u32[]{:S(2)}, u32[]{:S(2)}) collective-permute-start(bf16[2080,128]{1,0:T(8,128)(2,1)S(1)} %collective-permute-done.27.refs_6_.refs_2_), channel_id=1, source_target_pairs={{0,128},{16,144},{32,160},{48,176},{64,192},{80,208},{96,224},{112... | collective-permute-start | bytes 1597448 | tf_op jit(solution)/shard_map/ppermute | solution.py:350
  72.7 12.0 %collective-permute-start.21 = (bf16[4,128,384]{2,1,0:T(8,128)(2,1)S(1)}, bf16[4,128,384]{2,1,0:T(8,128)(2,1)S(1)}, u32[]{:S(2)}, u32[]{:S(2)}) collective-permute-start(bf16[4,128,384]{2,1,0:T(8,128)(2,1)S(1)} %shard_map.82.refs_1_), channel_id=1, source_target_pairs={{0,8},{1,9},{2,10},{3,11},{4,12},{5,13},{6,14},{7,15},{8,0},{9,1},... | collective-permute-start | bytes 1179656 | tf_op jit(solution)/shard_map/ppermute | solution.py:354
  82.6 19.6 %collective-permute-start.29 = (bf16[2080,128]{1,0:T(8,128)(2,1)S(1)}, bf16[2080,128]{1,0:T(8,128)(2,1)S(1)}, u32[]{:S(2)}, u32[]{:S(2)}) collective-permute-start(bf16[2080,128]{1,0:T(8,128)(2,1)S(1)} %collective-permute-done.28.refs_7_.refs_3_), channel_id=1, source_target_pairs={{0,16},{16,32},{32,48},{48,64},{64,80},{80,96},{96,112},{112,0},{1... | collective-permute-start | bytes 1597448 | tf_op jit(solution)/shard_map/ppermute | solution.py:350
  84.7 17.6 %collective-permute-start.32 = (bf16[2080,128]{1,0:T(8,128)(2,1)S(1)}, bf16[2080,128]{1,0:T(8,128)(2,1)S(1)}, u32[]{:S(2)}, u32[]{:S(2)}) collective-permute-start(bf16[2080,128]{1,0:T(8,128)(2,1)S(1)} %collective-permute-done.28.refs_7_.refs_3_), channel_id=1, source_target_pairs={{0,128},{16,144},{32,160},{48,176},{64,192},{80,208},{96,224},{112... | collective-permute-start | bytes 1597448 | tf_op jit(solution)/shard_map/ppermute | solution.py:350
  88.7 9.4 %collective-permute-start.24 = (bf16[4,128,384]{2,1,0:T(8,128)(2,1)S(1)}, bf16[4,128,384]{2,1,0:T(8,128)(2,1)S(1)}, u32[]{:S(2)}, u32[]{:S(2)}) collective-permute-start(bf16[4,128,384]{2,1,0:T(8,128)(2,1)S(1)} %get-tuple-element.36.refs_0_), channel_id=1, source_target_pairs={{0,2},{1,3},{2,0},{3,1},{4,6},{5,7},{6,4},{7,5},{8,10},{9,11},{10,... | collective-permute-start | bytes 1179656 | tf_op jit(solution)/shard_map/ppermute | solution.py:354
  90.3 11.9 %collective-permute-start.25 = (bf16[4,128,384]{2,1,0:T(8,128)(2,1)S(1)}, bf16[4,128,384]{2,1,0:T(8,128)(2,1)S(1)}, u32[]{:S(2)}, u32[]{:S(2)}) collective-permute-start(bf16[4,128,384]{2,1,0:T(8,128)(2,1)S(1)} %get-tuple-element.36.refs_0_), channel_id=1, source_target_pairs={{0,3},{1,0},{2,1},{3,2},{4,7},{5,4},{6,5},{7,6},{8,11},{9,8},{10,9... | collective-permute-start | bytes 1179656 | tf_op jit(solution)/shard_map/ppermute | solution.py:354
  110.4 7.9 %collective-permute-start.33 = (bf16[4,128,384]{2,1,0:T(8,128)(2,1)S(1)}, bf16[4,128,384]{2,1,0:T(8,128)(2,1)S(1)}, u32[]{:S(2)}, u32[]{:S(2)}) collective-permute-start(bf16[4,128,384]{2,1,0:T(8,128)(2,1)S(1)} %get-tuple-element.42), channel_id=1, source_target_pairs={{0,1},{1,2},{2,3},{3,0},{4,5},{5,6},{6,7},{7,4},{8,9},{9,10},{10,1... | collective-permute-start | bytes 1179656 | tf_op jit(solution)/shard_map/ppermute | solution.py:354
  110.4 9.5 %collective-permute-start.34 = (bf16[4,128,384]{2,1,0:T(8,128)(2,1)S(1)}, bf16[4,128,384]{2,1,0:T(8,128)(2,1)S(1)}, u32[]{:S(2)}, u32[]{:S(2)}) collective-permute-start(bf16[4,128,384]{2,1,0:T(8,128)(2,1)S(1)} %get-tuple-element.43), channel_id=1, source_target_pairs={{0,2},{1,3},{2,0},{3,1},{4,6},{5,7},{6,4},{7,5},{8,10},{9,11},{10,... | collective-permute-start | bytes 1179656 | tf_op jit(solution)/shard_map/ppermute | solution.py:354
  112.1 12.6 %collective-permute-start.35 = (bf16[4,128,384]{2,1,0:T(8,128)(2,1)S(1)}, bf16[4,128,384]{2,1,0:T(8,128)(2,1)S(1)}, u32[]{:S(2)}, u32[]{:S(2)}) collective-permute-start(bf16[4,128,384]{2,1,0:T(8,128)(2,1)S(1)} %get-tuple-element.44), channel_id=1, source_target_pairs={{0,3},{1,0},{2,1},{3,2},{4,7},{5,4},{6,5},{7,6},{8,11},{9,8},{10,9... | collective-permute-start | bytes 1179656 | tf_op jit(solution)/shard_map/ppermute | solution.py:354
  (22 other events, 150.3 us)

commit v4 on v3

--- a/solution.py
+++ b/solution.py
@@ -46,19 +46,25 @@
 
 
 def pack_kernel(place_ref, *refs):
-    sources, outs, sems = refs[:6], refs[6:8], refs[8]
+    sources, outs, slots, counts, sems = refs[:6], refs[6:8], refs[8:10], refs[10:12], refs[12]
+    small = [
+        pltpu.make_async_copy(source, target, sems.at[2 + k])
+        for k, (source, target) in enumerate(zip(sources[2:], slots + counts))
+    ]
     copies = [
         pltpu.make_async_copy(sources[k], outs[k].at[pl.ds(0, SLOTS * BLK)], sems.at[k])
         for k in range(2)
     ]
-    for copy in copies:
+    for copy in small + copies:
         copy.start()
+    for copy in small:
+        copy.wait()
     lane = lax.broadcasted_iota(jnp.int32, (TAIL, BLK), 1)
     for k, out in enumerate(outs):
-        slots, count = sources[2 + k], sources[4 + k]
-        row = jnp.where(lane == 2 * SLOTS, count[0], 0)
+        row = jnp.where(lane == 2 * SLOTS, counts[k][0], 0)
         for n in range(SLOTS):
-            model, hid = place_ref[4] * DBL + slots[n] // FBL, lax.rem(slots[n], FBL)
+            slot = slots[k][n]
+            model, hid = place_ref[4] * DBL + slot // FBL, lax.rem(slot, FBL)
             row = jnp.where(lane == n, hid if k else model, row)
             row = jnp.where(lane == SLOTS + n, model if k else hid, row)
         out[SLOTS * BLK : SPAN, :] = row.astype(F32).astype(BF16)
@@ -325,14 +331,16 @@
     shape = jax.ShapeDtypeStruct((SPAN, BLK), BF16)
     return pl.pallas_call(
         pack_kernel,
-        in_specs=[smem()] + [anywhere()] * 2 + [smem()] * 4,
+        in_specs=[smem()] + [pl.BlockSpec(memory_space=pltpu.HBM)] * 6,
         out_specs=[vmem()] * 2,
         out_shape=[shape] * 2,
-        scratch_shapes=[pltpu.SemaphoreType.DMA((2,))],
+        scratch_shapes=[pltpu.SMEM((SLOTS,), jnp.int32)] * 2
+        + [pltpu.SMEM((1,), jnp.int32)] * 2
+        + [pltpu.SemaphoreType.DMA((6,))],
         cost_estimate=cost(0, 1 << 20),
         compiler_params=PARAMS,
         name="pack",
-    )(place, *sources)
+    )(place, *[pltpu.with_memory_space_constraint(v, pltpu.HBM) for v in sources[:4]], *sources[4:])
 
 
 def add_up(kernel, place, bundles, outs):

time: 139 us -> 136 us (0.978)
  local copies, waits for them, and re-layouts: 3.3 us -> 0.09 us
    unnamed x12 -> x4, local copies, waits for them, and re-layouts: 3.22 us -> 0.01 us
where the time goes in v4:
time: 136 us
  waiting for transfers between devices  79.3 us (58%)
  starting transfers between devices  34.8 us (26%)
  Pallas kernels  18.7 us (14%)
  between operations  1.53 us (1%)
    ppermute x15, waiting for transfers between devices, on_cols(): return lax.ppermute(value, ('section', 'col'), perm)  44.7 us
    ppermute x25, waiting for transfers between devices, on_rows(): return lax.ppermute(value, ('section', 'row'), perm)  34.6 us
    ppermute x15, starting transfers between devices, on_cols(): return lax.ppermute(value, ('section', 'col'), perm)  24.3 us
    ppermute x25, starting transfers between devices, on_rows(): return lax.ppermute(value, ('section', 'row'), perm)  10.6 us
    pallas_call x2, Pallas kernels, project_out(): pl.pallas_call(functools.partial(out_kernel, phase), in_specs=[smem(), vm...  7.14 us
    pallas_call x1, Pallas kernels, later_in(): pl.pallas_call(later_in_kernel, in_specs=[smem()] + [vmem()] * (1 + SIDE)...  4.25 us
    pallas_call x1, Pallas kernels, first_in(): pl.pallas_call(first_in_kernel, in_specs=[vmem()] + [anywhere()] * GRID_R...  3.19 us
  transfers between devices with their start and end apart: 40, of which 27 were waited for; matrix products, arithmetic and copies ran while one was open for 0% of the time, Pallas kernels for 6%

profile of v4, /device:TPU:2, one launch (start us, length us, event | category | flops | bytes accessed | tf_op | source)
XLA Modules:
  0.0 135.5 jit_solution(9477434340711969701)
XLA Ops:
  8.7 6.3 %collective-permute-done.2.refs_1_ = bf16[1040,128]{1,0:T(8,128)(2,1)S(1)} collective-permute-done((bf16[1040,128]{1,0:T(8,128)(2,1)S(1)}, bf16[1040,128]{1,0:T(8,128)(2,1)S(1)}, u32[]{:S(2)}, u32[]{:S(2)}) %collective-permute-start.2) | collective-permute-done | bytes 266272 | tf_op jit(solution)/shard_map/ppermute | solution.py:358
  17.9 4.8 %collective-permute-done.3.refs_2_ = bf16[1040,128]{1,0:T(8,128)(2,1)S(1)} collective-permute-done((bf16[1040,128]{1,0:T(8,128)(2,1)S(1)}, bf16[1040,128]{1,0:T(8,128)(2,1)S(1)}, u32[]{:S(2)}, u32[]{:S(2)}) %collective-permute-start.3) | collective-permute-done | bytes 266272 | tf_op jit(solution)/shard_map/ppermute | solution.py:358
  26.9 3.6 %collective-permute-done.4.refs_3_ = bf16[1040,128]{1,0:T(8,128)(2,1)S(1)} collective-permute-done((bf16[1040,128]{1,0:T(8,128)(2,1)S(1)}, bf16[1040,128]{1,0:T(8,128)(2,1)S(1)}, u32[]{:S(2)}, u32[]{:S(2)}) %collective-permute-start.4) | collective-permute-done | bytes 266272 | tf_op jit(solution)/shard_map/ppermute | solution.py:358
  31.1 7.9 %collective-permute-done.12.refs_3_ = bf16[1040,128]{1,0:T(8,128)(2,1)S(1)} collective-permute-done((bf16[1040,128]{1,0:T(8,128)(2,1)S(1)}, bf16[1040,128]{1,0:T(8,128)(2,1)S(1)}, u32[]{:S(2)}, u32[]{:S(2)}) %collective-permute-start.12) | collective-permute-done | bytes 266272 | tf_op jit(solution)/shard_map/ppermute | solution.py:358
  39.0 2.8 %collective-permute-done.5.refs_4_ = bf16[1040,128]{1,0:T(8,128)(2,1)S(1)} collective-permute-done((bf16[1040,128]{1,0:T(8,128)(2,1)S(1)}, bf16[1040,128]{1,0:T(8,128)(2,1)S(1)}, u32[]{:S(2)}, u32[]{:S(2)}) %collective-permute-start.5) | collective-permute-done | bytes 266272 | tf_op jit(solution)/shard_map/ppermute | solution.py:358
  43.3 3.2 %first_in.1.hidden_ref = bf16[12,128,128]{2,1,0:T(8,128)(2,1)S(1)} custom-call(bf16[48,128,128]{2,1,0:T(8,128)(2,1)S(1)} %get-tuple-element.28.normed_ref, bf16[1040,128]{1,0:T(8,128)(2,1)S(1)} %broadcast_select_fusion.3.refs_0_, bf16[1040,128]{1,0:T(8,128)(2,1)S(1)} %collective-permute-done.2.refs_1_, bf16[1040,128]{1,0:T(8,128)(2,1)S(1)} %collective-permute-done.3.refs_2_, ...), custom_call_target="tpu_custom_call" | custom-call | flops 2147483648 | bytes 8388608 | tf_op jit(solution)/shard_map/first_in/pallas_call | solution.py:288
  46.5 3.0 %collective-permute-done.13.refs_4_ = bf16[1040,128]{1,0:T(8,128)(2,1)S(1)} collective-permute-done((bf16[1040,128]{1,0:T(8,128)(2,1)S(1)}, bf16[1040,128]{1,0:T(8,128)(2,1)S(1)}, u32[]{:S(2)}, u32[]{:S(2)}) %collective-permute-start.13) | collective-permute-done | bytes 266272 | tf_op jit(solution)/shard_map/ppermute | solution.py:358
  49.5 3.3 %project_out.2 = (bf16[4,128,384]{2,1,0:T(8,128)(2,1)S(1)}, bf16[4,128,384]{2,1,0:T(8,128)(2,1)S(1)}, bf16[4,128,384]{2,1,0:T(8,128)(2,1)S(1)}, bf16[4,128,384]{2,1,0:T(8,128)(2,1)S(1)}) custom-call(s32[5]{0:T(128)S(1)} %stack.32.place_ref, bf16[12,128,128]{2,1,0:T(8,128)(2,1)S(1)} %first_in.1.hidden_ref, ...), custom_call_target="tpu_custom_call" | custom-call | flops 2147483648 | bytes 8388608 | tf_op jit(solution)/shard_map/project_out/pallas_call | solution.py:318
  55.4 2.5 %collective-permute-start.19 = (bf16[4,128,384]{2,1,0:T(8,128)(2,1)S(1)}, bf16[4,128,384]{2,1,0:T(8,128)(2,1)S(1)}, u32[]{:S(2)}, u32[]{:S(2)}) collective-permute-start(bf16[4,128,384]{2,1,0:T(8,128)(2,1)S(1)} %get-tuple-element.34), channel_id=1, source_target_pairs={{0,3},{1,0},{2,1},{3,2},{4,7},{5,4},{6,5},{7,6},{8,11},{9,8},{10,9... | collective-permute-start | bytes 1179656 | tf_op jit(solution)/shard_map/ppermute | solution.py:362
  58.0 2.7 %collective-permute-done.17.refs_1_ = bf16[4,128,384]{2,1,0:T(8,128)(2,1)S(1)} collective-permute-done((bf16[4,128,384]{2,1,0:T(8,128)(2,1)S(1)}, bf16[4,128,384]{2,1,0:T(8,128)(2,1)S(1)}, u32[]{:S(2)}, u32[]{:S(2)}) %collective-permute-start.17) | collective-permute-done | bytes 393248 | tf_op jit(solution)/shard_map/ppermute | solution.py:362
  60.6 3.1 %collective-permute-done.18.refs_2_ = bf16[4,128,384]{2,1,0:T(8,128)(2,1)S(1)} collective-permute-done((bf16[4,128,384]{2,1,0:T(8,128)(2,1)S(1)}, bf16[4,128,384]{2,1,0:T(8,128)(2,1)S(1)}, u32[]{:S(2)}, u32[]{:S(2)}) %collective-permute-start.18) | collective-permute-done | bytes 393248 | tf_op jit(solution)/shard_map/ppermute | solution.py:362
  63.7 3.7 %collective-permute-done.19.refs_3_ = bf16[4,128,384]{2,1,0:T(8,128)(2,1)S(1)} collective-permute-done((bf16[4,128,384]{2,1,0:T(8,128)(2,1)S(1)}, bf16[4,128,384]{2,1,0:T(8,128)(2,1)S(1)}, u32[]{:S(2)}, u32[]{:S(2)}) %collective-permute-start.19) | collective-permute-done | bytes 393248 | tf_op jit(solution)/shard_map/ppermute | solution.py:362
  70.4 2.5 %collective-permute-start.21 = (bf16[4,128,384]{2,1,0:T(8,128)(2,1)S(1)}, bf16[4,128,384]{2,1,0:T(8,128)(2,1)S(1)}, u32[]{:S(2)}, u32[]{:S(2)}) collective-permute-start(bf16[4,128,384]{2,1,0:T(8,128)(2,1)S(1)} %shard_map.82.refs_1_), channel_id=1, source_target_pairs={{0,8},{1,9},{2,10},{3,11},{4,12},{5,13},{6,14},{7,15},{8,0},{9,1},... | collective-permute-start | bytes 1179656 | tf_op jit(solution)/shard_map/ppermute | solution.py:362
  72.9 3.8 %collective-permute-done.20.refs_2_ = bf16[4,128,384]{2,1,0:T(8,128)(2,1)S(1)} collective-permute-done((bf16[4,128,384]{2,1,0:T(8,128)(2,1)S(1)}, bf16[4,128,384]{2,1,0:T(8,128)(2,1)S(1)}, u32[]{:S(2)}, u32[]{:S(2)}) %collective-permute-start.20) | collective-permute-done | bytes 393248 | tf_op jit(solution)/shard_map/ppermute | solution.py:362
  89.6 3.6 %collective-permute-done.23.refs_1_ = bf16[4,128,384]{2,1,0:T(8,128)(2,1)S(1)} collective-permute-done((bf16[4,128,384]{2,1,0:T(8,128)(2,1)S(1)}, bf16[4,128,384]{2,1,0:T(8,128)(2,1)S(1)}, u32[]{:S(2)}, u32[]{:S(2)}) %collective-permute-start.23) | collective-permute-done | bytes 393248 | tf_op jit(solution)/shard_map/ppermute | solution.py:362
  93.2 2.6 %collective-permute-done.24.refs_2_ = bf16[4,128,384]{2,1,0:T(8,128)(2,1)S(1)} collective-permute-done((bf16[4,128,384]{2,1,0:T(8,128)(2,1)S(1)}, bf16[4,128,384]{2,1,0:T(8,128)(2,1)S(1)}, u32[]{:S(2)}, u32[]{:S(2)}) %collective-permute-start.24) | collective-permute-done | bytes 393248 | tf_op jit(solution)/shard_map/ppermute | solution.py:362
  95.8 4.1 %collective-permute-done.25.refs_3_ = bf16[4,128,384]{2,1,0:T(8,128)(2,1)S(1)} collective-permute-done((bf16[4,128,384]{2,1,0:T(8,128)(2,1)S(1)}, bf16[4,128,384]{2,1,0:T(8,128)(2,1)S(1)}, u32[]{:S(2)}, u32[]{:S(2)}) %collective-permute-start.25) | collective-permute-done | bytes 393248 | tf_op jit(solution)/shard_map/ppermute | solution.py:362
  100.0 4.2 %later_in.1.hidden_ref = bf16[12,128,128]{2,1,0:T(8,128)(2,1)S(1)} custom-call(s32[5]{0:T(128)S(1)} %stack.32.place_ref, f32[48,1,128]{2,1,0:T(1,128)S(1)} %get-tuple-element.53.gain_ref, bf16[4,128,384]{2,1,0:T(8,128)(2,1)S(1)} %get-tuple-element.36.refs_0_, bf16[4,128,384]{2,1,0:T(8,128)(2,1)S(1)} %collective-permute-done.23.refs_1_, ...), custom_call_target="tpu_custom_call" | custom-call | flops 2147483648 | bytes 12582912 | tf_op jit(solution)/shard_map/later_in/pallas_call | solution.py:301
  104.2 3.9 %project_out.3 = (bf16[4,128,384]{2,1,0:T(8,128)(2,1)S(1)}, bf16[4,128,384]{2,1,0:T(8,128)(2,1)S(1)}, bf16[4,128,384]{2,1,0:T(8,128)(2,1)S(1)}, bf16[4,128,384]{2,1,0:T(8,128)(2,1)S(1)}) custom-call(s32[5]{0:T(128)S(1)} %stack.32.place_ref, bf16[12,128,128]{2,1,0:T(8,128)(2,1)S(1)} %later_in.1.hidden_ref, ...), custom_call_target="tpu_custom_call" | custom-call | flops 2147483648 | bytes 8388608 | tf_op jit(solution)/shard_map/project_out/pallas_call | solution.py:318
  111.4 4.5 %collective-permute-done.33.refs_1_ = bf16[4,128,384]{2,1,0:T(8,128)(2,1)S(1)} collective-permute-done((bf16[4,128,384]{2,1,0:T(8,128)(2,1)S(1)}, bf16[4,128,384]{2,1,0:T(8,128)(2,1)S(1)}, u32[]{:S(2)}, u32[]{:S(2)}) %collective-permute-start.33) | collective-permute-done | bytes 393248 | tf_op jit(solution)/shard_map/ppermute | solution.py:362
  117.6 4.8 %collective-permute-done.35.refs_3_ = bf16[4,128,384]{2,1,0:T(8,128)(2,1)S(1)} collective-permute-done((bf16[4,128,384]{2,1,0:T(8,128)(2,1)S(1)}, bf16[4,128,384]{2,1,0:T(8,128)(2,1)S(1)}, u32[]{:S(2)}, u32[]{:S(2)}) %collective-permute-start.35) | collective-permute-done | bytes 393248 | tf_op jit(solution)/shard_map/ppermute | solution.py:362
  122.6 3.8 %collective-permute-start.38 = (bf16[128,384]{1,0:T(8,128)(2,1)S(1)}, bf16[128,384]{1,0:T(8,128)(2,1)S(1)}, u32[]{:S(2)}, u32[]{:S(2)}) collective-permute-start(bf16[128,384]{1,0:T(8,128)(2,1)S(1)} %get-tuple-element.48), channel_id=1, source_target_pairs={{0,12},{1,13},{2,14},{3,15},{4,0},{5,1},{6,2},{7,3},{8,4},{9,5},{1... | collective-permute-start | bytes 294920 | tf_op jit(solution)/shard_map/ppermute | solution.py:362
  127.4 2.3 %collective-permute-done.38 = bf16[128,384]{1,0:T(8,128)(2,1)S(1)} collective-permute-done((bf16[128,384]{1,0:T(8,128)(2,1)S(1)}, bf16[128,384]{1,0:T(8,128)(2,1)S(1)}, u32[]{:S(2)}, u32[]{:S(2)}) %collective-permute-start.38) | collective-permute-done | bytes 98336 | tf_op jit(solution)/shard_map/ppermute | solution.py:362
  129.7 3.0 %collective-permute-done.37 = bf16[128,384]{1,0:T(8,128)(2,1)S(1)} collective-permute-done((bf16[128,384]{1,0:T(8,128)(2,1)S(1)}, bf16[128,384]{1,0:T(8,128)(2,1)S(1)}, u32[]{:S(2)}, u32[]{:S(2)}) %collective-permute-start.37) | collective-permute-done | bytes 98336 | tf_op jit(solution)/shard_map/ppermute | solution.py:362
  (78 shorter events, 44.0 us)
Async XLA Ops:
  4.7 10.3 %collective-permute-start.2 = (bf16[1040,128]{1,0:T(8,128)(2,1)S(1)}, bf16[1040,128]{1,0:T(8,128)(2,1)S(1)}, u32[]{:S(2)}, u32[]{:S(2)}) collective-permute-start(bf16[1040,128]{1,0:T(8,128)(2,1)S(1)} %broadcast_select_fusion.3.refs_0_), channel_id=1, source_target_pairs={{0,16},{16,32},{32,48},{48,64},{64,80},{80,96},{96,112},{112,0},{1... | collective-permute-start | bytes 798728 | tf_op jit(solution)/shard_map/ppermute | solution.py:358
  6.7 11.1 %collective-permute-start.10 = (bf16[1040,128]{1,0:T(8,128)(2,1)S(1)}, bf16[1040,128]{1,0:T(8,128)(2,1)S(1)}, u32[]{:S(2)}, u32[]{:S(2)}) collective-permute-start(bf16[1040,128]{1,0:T(8,128)(2,1)S(1)} %broadcast_select_fusion.2.refs_0_), channel_id=1, source_target_pairs={{0,16},{16,32},{32,48},{48,64},{64,80},{80,96},{96,112},{112,0},{1... | collective-permute-start | bytes 798728 | tf_op jit(solution)/shard_map/ppermute | solution.py:358
  15.0 15.5 %collective-permute-start.6 = (bf16[1040,128]{1,0:T(8,128)(2,1)S(1)}, bf16[1040,128]{1,0:T(8,128)(2,1)S(1)}, u32[]{:S(2)}, u32[]{:S(2)}) collective-permute-start(bf16[1040,128]{1,0:T(8,128)(2,1)S(1)} %collective-permute-done.2.refs_1_), channel_id=1, source_target_pairs={{0,128},{16,144},{32,160},{48,176},{64,192},{80,208},{96,224},{112... | collective-permute-start | bytes 798728 | tf_op jit(solution)/shard_map/ppermute | solution.py:358
  22.9 20.3 %collective-permute-start.26 = (bf16[2080,128]{1,0:T(8,128)(2,1)S(1)}, bf16[2080,128]{1,0:T(8,128)(2,1)S(1)}, u32[]{:S(2)}, u32[]{:S(2)}) collective-permute-start(bf16[2080,128]{1,0:T(8,128)(2,1)S(1)} %pad_maximum_fusion.refs_4_.refs_0_), channel_id=1, source_target_pairs={{0,16},{16,32},{32,48},{48,64},{64,80},{80,96},{96,112},{112,0},{1... | collective-permute-start | bytes 1597448 | tf_op jit(solution)/shard_map/ppermute | solution.py:358
  25.5 13.5 %collective-permute-start.12 = (bf16[1040,128]{1,0:T(8,128)(2,1)S(1)}, bf16[1040,128]{1,0:T(8,128)(2,1)S(1)}, u32[]{:S(2)}, u32[]{:S(2)}) collective-permute-start(bf16[1040,128]{1,0:T(8,128)(2,1)S(1)} %collective-permute-done.11.refs_2_), channel_id=1, source_target_pairs={{0,16},{16,32},{32,48},{48,64},{64,80},{80,96},{96,112},{112,0},{1... | collective-permute-start | bytes 798728 | tf_op jit(solution)/shard_map/ppermute | solution.py:358
  30.4 11.4 %collective-permute-start.5 = (bf16[1040,128]{1,0:T(8,128)(2,1)S(1)}, bf16[1040,128]{1,0:T(8,128)(2,1)S(1)}, u32[]{:S(2)}, u32[]{:S(2)}) collective-permute-start(bf16[1040,128]{1,0:T(8,128)(2,1)S(1)} %collective-permute-done.4.refs_3_), channel_id=1, source_target_pairs={{0,16},{16,32},{32,48},{48,64},{64,80},{80,96},{96,112},{112,0},{1... | collective-permute-start | bytes 798728 | tf_op jit(solution)/shard_map/ppermute | solution.py:358
  30.6 11.3 %collective-permute-start.8 = (bf16[1040,128]{1,0:T(8,128)(2,1)S(1)}, bf16[1040,128]{1,0:T(8,128)(2,1)S(1)}, u32[]{:S(2)}, u32[]{:S(2)}) collective-permute-start(bf16[1040,128]{1,0:T(8,128)(2,1)S(1)} %collective-permute-done.4.refs_3_), channel_id=1, source_target_pairs={{0,128},{16,144},{32,160},{48,176},{64,192},{80,208},{96,224},{112... | collective-permute-start | bytes 798728 | tf_op jit(solution)/shard_map/ppermute | solution.py:358
  30.6 15.9 %collective-permute-start.14 = (bf16[1040,128]{1,0:T(8,128)(2,1)S(1)}, bf16[1040,128]{1,0:T(8,128)(2,1)S(1)}, u32[]{:S(2)}, u32[]{:S(2)}) collective-permute-start(bf16[1040,128]{1,0:T(8,128)(2,1)S(1)} %collective-permute-done.10.refs_1_), channel_id=1, source_target_pairs={{0,128},{16,144},{32,160},{48,176},{64,192},{80,208},{96,224},{112... | collective-permute-start | bytes 798728 | tf_op jit(solution)/shard_map/ppermute | solution.py:358
  43.2 26.7 %collective-permute-start.27 = (bf16[2080,128]{1,0:T(8,128)(2,1)S(1)}, bf16[2080,128]{1,0:T(8,128)(2,1)S(1)}, u32[]{:S(2)}, u32[]{:S(2)}) collective-permute-start(bf16[2080,128]{1,0:T(8,128)(2,1)S(1)} %collective-permute-done.26.refs_5_.refs_1_), channel_id=1, source_target_pairs={{0,16},{16,32},{32,48},{48,64},{64,80},{80,96},{96,112},{112,0},{1... | collective-permute-start | bytes 1597448 | tf_op jit(solution)/shard_map/ppermute | solution.py:358
  54.3 9.4 %collective-permute-start.18 = (bf16[4,128,384]{2,1,0:T(8,128)(2,1)S(1)}, bf16[4,128,384]{2,1,0:T(8,128)(2,1)S(1)}, u32[]{:S(2)}, u32[]{:S(2)}) collective-permute-start(bf16[4,128,384]{2,1,0:T(8,128)(2,1)S(1)} %get-tuple-element.33), channel_id=1, source_target_pairs={{0,2},{1,3},{2,0},{3,1},{4,6},{5,7},{6,4},{7,5},{8,10},{9,11},{10,... | collective-permute-start | bytes 1179656 | tf_op jit(solution)/shard_map/ppermute | solution.py:362
  55.4 12.0 %collective-permute-start.19 = (bf16[4,128,384]{2,1,0:T(8,128)(2,1)S(1)}, bf16[4,128,384]{2,1,0:T(8,128)(2,1)S(1)}, u32[]{:S(2)}, u32[]{:S(2)}) collective-permute-start(bf16[4,128,384]{2,1,0:T(8,128)(2,1)S(1)} %get-tuple-element.34), channel_id=1, source_target_pairs={{0,3},{1,0},{2,1},{3,2},{4,7},{5,4},{6,5},{7,6},{8,11},{9,8},{10,9... | collective-permute-start | bytes 1179656 | tf_op jit(solution)/shard_map/ppermute | solution.py:362
  67.7 9.1 %collective-permute-start.20 = (bf16[4,128,384]{2,1,0:T(8,128)(2,1)S(1)}, bf16[4,128,384]{2,1,0:T(8,128)(2,1)S(1)}, u32[]{:S(2)}, u32[]{:S(2)}) collective-permute-start(bf16[4,128,384]{2,1,0:T(8,128)(2,1)S(1)} %shard_map.82.refs_1_), channel_id=1, source_target_pairs={{0,4},{1,5},{2,6},{3,7},{4,8},{5,9},{6,10},{7,11},{8,12},{9,13},{1... | collective-permute-start | bytes 1179656 | tf_op jit(solution)/shard_map/ppermute | solution.py:362
  69.9 10.5 %collective-permute-start.28 = (bf16[2080,128]{1,0:T(8,128)(2,1)S(1)}, bf16[2080,128]{1,0:T(8,128)(2,1)S(1)}, u32[]{:S(2)}, u32[]{:S(2)}) collective-permute-start(bf16[2080,128]{1,0:T(8,128)(2,1)S(1)} %collective-permute-done.27.refs_6_.refs_2_), channel_id=1, source_target_pairs={{0,16},{16,32},{32,48},{48,64},{64,80},{80,96},{96,112},{112,0},{1... | collective-permute-start | bytes 1597448 | tf_op jit(solution)/shard_map/ppermute | solution.py:358
  69.9 16.6 %collective-permute-start.30 = (bf16[2080,128]{1,0:T(8,128)(2,1)S(1)}, bf16[2080,128]{1,0:T(8,128)(2,1)S(1)}, u32[]{:S(2)}, u32[]{:S(2)}) collective-permute-start(bf16[2080,128]{1,0:T(8,128)(2,1)S(1)} %collective-permute-done.26.refs_5_.refs_1_), channel_id=1, source_target_pairs={{0,128},{16,144},{32,160},{48,176},{64,192},{80,208},{96,224},{112... | collective-permute-start | bytes 1597448 | tf_op jit(solution)/shard_map/ppermute | solution.py:358
  69.9 18.1 %collective-permute-start.31 = (bf16[2080,128]{1,0:T(8,128)(2,1)S(1)}, bf16[2080,128]{1,0:T(8,128)(2,1)S(1)}, u32[]{:S(2)}, u32[]{:S(2)}) collective-permute-start(bf16[2080,128]{1,0:T(8,128)(2,1)S(1)} %collective-permute-done.27.refs_6_.refs_2_), channel_id=1, source_target_pairs={{0,128},{16,144},{32,160},{48,176},{64,192},{80,208},{96,224},{112... | collective-permute-start | bytes 1597448 | tf_op jit(solution)/shard_map/ppermute | solution.py:358
  70.4 12.0 %collective-permute-start.21 = (bf16[4,128,384]{2,1,0:T(8,128)(2,1)S(1)}, bf16[4,128,384]{2,1,0:T(8,128)(2,1)S(1)}, u32[]{:S(2)}, u32[]{:S(2)}) collective-permute-start(bf16[4,128,384]{2,1,0:T(8,128)(2,1)S(1)} %shard_map.82.refs_1_), channel_id=1, source_target_pairs={{0,8},{1,9},{2,10},{3,11},{4,12},{5,13},{6,14},{7,15},{8,0},{9,1},... | collective-permute-start | bytes 1179656 | tf_op jit(solution)/shard_map/ppermute | solution.py:362
  80.4 19.6 %collective-permute-start.29 = (bf16[2080,128]{1,0:T(8,128)(2,1)S(1)}, bf16[2080,128]{1,0:T(8,128)(2,1)S(1)}, u32[]{:S(2)}, u32[]{:S(2)}) collective-permute-start(bf16[2080,128]{1,0:T(8,128)(2,1)S(1)} %collective-permute-done.28.refs_7_.refs_3_), channel_id=1, source_target_pairs={{0,16},{16,32},{32,48},{48,64},{64,80},{80,96},{96,112},{112,0},{1... | collective-permute-start | bytes 1597448 | tf_op jit(solution)/shard_map/ppermute | solution.py:358
  82.4 17.6 %collective-permute-start.32 = (bf16[2080,128]{1,0:T(8,128)(2,1)S(1)}, bf16[2080,128]{1,0:T(8,128)(2,1)S(1)}, u32[]{:S(2)}, u32[]{:S(2)}) collective-permute-start(bf16[2080,128]{1,0:T(8,128)(2,1)S(1)} %collective-permute-done.28.refs_7_.refs_3_), channel_id=1, source_target_pairs={{0,128},{16,144},{32,160},{48,176},{64,192},{80,208},{96,224},{112... | collective-permute-start | bytes 1597448 | tf_op jit(solution)/shard_map/ppermute | solution.py:358
  85.4 7.9 %collective-permute-start.23 = (bf16[4,128,384]{2,1,0:T(8,128)(2,1)S(1)}, bf16[4,128,384]{2,1,0:T(8,128)(2,1)S(1)}, u32[]{:S(2)}, u32[]{:S(2)}) collective-permute-start(bf16[4,128,384]{2,1,0:T(8,128)(2,1)S(1)} %get-tuple-element.36.refs_0_), channel_id=1, source_target_pairs={{0,1},{1,2},{2,3},{3,0},{4,5},{5,6},{6,7},{7,4},{8,9},{9,10},{10,1... | collective-permute-start | bytes 1179656 | tf_op jit(solution)/shard_map/ppermute | solution.py:362
  86.5 9.4 %collective-permute-start.24 = (bf16[4,128,384]{2,1,0:T(8,128)(2,1)S(1)}, bf16[4,128,384]{2,1,0:T(8,128)(2,1)S(1)}, u32[]{:S(2)}, u32[]{:S(2)}) collective-permute-start(bf16[4,128,384]{2,1,0:T(8,128)(2,1)S(1)} %get-tuple-element.36.refs_0_), channel_id=1, source_target_pairs={{0,2},{1,3},{2,0},{3,1},{4,6},{5,7},{6,4},{7,5},{8,10},{9,11},{10,... | collective-permute-start | bytes 1179656 | tf_op jit(solution)/shard_map/ppermute | solution.py:362
  88.0 11.9 %collective-permute-start.25 = (bf16[4,128,384]{2,1,0:T(8,128)(2,1)S(1)}, bf16[4,128,384]{2,1,0:T(8,128)(2,1)S(1)}, u32[]{:S(2)}, u32[]{:S(2)}) collective-permute-start(bf16[4,128,384]{2,1,0:T(8,128)(2,1)S(1)} %get-tuple-element.36.refs_0_), channel_id=1, source_target_pairs={{0,3},{1,0},{2,1},{3,2},{4,7},{5,4},{6,5},{7,6},{8,11},{9,8},{10,9... | collective-permute-start | bytes 1179656 | tf_op jit(solution)/shard_map/ppermute | solution.py:362
  108.1 7.9 %collective-permute-start.33 = (bf16[4,128,384]{2,1,0:T(8,128)(2,1)S(1)}, bf16[4,128,384]{2,1,0:T(8,128)(2,1)S(1)}, u32[]{:S(2)}, u32[]{:S(2)}) collective-permute-start(bf16[4,128,384]{2,1,0:T(8,128)(2,1)S(1)} %get-tuple-element.42), channel_id=1, source_target_pairs={{0,1},{1,2},{2,3},{3,0},{4,5},{5,6},{6,7},{7,4},{8,9},{9,10},{10,1... | collective-permute-start | bytes 1179656 | tf_op jit(solution)/shard_map/ppermute | solution.py:362
  108.2 9.5 %collective-permute-start.34 = (bf16[4,128,384]{2,1,0:T(8,128)(2,1)S(1)}, bf16[4,128,384]{2,1,0:T(8,128)(2,1)S(1)}, u32[]{:S(2)}, u32[]{:S(2)}) collective-permute-start(bf16[4,128,384]{2,1,0:T(8,128)(2,1)S(1)} %get-tuple-element.43), channel_id=1, source_target_pairs={{0,2},{1,3},{2,0},{3,1},{4,6},{5,7},{6,4},{7,5},{8,10},{9,11},{10,... | collective-permute-start | bytes 1179656 | tf_op jit(solution)/shard_map/ppermute | solution.py:362
  109.8 12.6 %collective-permute-start.35 = (bf16[4,128,384]{2,1,0:T(8,128)(2,1)S(1)}, bf16[4,128,384]{2,1,0:T(8,128)(2,1)S(1)}, u32[]{:S(2)}, u32[]{:S(2)}) collective-permute-start(bf16[4,128,384]{2,1,0:T(8,128)(2,1)S(1)} %get-tuple-element.44), channel_id=1, source_target_pairs={{0,3},{1,0},{2,1},{3,2},{4,7},{5,4},{6,5},{7,6},{8,11},{9,8},{10,9... | collective-permute-start | bytes 1179656 | tf_op jit(solution)/shard_map/ppermute | solution.py:362
  (18 other events, 147.1 us)

commit v5 on v4

--- a/solution.py
+++ b/solution.py
@@ -1,5 +1,3 @@
-import functools
-
 import jax
 import jax.numpy as jnp
 from jax import lax
@@ -15,6 +13,8 @@
 TAIL = 16
 SPAN = 1024 + TAIL
 GRID_ROWS = 8
+EARLY = (0, 1, 2, 3, 5, 6)
+LATE = (4, 7)
 SIDE = 4
 DBL = 6
 FBL = 12
@@ -89,13 +89,13 @@
         )
     for copy in copies:
         copy.start()
-    return copies[:GRID_ROWS], copies[GRID_ROWS:]
+    return copies[: len(cells)], copies[len(cells) :]
 
 
 def read_table(copies, tails, table):
     for copy in copies:
         copy.wait()
-    for i in range(GRID_ROWS):
+    for i in range(len(copies)):
         rows = tails[i * TAIL : (i + 1) * TAIL, :].astype(F32).astype(jnp.int32)
         table[i : i + 1, :] = rows[0:1, :]
 
@@ -103,7 +103,7 @@
 def list_blocks(table, small, dummy, blocks):
     pltpu.sync_copy(table, small)
     used = 0
-    for i in range(GRID_ROWS):
+    for i in range(table.shape[0]):
         for n in range(SLOTS):
             blocks[0, used + n] = i * SLOTS + n
             blocks[1, used + n] = small[i, n]
@@ -154,9 +154,9 @@
         own_ref[e] = x_ref[0, :, pl.ds(start, WIDTH)]
 
 
-def first_in_kernel(normed_ref, *refs):
-    cells = refs[:GRID_ROWS]
-    hidden_ref, total, weights, tails, table, small, blocks, sems = refs[GRID_ROWS:]
+def early_in_kernel(normed_ref, *refs):
+    cells = refs[: len(EARLY)]
+    total, weights, tails, table, small, blocks, sems = refs[len(EARLY) :]
     tail_copies, copies = fetch(cells, 0, weights, tails, sems)
     read_table(tail_copies, tails, table)
     total[...] = jnp.zeros_like(total)
@@ -164,15 +164,68 @@
     for copy in copies:
         copy.wait()
     block_sum(normed_ref, weights, blocks, used, total)
+
+
+def late_in_kernel(normed_ref, early_ref, *refs):
+    cells = refs[: len(LATE)]
+    hidden_ref, total, weights, tails, table, small, blocks, sems = refs[len(LATE) :]
+    tail_copies, copies = fetch(cells, 0, weights, tails, sems)
+    read_table(tail_copies, tails, table)
+    total[...] = early_ref[...]
+    used = list_blocks(table, small, FBL, blocks)
+    for copy in copies:
+        copy.wait()
+    block_sum(normed_ref, weights, blocks, used, total)
     gelu_into(total, hidden_ref)
 
 
-def later_in_kernel(place_ref, gain_ref, *refs):
+def send_out(place_ref, total, sends, relative):
+    for d in range(SIDE):
+        for e in range(SIDE):
+            second = digit(place_ref[3] + e) if relative else e
+            chunk = chunk_of(place_ref, digit(place_ref[2] + d), second)
+            for q in range(CHUNK):
+                sends[d][e, :, q * BLK : (q + 1) * BLK] = total[chunk * CHUNK + q].astype(BF16)
+
+
+def early_out_kernel(hidden_ref, *refs):
+    cells = refs[: len(EARLY)]
+    total, weights, tails, table, small, blocks, sems = refs[len(EARLY) :]
+    tail_copies, copies = fetch(cells, 0, weights, tails, sems)
+    read_table(tail_copies, tails, table)
+    total[...] = jnp.zeros_like(total)
+    used = list_blocks(table, small, BLOCKS, blocks)
+    for copy in copies:
+        copy.wait()
+    block_sum(hidden_ref, weights, blocks, used, total)
+
+
+def late_out_kernel(place_ref, hidden_ref, early_ref, *refs):
+    cells = refs[: len(LATE)]
+    sends = refs[len(LATE) : len(LATE) + SIDE]
+    total, weights, tails, table, small, blocks, sems = refs[len(LATE) + SIDE :]
+    tail_copies, copies = fetch(cells, 0, weights, tails, sems)
+    read_table(tail_copies, tails, table)
+    total[...] = early_ref[...]
+    used = list_blocks(table, small, BLOCKS, blocks)
+    for copy in copies:
+        copy.wait()
+    block_sum(hidden_ref, weights, blocks, used, total)
+    send_out(place_ref, total, sends, False)
+
+
+def later_kernel(place_ref, gain_ref, *refs):
     bundles = refs[:SIDE]
     cells = refs[SIDE : SIDE + GRID_ROWS]
-    hidden_ref, normed, total, weights, tails, table, small, blocks, sems = refs[SIDE + GRID_ROWS :]
-    tail_copies, copies = fetch(cells, 0, weights, tails, sems)
-    read_table(tail_copies, tails, table)
+    sends = refs[SIDE + GRID_ROWS : 2 * SIDE + GRID_ROWS]
+    normed, hidden, total_in, total_out = refs[2 * SIDE + GRID_ROWS : 2 * SIDE + GRID_ROWS + 4]
+    work = refs[2 * SIDE + GRID_ROWS + 4 :]
+    works = (work[: len(work) // 2], work[len(work) // 2 :])
+    flights = []
+    for k, (weights, tails, table, small, blocks, sems) in enumerate(works):
+        flights.append(fetch(cells, k * SPAN, weights, tails, sems))
+    for (tail_copies, _), (_, tails, table, _, _, _) in zip(flights, works):
+        read_table(tail_copies, tails, table)
     squares = jnp.zeros((TOK, BLK), F32)
     for d in range(SIDE):
         for e in range(SIDE):
@@ -188,31 +241,19 @@
                 k = chunk * CHUNK + q
                 part = bundles[d][e, :, q * BLK : (q + 1) * BLK].astype(F32)
                 normed[k] = (part * scale * gain_ref[k]).astype(BF16)
-    total[...] = jnp.zeros_like(total)
-    used = list_blocks(table, small, FBL, blocks)
-    for copy in copies:
-        copy.wait()
-    block_sum(normed, weights, blocks, used, total)
-    gelu_into(total, hidden_ref)
-
-
-def out_kernel(phase, place_ref, hidden_ref, *refs):
-    cells = refs[:GRID_ROWS]
-    sends = refs[GRID_ROWS : GRID_ROWS + SIDE]
-    total, weights, tails, table, small, blocks, sems = refs[GRID_ROWS + SIDE :]
-    tail_copies, copies = fetch(cells, phase * SPAN, weights, tails, sems)
-    read_table(tail_copies, tails, table)
-    total[...] = jnp.zeros_like(total)
-    used = list_blocks(table, small, BLOCKS, blocks)
-    for copy in copies:
-        copy.wait()
-    block_sum(hidden_ref, weights, blocks, used, total)
-    for d in range(SIDE):
-        for e in range(SIDE):
-            second = digit(place_ref[3] + e) if phase else e
-            chunk = chunk_of(place_ref, digit(place_ref[2] + d), second)
-            for q in range(CHUNK):
-                sends[d][e, :, q * BLK : (q + 1) * BLK] = total[chunk * CHUNK + q].astype(BF16)
+    totals = (total_in, total_out)
+    used = []
+    for total, dummy, (_, _, table, small, blocks, _) in zip(totals, (FBL, BLOCKS), works):
+        total[...] = jnp.zeros_like(total)
+        used.append(list_blocks(table, small, dummy, blocks))
+    for k, dense in enumerate((normed, hidden)):
+        weights, _, _, _, blocks, _ = works[k]
+        for copy in flights[k][1]:
+            copy.wait()
+        block_sum(dense, weights, blocks, used[k], totals[k])
+        if k == 0:
+            gelu_into(total_in, hidden)
+    send_out(place_ref, total_out, sends, True)
 
 
 def sum_of(refs, index):
@@ -224,7 +265,7 @@
 
 def whole_sum_kernel(*refs):
     for e in range(SIDE):
-        refs[-1][e] = sum_of(refs[:-1], e).astype(BF16)
+        refs[-1][e] = sum_of(refs[:-1], e).astype(refs[-1].dtype)
 
 
 def merge_kernel(place_ref, *refs):
@@ -243,14 +284,17 @@
     return pl.CostEstimate(flops=blocks * 2 * BLK**3, bytes_accessed=moved, transcendentals=0)
 
 
-WORK = [
-    pltpu.VMEM((GRID_ROWS * SLOTS * BLK, BLK), BF16),
-    pltpu.VMEM((GRID_ROWS * TAIL, BLK), BF16),
-    pltpu.VMEM((GRID_ROWS, BLK), jnp.int32),
-    pltpu.SMEM((GRID_ROWS, BLK), jnp.int32),
-    pltpu.SMEM((3, GRID_ROWS * SLOTS + 2 * SLOTS), jnp.int32),
-    pltpu.SemaphoreType.DMA((2, GRID_ROWS)),
-]
+def work(cells):
+    return [
+        pltpu.VMEM((cells * SLOTS * BLK, BLK), BF16),
+        pltpu.VMEM((cells * TAIL, BLK), BF16),
+        pltpu.VMEM((cells, BLK), jnp.int32),
+        pltpu.SMEM((cells, BLK), jnp.int32),
+        pltpu.SMEM((3, cells * SLOTS + 2 * SLOTS), jnp.int32),
+        pltpu.SemaphoreType.DMA((2, cells)),
+    ]
+
+
 PARAMS = pltpu.CompilerParams(vmem_limit_bytes=16 << 20)
 NORMED = jax.ShapeDtypeStruct((BLOCKS, TOK, BLK), BF16)
 HIDDEN = jax.ShapeDtypeStruct((FBL, TOK, BLK), BF16)
@@ -284,47 +328,76 @@
     return pl.BlockSpec(memory_space=pl.ANY)
 
 
-def first_in(normed, cells):
-    return pl.pallas_call(
-        first_in_kernel,
-        in_specs=[vmem()] + [anywhere()] * GRID_ROWS,
+def early_in(normed, cells):
+    return pl.pallas_call(
+        early_in_kernel,
+        in_specs=[vmem()] + [anywhere()] * len(EARLY),
+        out_specs=vmem(),
+        out_shape=jax.ShapeDtypeStruct((FBL + 1, TOK, BLK), F32),
+        scratch_shapes=work(len(EARLY)),
+        cost_estimate=cost(384, 6 << 20),
+        compiler_params=PARAMS,
+        name="early_in",
+    )(normed, *[cells[i] for i in EARLY])
+
+
+def late_in(normed, early, cells):
+    return pl.pallas_call(
+        late_in_kernel,
+        in_specs=[vmem()] * 2 + [anywhere()] * len(LATE),
         out_specs=vmem(),
         out_shape=HIDDEN,
-        scratch_shapes=[pltpu.VMEM((FBL + 1, TOK, BLK), F32)] + WORK,
-        cost_estimate=cost(512, 8 << 20),
-        compiler_params=PARAMS,
-        name="first_in",
-    )(normed, *cells)
-
-
-def later_in(place, gain, bundles, cells):
-    return pl.pallas_call(
-        later_in_kernel,
+        scratch_shapes=[pltpu.VMEM((FBL + 1, TOK, BLK), F32)] + work(len(LATE)),
+        cost_estimate=cost(128, 3 << 20),
+        compiler_params=PARAMS,
+        name="late_in",
+    )(normed, early, *[cells[i] for i in LATE])
+
+
+def later_both(place, gain, bundles, cells):
+    return pl.pallas_call(
+        later_kernel,
         in_specs=[smem()] + [vmem()] * (1 + SIDE) + [anywhere()] * GRID_ROWS,
-        out_specs=vmem(),
-        out_shape=HIDDEN,
+        out_specs=[vmem()] * SIDE,
+        out_shape=[BUNDLE] * SIDE,
         scratch_shapes=[
             pltpu.VMEM((BLOCKS, TOK, BLK), BF16),
+            pltpu.VMEM((FBL, TOK, BLK), BF16),
             pltpu.VMEM((FBL + 1, TOK, BLK), F32),
+            pltpu.VMEM((BLOCKS + 1, TOK, BLK), F32),
         ]
-        + WORK,
-        cost_estimate=cost(512, 12 << 20),
-        compiler_params=PARAMS,
-        name="later_in",
+        + work(GRID_ROWS)
+        + work(GRID_ROWS),
+        cost_estimate=cost(1024, 16 << 20),
+        compiler_params=pltpu.CompilerParams(vmem_limit_bytes=24 << 20),
+        name="later_both",
     )(place, gain, *bundles, *cells)
 
 
-def project_out(phase, place, hidden, cells):
-    return pl.pallas_call(
-        functools.partial(out_kernel, phase),
-        in_specs=[smem(), vmem()] + [anywhere()] * GRID_ROWS,
+def early_out(hidden, cells):
+    return pl.pallas_call(
+        early_out_kernel,
+        in_specs=[vmem()] + [anywhere()] * len(EARLY),
+        out_specs=vmem(),
+        out_shape=jax.ShapeDtypeStruct((BLOCKS + 1, TOK, BLK), F32),
+        scratch_shapes=work(len(EARLY)),
+        cost_estimate=cost(384, 6 << 20),
+        compiler_params=PARAMS,
+        name="early_out",
+    )(hidden, *[cells[i] for i in EARLY])
+
+
+def late_out(place, hidden, early, cells):
+    return pl.pallas_call(
+        late_out_kernel,
+        in_specs=[smem()] + [vmem()] * 2 + [anywhere()] * len(LATE),
         out_specs=[vmem()] * SIDE,
         out_shape=[BUNDLE] * SIDE,
-        scratch_shapes=[pltpu.VMEM((BLOCKS + 1, TOK, BLK), F32)] + WORK,
-        cost_estimate=cost(512, 8 << 20),
-        compiler_params=PARAMS,
-        name="project_out",
-    )(place, hidden, *cells)
+        scratch_shapes=[pltpu.VMEM((BLOCKS + 1, TOK, BLK), F32)] + work(len(LATE)),
+        cost_estimate=cost(128, 6 << 20),
+        compiler_params=PARAMS,
+        name="late_out",
+    )(place, hidden, early, *[cells[i] for i in LATE])
 
 
 def pack(place, *sources):
@@ -436,16 +509,20 @@
     gains = [jnp.where(mine, own_gain, other_gain), jnp.where(mine, other_gain, own_gain)]
 
     normed, own_x = first_norm(micro, place, inputs, gains[0])
-    hidden = first_in(normed, cells_in)
-    bundles = project_out(0, place, hidden, cells_out)
+    early = early_in(normed, cells_in)
+    hidden = late_in(normed, early, cells_in)
+    early = early_out(hidden, cells_out)
+    bundles = late_out(place, hidden, early, cells_out)
     landed = spread(bundles, True)
     sums = add_up(whole_sum_kernel, None, [bundles[0]] + landed, [BUNDLE])[0]
     landed = spread(sums, False)
-    middle, piece = add_up(merge_kernel, place, [own_x, sums] + landed, [BUNDLE, PIECE])
+    base = add_up(
+        whole_sum_kernel, None, [own_x, sums], [jax.ShapeDtypeStruct(BUNDLE.shape, F32)]
+    )[0]
+    middle, piece = add_up(merge_kernel, place, [base] + landed, [BUNDLE, PIECE])
 
     bundles = [middle] + spread(middle, True)
-    hidden = later_in(place, gains[1], bundles, later_cells)
-    bundles = project_out(1, place, hidden, later_cells)
+    bundles = later_both(place, gains[1], bundles, later_cells)
     landed = spread(bundles, True)
     sums = add_up(
         piece_sum_kernel,

time: 136 us -> 136 us (level)
  waiting for transfers between devices: 79.3 us -> 74.7 us
  starting transfers between devices: 34.8 us -> 38.6 us
    ppermute x15, starting transfers between devices: 24.3 us -> 27.9 us  [on_cols(): return lax.ppermute(value, ('section', 'col'), perm)]
    ppermute x15, waiting for transfers between devices: 44.7 us -> 41.4 us  [on_cols(): return lax.ppermute(value, ('section', 'col'), perm)]
    pallas_call x4 -> x5, Pallas kernels: 14.6 us -> 15.4 us  [the longest x1 7.35 us: later_both(): pl.pallas_call(later_kernel, in_specs=[smem()] + [vmem()] * (1 + SIDE) +...]
  transfers between devices with their start and end apart: 40 -> 40, of which waited for: 27 -> 25; matrix products, arithmetic and copies ran while one was open for 0% -> 0% of each run, Pallas kernels for 6% -> 8%
where the time goes in v5:
time: 136 us; the launch traced here: 135 us
  waiting for transfers between devices  74.7 us (55%)
  starting transfers between devices  38.6 us (28%)
  Pallas kernels  19.5 us (14%)
  between operations  1.52 us (1%)
    ppermute x15, waiting for transfers between devices, on_cols(): return lax.ppermute(value, ('section', 'col'), perm)  41.4 us
    ppermute x25, waiting for transfers between devices, on_rows(): return lax.ppermute(value, ('section', 'row'), perm)  33.3 us
    ppermute x15, starting transfers between devices, on_cols(): return lax.ppermute(value, ('section', 'col'), perm)  27.9 us
    ppermute x25, starting transfers between devices, on_rows(): return lax.ppermute(value, ('section', 'row'), perm)  10.7 us
    pallas_call x1, Pallas kernels, later_both(): pl.pallas_call(later_kernel, in_specs=[smem()] + [vmem()] * (1 + SIDE) +...  7.35 us
  transfers between devices with their start and end apart: 40, of which 25 were waited for; matrix products, arithmetic and copies ran while one was open for 0% of the time, Pallas kernels for 8%

profile of v5, /device:TPU:2, one launch (start us, length us, event | category | flops | bytes accessed | tf_op | source)
XLA Modules:
  0.0 135.4 jit_solution(5934749539032804782)
XLA Ops:
  8.7 6.3 %collective-permute-done.2.refs_1_ = bf16[1040,128]{1,0:T(8,128)(2,1)S(1)} collective-permute-done((bf16[1040,128]{1,0:T(8,128)(2,1)S(1)}, bf16[1040,128]{1,0:T(8,128)(2,1)S(1)}, u32[]{:S(2)}, u32[]{:S(2)}) %collective-permute-start.2) | collective-permute-done | bytes 266272 | tf_op jit(solution)/shard_map/ppermute | solution.py:431
  17.9 4.8 %collective-permute-done.3.refs_2_ = bf16[1040,128]{1,0:T(8,128)(2,1)S(1)} collective-permute-done((bf16[1040,128]{1,0:T(8,128)(2,1)S(1)}, bf16[1040,128]{1,0:T(8,128)(2,1)S(1)}, u32[]{:S(2)}, u32[]{:S(2)}) %collective-permute-start.3) | collective-permute-done | bytes 266272 | tf_op jit(solution)/shard_map/ppermute | solution.py:431
  25.9 4.4 %collective-permute-done.4.refs_3_ = bf16[1040,128]{1,0:T(8,128)(2,1)S(1)} collective-permute-done((bf16[1040,128]{1,0:T(8,128)(2,1)S(1)}, bf16[1040,128]{1,0:T(8,128)(2,1)S(1)}, u32[]{:S(2)}, u32[]{:S(2)}) %collective-permute-start.4) | collective-permute-done | bytes 266272 | tf_op jit(solution)/shard_map/ppermute | solution.py:431
  30.8 2.3 %collective-permute-done.12.refs_3_ = bf16[1040,128]{1,0:T(8,128)(2,1)S(1)} collective-permute-done((bf16[1040,128]{1,0:T(8,128)(2,1)S(1)}, bf16[1040,128]{1,0:T(8,128)(2,1)S(1)}, u32[]{:S(2)}, u32[]{:S(2)}) %collective-permute-start.12) | collective-permute-done | bytes 266272 | tf_op jit(solution)/shard_map/ppermute | solution.py:431
  34.4 7.3 %collective-permute-done.7.refs_0_ = bf16[1040,128]{1,0:T(8,128)(2,1)S(1)} collective-permute-done((bf16[1040,128]{1,0:T(8,128)(2,1)S(1)}, bf16[1040,128]{1,0:T(8,128)(2,1)S(1)}, u32[]{:S(2)}, u32[]{:S(2)}) %collective-permute-start.7) | collective-permute-done | bytes 266272 | tf_op jit(solution)/shard_map/ppermute | solution.py:431
  41.7 2.4 %early_in.1.early_ref = f32[13,128,128]{2,1,0:T(8,128)S(1)} custom-call(bf16[48,128,128]{2,1,0:T(8,128)(2,1)S(1)} %get-tuple-element.28.normed_ref, bf16[1040,128]{1,0:T(8,128)(2,1)S(1)} %broadcast_select_fusion.3.refs_0_, bf16[1040,128]{1,0:T(8,128)(2,1)S(1)} %collective-permute-done.2.refs_1_, bf16[1040,128]{1,0:T(8,128)(2,1)S(1)} %collective-permute-done.3.refs_2_, ...), custom_call_target="tpu_custom_call" | custom-call | flops 1610612736 | bytes 6291456 | tf_op jit(solution)/shard_map/early_in/pallas_call | solution.py:332
  45.6 2.2 %early_out.1.early_ref = f32[49,128,128]{2,1,0:T(8,128)S(1)} custom-call(bf16[12,128,128]{2,1,0:T(8,128)(2,1)S(1)} %late_in.1.hidden_ref, bf16[1040,128]{1,0:T(8,128)(2,1)S(1)} %broadcast_select_fusion.2.refs_0_, bf16[1040,128]{1,0:T(8,128)(2,1)S(1)} %collective-permute-done.10.refs_1_, bf16[1040,128]{1,0:T(8,128)(2,1)S(1)} %collective-permute-done.11.refs_2_, ...), custom_call_target="tpu_custom_call" | custom-call | flops 1610612736 | bytes 6291456 | tf_op jit(solution)/shard_map/early_out/pallas_call | solution.py:378
  49.3 2.0 %late_out.1 = (bf16[4,128,384]{2,1,0:T(8,128)(2,1)S(1)}, bf16[4,128,384]{2,1,0:T(8,128)(2,1)S(1)}, bf16[4,128,384]{2,1,0:T(8,128)(2,1)S(1)}, bf16[4,128,384]{2,1,0:T(8,128)(2,1)S(1)}) custom-call(s32[5]{0:T(128)S(1)} %stack.32.place_ref, bf16[12,128,128]{2,1,0:T(8,128)(2,1)S(1)} %late_in.1.hidden_ref, f32[49,128,128]{2,1,0:T(8,128)S(1)} %early_out.1.early_ref, ...), custom_call_target="tpu_custom_call" | custom-call | flops 536870912 | bytes 6291456 | tf_op jit(solution)/shard_map/late_out/pallas_call | solution.py:391
  54.0 2.2 %collective-permute-start.19 = (bf16[4,128,384]{2,1,0:T(8,128)(2,1)S(1)}, bf16[4,128,384]{2,1,0:T(8,128)(2,1)S(1)}, u32[]{:S(2)}, u32[]{:S(2)}) collective-permute-start(bf16[4,128,384]{2,1,0:T(8,128)(2,1)S(1)} %get-tuple-element.34), channel_id=1, source_target_pairs={{0,3},{1,0},{2,1},{3,2},{4,7},{5,4},{6,5},{7,6},{8,11},{9,8},{10,9... | collective-permute-start | bytes 1179656 | tf_op jit(solution)/shard_map/ppermute | solution.py:435
  56.2 3.0 %collective-permute-done.17.refs_1_ = bf16[4,128,384]{2,1,0:T(8,128)(2,1)S(1)} collective-permute-done((bf16[4,128,384]{2,1,0:T(8,128)(2,1)S(1)}, bf16[4,128,384]{2,1,0:T(8,128)(2,1)S(1)}, u32[]{:S(2)}, u32[]{:S(2)}) %collective-permute-start.17) | collective-permute-done | bytes 393248 | tf_op jit(solution)/shard_map/ppermute | solution.py:435
  59.2 3.1 %collective-permute-done.18.refs_2_ = bf16[4,128,384]{2,1,0:T(8,128)(2,1)S(1)} collective-permute-done((bf16[4,128,384]{2,1,0:T(8,128)(2,1)S(1)}, bf16[4,128,384]{2,1,0:T(8,128)(2,1)S(1)}, u32[]{:S(2)}, u32[]{:S(2)}) %collective-permute-start.18) | collective-permute-done | bytes 393248 | tf_op jit(solution)/shard_map/ppermute | solution.py:435
  62.3 3.7 %collective-permute-done.19.refs_3_ = bf16[4,128,384]{2,1,0:T(8,128)(2,1)S(1)} collective-permute-done((bf16[4,128,384]{2,1,0:T(8,128)(2,1)S(1)}, bf16[4,128,384]{2,1,0:T(8,128)(2,1)S(1)}, u32[]{:S(2)}, u32[]{:S(2)}) %collective-permute-start.19) | collective-permute-done | bytes 393248 | tf_op jit(solution)/shard_map/ppermute | solution.py:435
  69.5 2.5 %collective-permute-start.21 = (bf16[4,128,384]{2,1,0:T(8,128)(2,1)S(1)}, bf16[4,128,384]{2,1,0:T(8,128)(2,1)S(1)}, u32[]{:S(2)}, u32[]{:S(2)}) collective-permute-start(bf16[4,128,384]{2,1,0:T(8,128)(2,1)S(1)} %shard_map.82.refs_1_), channel_id=1, source_target_pairs={{0,8},{1,9},{2,10},{3,11},{4,12},{5,13},{6,14},{7,15},{8,0},{9,1},... | collective-permute-start | bytes 1179656 | tf_op jit(solution)/shard_map/ppermute | solution.py:435
  72.0 3.3 %collective-permute-done.20.refs_1_ = bf16[4,128,384]{2,1,0:T(8,128)(2,1)S(1)} collective-permute-done((bf16[4,128,384]{2,1,0:T(8,128)(2,1)S(1)}, bf16[4,128,384]{2,1,0:T(8,128)(2,1)S(1)}, u32[]{:S(2)}, u32[]{:S(2)}) %collective-permute-start.20) | collective-permute-done | bytes 393248 | tf_op jit(solution)/shard_map/ppermute | solution.py:435
  80.9 2.2 %collective-permute-done.22.refs_3_ = bf16[4,128,384]{2,1,0:T(8,128)(2,1)S(1)} collective-permute-done((bf16[4,128,384]{2,1,0:T(8,128)(2,1)S(1)}, bf16[4,128,384]{2,1,0:T(8,128)(2,1)S(1)}, u32[]{:S(2)}, u32[]{:S(2)}) %collective-permute-start.22) | collective-permute-done | bytes 393248 | tf_op jit(solution)/shard_map/ppermute | solution.py:435
  88.3 3.6 %collective-permute-done.23.refs_1_ = bf16[4,128,384]{2,1,0:T(8,128)(2,1)S(1)} collective-permute-done((bf16[4,128,384]{2,1,0:T(8,128)(2,1)S(1)}, bf16[4,128,384]{2,1,0:T(8,128)(2,1)S(1)}, u32[]{:S(2)}, u32[]{:S(2)}) %collective-permute-start.23) | collective-permute-done | bytes 393248 | tf_op jit(solution)/shard_map/ppermute | solution.py:435
  91.9 2.6 %collective-permute-done.24.refs_2_ = bf16[4,128,384]{2,1,0:T(8,128)(2,1)S(1)} collective-permute-done((bf16[4,128,384]{2,1,0:T(8,128)(2,1)S(1)}, bf16[4,128,384]{2,1,0:T(8,128)(2,1)S(1)}, u32[]{:S(2)}, u32[]{:S(2)}) %collective-permute-start.24) | collective-permute-done | bytes 393248 | tf_op jit(solution)/shard_map/ppermute | solution.py:435
  94.5 3.8 %collective-permute-done.25.refs_3_ = bf16[4,128,384]{2,1,0:T(8,128)(2,1)S(1)} collective-permute-done((bf16[4,128,384]{2,1,0:T(8,128)(2,1)S(1)}, bf16[4,128,384]{2,1,0:T(8,128)(2,1)S(1)}, u32[]{:S(2)}, u32[]{:S(2)}) %collective-permute-start.25) | collective-permute-done | bytes 393248 | tf_op jit(solution)/shard_map/ppermute | solution.py:435
  98.4 7.4 %later_both.1 = (bf16[4,128,384]{2,1,0:T(8,128)(2,1)S(1)}, bf16[4,128,384]{2,1,0:T(8,128)(2,1)S(1)}, bf16[4,128,384]{2,1,0:T(8,128)(2,1)S(1)}, bf16[4,128,384]{2,1,0:T(8,128)(2,1)S(1)}) custom-call(s32[5]{0:T(128)S(1)} %stack.32.place_ref, f32[48,1,128]{2,1,0:T(1,128)S(1)} %get-tuple-element.53.gain_ref, bf16[4,128,384]{2,1,0:T(8,128)(2,1)S(1)} %get-tuple-element.36.refs_0_, ...), custom_call_target="tpu_custom_call" | custom-call | flops 4294967296 | bytes 16777216 | tf_op jit(solution)/shard_map/later_both/pallas_call | solution.py:358
  109.0 4.6 %collective-permute-done.33.refs_1_ = bf16[4,128,384]{2,1,0:T(8,128)(2,1)S(1)} collective-permute-done((bf16[4,128,384]{2,1,0:T(8,128)(2,1)S(1)}, bf16[4,128,384]{2,1,0:T(8,128)(2,1)S(1)}, u32[]{:S(2)}, u32[]{:S(2)}) %collective-permute-start.33) | collective-permute-done | bytes 393248 | tf_op jit(solution)/shard_map/ppermute | solution.py:435
  115.3 4.1 %collective-permute-done.35.refs_3_ = bf16[4,128,384]{2,1,0:T(8,128)(2,1)S(1)} collective-permute-done((bf16[4,128,384]{2,1,0:T(8,128)(2,1)S(1)}, bf16[4,128,384]{2,1,0:T(8,128)(2,1)S(1)}, u32[]{:S(2)}, u32[]{:S(2)}) %collective-permute-start.35) | collective-permute-done | bytes 393248 | tf_op jit(solution)/shard_map/ppermute | solution.py:435
  119.6 4.1 %collective-permute-start.38 = (bf16[128,384]{1,0:T(8,128)(2,1)S(1)}, bf16[128,384]{1,0:T(8,128)(2,1)S(1)}, u32[]{:S(2)}, u32[]{:S(2)}) collective-permute-start(bf16[128,384]{1,0:T(8,128)(2,1)S(1)} %get-tuple-element.48), channel_id=1, source_target_pairs={{0,12},{1,13},{2,14},{3,15},{4,0},{5,1},{6,2},{7,3},{8,4},{9,5},{1... | collective-permute-start | bytes 294920 | tf_op jit(solution)/shard_map/ppermute | solution.py:435
  123.6 3.8 %collective-permute-start.37 = (bf16[128,384]{1,0:T(8,128)(2,1)S(1)}, bf16[128,384]{1,0:T(8,128)(2,1)S(1)}, u32[]{:S(2)}, u32[]{:S(2)}) collective-permute-start(bf16[128,384]{1,0:T(8,128)(2,1)S(1)} %get-tuple-element.47), channel_id=1, source_target_pairs={{0,8},{1,9},{2,10},{3,11},{4,12},{5,13},{6,14},{7,15},{8,0},{9,1},... | collective-permute-start | bytes 294920 | tf_op jit(solution)/shard_map/ppermute | solution.py:435
  130.0 3.2 %collective-permute-done.36 = bf16[128,384]{1,0:T(8,128)(2,1)S(1)} collective-permute-done((bf16[128,384]{1,0:T(8,128)(2,1)S(1)}, bf16[128,384]{1,0:T(8,128)(2,1)S(1)}, u32[]{:S(2)}, u32[]{:S(2)}) %collective-permute-start.36) | collective-permute-done | bytes 98336 | tf_op jit(solution)/shard_map/ppermute | solution.py:435
  (80 shorter events, 45.1 us)
Async XLA Ops:
  4.7 10.3 %collective-permute-start.2 = (bf16[1040,128]{1,0:T(8,128)(2,1)S(1)}, bf16[1040,128]{1,0:T(8,128)(2,1)S(1)}, u32[]{:S(2)}, u32[]{:S(2)}) collective-permute-start(bf16[1040,128]{1,0:T(8,128)(2,1)S(1)} %broadcast_select_fusion.3.refs_0_), channel_id=1, source_target_pairs={{0,16},{16,32},{32,48},{48,64},{64,80},{80,96},{96,112},{112,0},{1... | collective-permute-start | bytes 798728 | tf_op jit(solution)/shard_map/ppermute | solution.py:431
  6.7 11.1 %collective-permute-start.10 = (bf16[1040,128]{1,0:T(8,128)(2,1)S(1)}, bf16[1040,128]{1,0:T(8,128)(2,1)S(1)}, u32[]{:S(2)}, u32[]{:S(2)}) collective-permute-start(bf16[1040,128]{1,0:T(8,128)(2,1)S(1)} %broadcast_select_fusion.2.refs_0_), channel_id=1, source_target_pairs={{0,16},{16,32},{32,48},{48,64},{64,80},{80,96},{96,112},{112,0},{1... | collective-permute-start | bytes 798728 | tf_op jit(solution)/shard_map/ppermute | solution.py:431
  15.0 10.5 %collective-permute-start = (f32[48,1,128]{2,1,0:T(1,128)S(1)}, f32[48,1,128]{2,1,0:T(1,128)S(1)}, u32[]{:S(2)}, u32[]{:S(2)}) collective-permute-start(f32[48,1,128]{2,1,0:T(1,128)S(1)} %bitcast.24), channel_id=1, source_target_pairs={{0,128},{16,144},{32,160},{48,176},{64,192},{80,208},{96,224},{112... | collective-permute-start | bytes 73736 | tf_op jit(solution)/shard_map/ppermute | solution.py:431
  17.0 13.3 %collective-permute-start.5 = (bf16[1040,128]{1,0:T(8,128)(2,1)S(1)}, bf16[1040,128]{1,0:T(8,128)(2,1)S(1)}, u32[]{:S(2)}, u32[]{:S(2)}) collective-permute-start(bf16[1040,128]{1,0:T(8,128)(2,1)S(1)} %collective-permute-done.2.refs_1_), channel_id=1, source_target_pairs={{0,128},{16,144},{32,160},{48,176},{64,192},{80,208},{96,224},{112... | collective-permute-start | bytes 798728 | tf_op jit(solution)/shard_map/ppermute | solution.py:431
  25.6 18.6 %collective-permute-start.26 = (bf16[2080,128]{1,0:T(8,128)(2,1)S(1)}, bf16[2080,128]{1,0:T(8,128)(2,1)S(1)}, u32[]{:S(2)}, u32[]{:S(2)}) collective-permute-start(bf16[2080,128]{1,0:T(8,128)(2,1)S(1)} %pad_maximum_fusion.refs_4_), channel_id=1, source_target_pairs={{0,16},{16,32},{32,48},{48,64},{64,80},{80,96},{96,112},{112,0},{1... | collective-permute-start | bytes 1597448 | tf_op jit(solution)/shard_map/ppermute | solution.py:431
  30.3 11.4 %collective-permute-start.7 = (bf16[1040,128]{1,0:T(8,128)(2,1)S(1)}, bf16[1040,128]{1,0:T(8,128)(2,1)S(1)}, u32[]{:S(2)}, u32[]{:S(2)}) collective-permute-start(bf16[1040,128]{1,0:T(8,128)(2,1)S(1)} %collective-permute-done.4.refs_3_), channel_id=1, source_target_pairs={{0,16},{16,32},{32,48},{48,64},{64,80},{80,96},{96,112},{112,0},{1... | collective-permute-start | bytes 798728 | tf_op jit(solution)/shard_map/ppermute | solution.py:431
  30.3 11.4 %collective-permute-start.8 = (bf16[1040,128]{1,0:T(8,128)(2,1)S(1)}, bf16[1040,128]{1,0:T(8,128)(2,1)S(1)}, u32[]{:S(2)}, u32[]{:S(2)}) collective-permute-start(bf16[1040,128]{1,0:T(8,128)(2,1)S(1)} %collective-permute-done.4.refs_3_), channel_id=1, source_target_pairs={{0,128},{16,144},{32,160},{48,176},{64,192},{80,208},{96,224},{112... | collective-permute-start | bytes 798728 | tf_op jit(solution)/shard_map/ppermute | solution.py:431
  30.3 15.3 %collective-permute-start.13 = (bf16[1040,128]{1,0:T(8,128)(2,1)S(1)}, bf16[1040,128]{1,0:T(8,128)(2,1)S(1)}, u32[]{:S(2)}, u32[]{:S(2)}) collective-permute-start(bf16[1040,128]{1,0:T(8,128)(2,1)S(1)} %collective-permute-done.10.refs_1_), channel_id=1, source_target_pairs={{0,128},{16,144},{32,160},{48,176},{64,192},{80,208},{96,224},{112... | collective-permute-start | bytes 798728 | tf_op jit(solution)/shard_map/ppermute | solution.py:431
  33.1 12.5 %collective-permute-start.14 = (bf16[1040,128]{1,0:T(8,128)(2,1)S(1)}, bf16[1040,128]{1,0:T(8,128)(2,1)S(1)}, u32[]{:S(2)}, u32[]{:S(2)}) collective-permute-start(bf16[1040,128]{1,0:T(8,128)(2,1)S(1)} %collective-permute-done.11.refs_2_), channel_id=1, source_target_pairs={{0,128},{16,144},{32,160},{48,176},{64,192},{80,208},{96,224},{112... | collective-permute-start | bytes 798728 | tf_op jit(solution)/shard_map/ppermute | solution.py:431
  44.1 24.0 %collective-permute-start.27 = (bf16[2080,128]{1,0:T(8,128)(2,1)S(1)}, bf16[2080,128]{1,0:T(8,128)(2,1)S(1)}, u32[]{:S(2)}, u32[]{:S(2)}) collective-permute-start(bf16[2080,128]{1,0:T(8,128)(2,1)S(1)} %collective-permute-done.26.refs_5_), channel_id=1, source_target_pairs={{0,16},{16,32},{32,48},{48,64},{64,80},{80,96},{96,112},{112,0},{1... | collective-permute-start | bytes 1597448 | tf_op jit(solution)/shard_map/ppermute | solution.py:431
  52.9 9.4 %collective-permute-start.18 = (bf16[4,128,384]{2,1,0:T(8,128)(2,1)S(1)}, bf16[4,128,384]{2,1,0:T(8,128)(2,1)S(1)}, u32[]{:S(2)}, u32[]{:S(2)}) collective-permute-start(bf16[4,128,384]{2,1,0:T(8,128)(2,1)S(1)} %get-tuple-element.33), channel_id=1, source_target_pairs={{0,2},{1,3},{2,0},{3,1},{4,6},{5,7},{6,4},{7,5},{8,10},{9,11},{10,... | collective-permute-start | bytes 1179656 | tf_op jit(solution)/shard_map/ppermute | solution.py:435
  54.0 12.0 %collective-permute-start.19 = (bf16[4,128,384]{2,1,0:T(8,128)(2,1)S(1)}, bf16[4,128,384]{2,1,0:T(8,128)(2,1)S(1)}, u32[]{:S(2)}, u32[]{:S(2)}) collective-permute-start(bf16[4,128,384]{2,1,0:T(8,128)(2,1)S(1)} %get-tuple-element.34), channel_id=1, source_target_pairs={{0,3},{1,0},{2,1},{3,2},{4,7},{5,4},{6,5},{7,6},{8,11},{9,8},{10,9... | collective-permute-start | bytes 1179656 | tf_op jit(solution)/shard_map/ppermute | solution.py:435
  66.3 9.1 %collective-permute-start.20 = (bf16[4,128,384]{2,1,0:T(8,128)(2,1)S(1)}, bf16[4,128,384]{2,1,0:T(8,128)(2,1)S(1)}, u32[]{:S(2)}, u32[]{:S(2)}) collective-permute-start(bf16[4,128,384]{2,1,0:T(8,128)(2,1)S(1)} %shard_map.82.refs_1_), channel_id=1, source_target_pairs={{0,4},{1,5},{2,6},{3,7},{4,8},{5,9},{6,10},{7,11},{8,12},{9,13},{1... | collective-permute-start | bytes 1179656 | tf_op jit(solution)/shard_map/ppermute | solution.py:435
  68.1 10.5 %collective-permute-start.28 = (bf16[2080,128]{1,0:T(8,128)(2,1)S(1)}, bf16[2080,128]{1,0:T(8,128)(2,1)S(1)}, u32[]{:S(2)}, u32[]{:S(2)}) collective-permute-start(bf16[2080,128]{1,0:T(8,128)(2,1)S(1)} %collective-permute-done.27.refs_6_), channel_id=1, source_target_pairs={{0,16},{16,32},{32,48},{48,64},{64,80},{80,96},{96,112},{112,0},{1... | collective-permute-start | bytes 1597448 | tf_op jit(solution)/shard_map/ppermute | solution.py:431
  69.0 16.2 %collective-permute-start.30 = (bf16[2080,128]{1,0:T(8,128)(2,1)S(1)}, bf16[2080,128]{1,0:T(8,128)(2,1)S(1)}, u32[]{:S(2)}, u32[]{:S(2)}) collective-permute-start(bf16[2080,128]{1,0:T(8,128)(2,1)S(1)} %collective-permute-done.26.refs_5_), channel_id=1, source_target_pairs={{0,128},{16,144},{32,160},{48,176},{64,192},{80,208},{96,224},{112... | collective-permute-start | bytes 1597448 | tf_op jit(solution)/shard_map/ppermute | solution.py:431
  69.0 17.4 %collective-permute-start.31 = (bf16[2080,128]{1,0:T(8,128)(2,1)S(1)}, bf16[2080,128]{1,0:T(8,128)(2,1)S(1)}, u32[]{:S(2)}, u32[]{:S(2)}) collective-permute-start(bf16[2080,128]{1,0:T(8,128)(2,1)S(1)} %collective-permute-done.27.refs_6_), channel_id=1, source_target_pairs={{0,128},{16,144},{32,160},{48,176},{64,192},{80,208},{96,224},{112... | collective-permute-start | bytes 1597448 | tf_op jit(solution)/shard_map/ppermute | solution.py:431
  69.5 11.3 %collective-permute-start.21 = (bf16[4,128,384]{2,1,0:T(8,128)(2,1)S(1)}, bf16[4,128,384]{2,1,0:T(8,128)(2,1)S(1)}, u32[]{:S(2)}, u32[]{:S(2)}) collective-permute-start(bf16[4,128,384]{2,1,0:T(8,128)(2,1)S(1)} %shard_map.82.refs_1_), channel_id=1, source_target_pairs={{0,8},{1,9},{2,10},{3,11},{4,12},{5,13},{6,14},{7,15},{8,0},{9,1},... | collective-permute-start | bytes 1179656 | tf_op jit(solution)/shard_map/ppermute | solution.py:435
  78.6 19.8 %collective-permute-start.29 = (bf16[2080,128]{1,0:T(8,128)(2,1)S(1)}, bf16[2080,128]{1,0:T(8,128)(2,1)S(1)}, u32[]{:S(2)}, u32[]{:S(2)}) collective-permute-start(bf16[2080,128]{1,0:T(8,128)(2,1)S(1)} %collective-permute-done.28.refs_7_), channel_id=1, source_target_pairs={{0,16},{16,32},{32,48},{48,64},{64,80},{80,96},{96,112},{112,0},{1... | collective-permute-start | bytes 1597448 | tf_op jit(solution)/shard_map/ppermute | solution.py:431
  80.8 17.6 %collective-permute-start.32 = (bf16[2080,128]{1,0:T(8,128)(2,1)S(1)}, bf16[2080,128]{1,0:T(8,128)(2,1)S(1)}, u32[]{:S(2)}, u32[]{:S(2)}) collective-permute-start(bf16[2080,128]{1,0:T(8,128)(2,1)S(1)} %collective-permute-done.28.refs_7_), channel_id=1, source_target_pairs={{0,128},{16,144},{32,160},{48,176},{64,192},{80,208},{96,224},{112... | collective-permute-start | bytes 1597448 | tf_op jit(solution)/shard_map/ppermute | solution.py:431
  85.2 9.4 %collective-permute-start.24 = (bf16[4,128,384]{2,1,0:T(8,128)(2,1)S(1)}, bf16[4,128,384]{2,1,0:T(8,128)(2,1)S(1)}, u32[]{:S(2)}, u32[]{:S(2)}) collective-permute-start(bf16[4,128,384]{2,1,0:T(8,128)(2,1)S(1)} %get-tuple-element.36.refs_0_), channel_id=1, source_target_pairs={{0,2},{1,3},{2,0},{3,1},{4,6},{5,7},{6,4},{7,5},{8,10},{9,11},{10,... | collective-permute-start | bytes 1179656 | tf_op jit(solution)/shard_map/ppermute | solution.py:435
  86.4 12.0 %collective-permute-start.25 = (bf16[4,128,384]{2,1,0:T(8,128)(2,1)S(1)}, bf16[4,128,384]{2,1,0:T(8,128)(2,1)S(1)}, u32[]{:S(2)}, u32[]{:S(2)}) collective-permute-start(bf16[4,128,384]{2,1,0:T(8,128)(2,1)S(1)} %get-tuple-element.36.refs_0_), channel_id=1, source_target_pairs={{0,3},{1,0},{2,1},{3,2},{4,7},{5,4},{6,5},{7,6},{8,11},{9,8},{10,9... | collective-permute-start | bytes 1179656 | tf_op jit(solution)/shard_map/ppermute | solution.py:435
  105.8 9.5 %collective-permute-start.34 = (bf16[4,128,384]{2,1,0:T(8,128)(2,1)S(1)}, bf16[4,128,384]{2,1,0:T(8,128)(2,1)S(1)}, u32[]{:S(2)}, u32[]{:S(2)}) collective-permute-start(bf16[4,128,384]{2,1,0:T(8,128)(2,1)S(1)} %get-tuple-element.43), channel_id=1, source_target_pairs={{0,2},{1,3},{2,0},{3,1},{4,6},{5,7},{6,4},{7,5},{8,10},{9,11},{10,... | collective-permute-start | bytes 1179656 | tf_op jit(solution)/shard_map/ppermute | solution.py:435
  107.4 12.0 %collective-permute-start.35 = (bf16[4,128,384]{2,1,0:T(8,128)(2,1)S(1)}, bf16[4,128,384]{2,1,0:T(8,128)(2,1)S(1)}, u32[]{:S(2)}, u32[]{:S(2)}) collective-permute-start(bf16[4,128,384]{2,1,0:T(8,128)(2,1)S(1)} %get-tuple-element.44), channel_id=1, source_target_pairs={{0,3},{1,0},{2,1},{3,2},{4,7},{5,4},{6,5},{7,6},{8,11},{9,8},{10,9... | collective-permute-start | bytes 1179656 | tf_op jit(solution)/shard_map/ppermute | solution.py:435
  119.6 9.2 %collective-permute-start.38 = (bf16[128,384]{1,0:T(8,128)(2,1)S(1)}, bf16[128,384]{1,0:T(8,128)(2,1)S(1)}, u32[]{:S(2)}, u32[]{:S(2)}) collective-permute-start(bf16[128,384]{1,0:T(8,128)(2,1)S(1)} %get-tuple-element.48), channel_id=1, source_target_pairs={{0,12},{1,13},{2,14},{3,15},{4,0},{5,1},{6,2},{7,3},{8,4},{9,5},{1... | collective-permute-start | bytes 294920 | tf_op jit(solution)/shard_map/ppermute | solution.py:435
  (18 other events, 145.2 us)

commit v6 on v4

--- a/solution.py
+++ b/solution.py
@@ -1,5 +1,3 @@
-import functools
-
 import jax
 import jax.numpy as jnp
 from jax import lax
@@ -11,7 +9,7 @@
 EPSILON = 1e-05
 BLK = 128
 SLOTS = 8
-UNROLL = 4
+UNROLL = 8
 TAIL = 16
 SPAN = 1024 + TAIL
 GRID_ROWS = 8
@@ -167,12 +165,41 @@
     gelu_into(total, hidden_ref)
 
 
-def later_in_kernel(place_ref, gain_ref, *refs):
+def send_out(place_ref, total, sends, relative):
+    for d in range(SIDE):
+        for e in range(SIDE):
+            second = digit(place_ref[3] + e) if relative else e
+            chunk = chunk_of(place_ref, digit(place_ref[2] + d), second)
+            for q in range(CHUNK):
+                sends[d][e, :, q * BLK : (q + 1) * BLK] = total[chunk * CHUNK + q].astype(BF16)
+
+
+def first_out_kernel(place_ref, hidden_ref, *refs):
+    cells = refs[:GRID_ROWS]
+    sends = refs[GRID_ROWS : GRID_ROWS + SIDE]
+    total, weights, tails, table, small, blocks, sems = refs[GRID_ROWS + SIDE :]
+    tail_copies, copies = fetch(cells, 0, weights, tails, sems)
+    read_table(tail_copies, tails, table)
+    total[...] = jnp.zeros_like(total)
+    used = list_blocks(table, small, BLOCKS, blocks)
+    for copy in copies:
+        copy.wait()
+    block_sum(hidden_ref, weights, blocks, used, total)
+    send_out(place_ref, total, sends, False)
+
+
+def later_kernel(place_ref, gain_ref, *refs):
     bundles = refs[:SIDE]
     cells = refs[SIDE : SIDE + GRID_ROWS]
-    hidden_ref, normed, total, weights, tails, table, small, blocks, sems = refs[SIDE + GRID_ROWS :]
-    tail_copies, copies = fetch(cells, 0, weights, tails, sems)
-    read_table(tail_copies, tails, table)
+    sends = refs[SIDE + GRID_ROWS : 2 * SIDE + GRID_ROWS]
+    normed, hidden, total_in, total_out = refs[2 * SIDE + GRID_ROWS : 2 * SIDE + GRID_ROWS + 4]
+    work = refs[2 * SIDE + GRID_ROWS + 4 :]
+    works = (work[: len(work) // 2], work[len(work) // 2 :])
+    flights = []
+    for k, (weights, tails, table, small, blocks, sems) in enumerate(works):
+        flights.append(fetch(cells, k * SPAN, weights, tails, sems))
+    for (tail_copies, _), (_, tails, table, _, _, _) in zip(flights, works):
+        read_table(tail_copies, tails, table)
     squares = jnp.zeros((TOK, BLK), F32)
     for d in range(SIDE):
         for e in range(SIDE):
@@ -188,31 +215,19 @@
                 k = chunk * CHUNK + q
                 part = bundles[d][e, :, q * BLK : (q + 1) * BLK].astype(F32)
                 normed[k] = (part * scale * gain_ref[k]).astype(BF16)
-    total[...] = jnp.zeros_like(total)
-    used = list_blocks(table, small, FBL, blocks)
-    for copy in copies:
-        copy.wait()
-    block_sum(normed, weights, blocks, used, total)
-    gelu_into(total, hidden_ref)
-
-
-def out_kernel(phase, place_ref, hidden_ref, *refs):
-    cells = refs[:GRID_ROWS]
-    sends = refs[GRID_ROWS : GRID_ROWS + SIDE]
-    total, weights, tails, table, small, blocks, sems = refs[GRID_ROWS + SIDE :]
-    tail_copies, copies = fetch(cells, phase * SPAN, weights, tails, sems)
-    read_table(tail_copies, tails, table)
-    total[...] = jnp.zeros_like(total)
-    used = list_blocks(table, small, BLOCKS, blocks)
-    for copy in copies:
-        copy.wait()
-    block_sum(hidden_ref, weights, blocks, used, total)
-    for d in range(SIDE):
-        for e in range(SIDE):
-            second = digit(place_ref[3] + e) if phase else e
-            chunk = chunk_of(place_ref, digit(place_ref[2] + d), second)
-            for q in range(CHUNK):
-                sends[d][e, :, q * BLK : (q + 1) * BLK] = total[chunk * CHUNK + q].astype(BF16)
+    totals = (total_in, total_out)
+    used = []
+    for total, dummy, (_, _, table, small, blocks, _) in zip(totals, (FBL, BLOCKS), works):
+        total[...] = jnp.zeros_like(total)
+        used.append(list_blocks(table, small, dummy, blocks))
+    for k, dense in enumerate((normed, hidden)):
+        weights, _, _, _, blocks, _ = works[k]
+        for copy in flights[k][1]:
+            copy.wait()
+        block_sum(dense, weights, blocks, used[k], totals[k])
+        if k == 0:
+            gelu_into(total_in, hidden)
+    send_out(place_ref, total_out, sends, True)
 
 
 def sum_of(refs, index):
@@ -297,26 +312,29 @@
     )(normed, *cells)
 
 
-def later_in(place, gain, bundles, cells):
+def later_both(place, gain, bundles, cells):
     return pl.pallas_call(
-        later_in_kernel,
+        later_kernel,
         in_specs=[smem()] + [vmem()] * (1 + SIDE) + [anywhere()] * GRID_ROWS,
-        out_specs=vmem(),
-        out_shape=HIDDEN,
+        out_specs=[vmem()] * SIDE,
+        out_shape=[BUNDLE] * SIDE,
         scratch_shapes=[
             pltpu.VMEM((BLOCKS, TOK, BLK), BF16),
+            pltpu.VMEM((FBL, TOK, BLK), BF16),
             pltpu.VMEM((FBL + 1, TOK, BLK), F32),
+            pltpu.VMEM((BLOCKS + 1, TOK, BLK), F32),
         ]
+        + WORK
         + WORK,
-        cost_estimate=cost(512, 12 << 20),
-        compiler_params=PARAMS,
-        name="later_in",
+        cost_estimate=cost(1024, 16 << 20),
+        compiler_params=pltpu.CompilerParams(vmem_limit_bytes=24 << 20),
+        name="later_both",
     )(place, gain, *bundles, *cells)
 
 
-def project_out(phase, place, hidden, cells):
+def project_out(place, hidden, cells):
     return pl.pallas_call(
-        functools.partial(out_kernel, phase),
+        first_out_kernel,
         in_specs=[smem(), vmem()] + [anywhere()] * GRID_ROWS,
         out_specs=[vmem()] * SIDE,
         out_shape=[BUNDLE] * SIDE,
@@ -437,15 +455,14 @@
 
     normed, own_x = first_norm(micro, place, inputs, gains[0])
     hidden = first_in(normed, cells_in)
-    bundles = project_out(0, place, hidden, cells_out)
+    bundles = project_out(place, hidden, cells_out)
     landed = spread(bundles, True)
     sums = add_up(whole_sum_kernel, None, [bundles[0]] + landed, [BUNDLE])[0]
     landed = spread(sums, False)
     middle, piece = add_up(merge_kernel, place, [own_x, sums] + landed, [BUNDLE, PIECE])
 
     bundles = [middle] + spread(middle, True)
-    hidden = later_in(place, gains[1], bundles, later_cells)
-    bundles = project_out(1, place, hidden, later_cells)
+    bundles = later_both(place, gains[1], bundles, later_cells)
     landed = spread(bundles, True)
     sums = add_up(
         piece_sum_kernel,

time: 136 us -> 134 us (0.985)
  Pallas kernels: 18.7 us -> 16.1 us
    pallas_call x3 -> x2, Pallas kernels: 11.4 us -> 9.23 us  [the longest x1 6.34 us: later_both(): pl.pallas_call(later_kernel, in_specs=[smem()] + [vmem()] * (1 + SIDE) +...]
where the time goes in v6:
time: 134 us
  waiting for transfers between devices  79.6 us (59%)
  starting transfers between devices  35.7 us (27%)
  Pallas kernels  16.1 us (12%)
  between operations  1.52 us (1%)
    ppermute x15, waiting for transfers between devices, on_cols(): return lax.ppermute(value, ('section', 'col'), perm)  44.7 us
    ppermute x25, waiting for transfers between devices, on_rows(): return lax.ppermute(value, ('section', 'row'), perm)  34.9 us
    ppermute x15, starting transfers between devices, on_cols(): return lax.ppermute(value, ('section', 'col'), perm)  25.1 us
    ppermute x25, starting transfers between devices, on_rows(): return lax.ppermute(value, ('section', 'row'), perm)  10.6 us
    pallas_call x1, Pallas kernels, later_both(): pl.pallas_call(later_kernel, in_specs=[smem()] + [vmem()] * (1 + SIDE) +...  6.34 us
    pallas_call x1, Pallas kernels, project_out(): pl.pallas_call(first_out_kernel, in_specs=[smem(), vmem()] + [anywhere()]...  2.89 us
    pallas_call x1, Pallas kernels, first_in(): pl.pallas_call(first_in_kernel, in_specs=[vmem()] + [anywhere()] * GRID_R...  2.73 us
  transfers between devices with their start and end apart: 40, of which 27 were waited for; matrix products, arithmetic and copies ran while one was open for 0% of the time, Pallas kernels for 6%

profile of v6, /device:TPU:2, one launch (start us, length us, event | category | flops | bytes accessed | tf_op | source)
XLA Modules:
  0.0 134.1 jit_solution(17258305672357846348)
XLA Ops:
  8.7 6.3 %collective-permute-done.2.refs_1_ = bf16[1040,128]{1,0:T(8,128)(2,1)S(1)} collective-permute-done((bf16[1040,128]{1,0:T(8,128)(2,1)S(1)}, bf16[1040,128]{1,0:T(8,128)(2,1)S(1)}, u32[]{:S(2)}, u32[]{:S(2)}) %collective-permute-start.2) | collective-permute-done | bytes 266272 | tf_op jit(solution)/shard_map/ppermute | solution.py:376
  17.9 4.8 %collective-permute-done.3.refs_2_ = bf16[1040,128]{1,0:T(8,128)(2,1)S(1)} collective-permute-done((bf16[1040,128]{1,0:T(8,128)(2,1)S(1)}, bf16[1040,128]{1,0:T(8,128)(2,1)S(1)}, u32[]{:S(2)}, u32[]{:S(2)}) %collective-permute-start.3) | collective-permute-done | bytes 266272 | tf_op jit(solution)/shard_map/ppermute | solution.py:376
  26.9 3.6 %collective-permute-done.4.refs_3_ = bf16[1040,128]{1,0:T(8,128)(2,1)S(1)} collective-permute-done((bf16[1040,128]{1,0:T(8,128)(2,1)S(1)}, bf16[1040,128]{1,0:T(8,128)(2,1)S(1)}, u32[]{:S(2)}, u32[]{:S(2)}) %collective-permute-start.4) | collective-permute-done | bytes 266272 | tf_op jit(solution)/shard_map/ppermute | solution.py:376
  31.1 7.9 %collective-permute-done.12.refs_3_ = bf16[1040,128]{1,0:T(8,128)(2,1)S(1)} collective-permute-done((bf16[1040,128]{1,0:T(8,128)(2,1)S(1)}, bf16[1040,128]{1,0:T(8,128)(2,1)S(1)}, u32[]{:S(2)}, u32[]{:S(2)}) %collective-permute-start.12) | collective-permute-done | bytes 266272 | tf_op jit(solution)/shard_map/ppermute | solution.py:376
  39.0 2.8 %collective-permute-done.5.refs_4_ = bf16[1040,128]{1,0:T(8,128)(2,1)S(1)} collective-permute-done((bf16[1040,128]{1,0:T(8,128)(2,1)S(1)}, bf16[1040,128]{1,0:T(8,128)(2,1)S(1)}, u32[]{:S(2)}, u32[]{:S(2)}) %collective-permute-start.5) | collective-permute-done | bytes 266272 | tf_op jit(solution)/shard_map/ppermute | solution.py:376
  43.3 2.7 %first_in.1.hidden_ref = bf16[12,128,128]{2,1,0:T(8,128)(2,1)S(1)} custom-call(bf16[48,128,128]{2,1,0:T(8,128)(2,1)S(1)} %get-tuple-element.28.normed_ref, bf16[1040,128]{1,0:T(8,128)(2,1)S(1)} %broadcast_select_fusion.3.refs_0_, bf16[1040,128]{1,0:T(8,128)(2,1)S(1)} %collective-permute-done.2.refs_1_, bf16[1040,128]{1,0:T(8,128)(2,1)S(1)} %collective-permute-done.3.refs_2_, ...), custom_call_target="tpu_custom_call" | custom-call | flops 2147483648 | bytes 8388608 | tf_op jit(solution)/shard_map/first_in/pallas_call | solution.py:303
  46.0 3.4 %collective-permute-done.13.refs_4_ = bf16[1040,128]{1,0:T(8,128)(2,1)S(1)} collective-permute-done((bf16[1040,128]{1,0:T(8,128)(2,1)S(1)}, bf16[1040,128]{1,0:T(8,128)(2,1)S(1)}, u32[]{:S(2)}, u32[]{:S(2)}) %collective-permute-start.13) | collective-permute-done | bytes 266272 | tf_op jit(solution)/shard_map/ppermute | solution.py:376
  49.5 2.9 %project_out.1 = (bf16[4,128,384]{2,1,0:T(8,128)(2,1)S(1)}, bf16[4,128,384]{2,1,0:T(8,128)(2,1)S(1)}, bf16[4,128,384]{2,1,0:T(8,128)(2,1)S(1)}, bf16[4,128,384]{2,1,0:T(8,128)(2,1)S(1)}) custom-call(s32[5]{0:T(128)S(1)} %stack.32.place_ref, bf16[12,128,128]{2,1,0:T(8,128)(2,1)S(1)} %first_in.1.hidden_ref, ...), custom_call_target="tpu_custom_call" | custom-call | flops 2147483648 | bytes 8388608 | tf_op jit(solution)/shard_map/project_out/pallas_call | solution.py:336
  55.1 2.4 %collective-permute-start.19 = (bf16[4,128,384]{2,1,0:T(8,128)(2,1)S(1)}, bf16[4,128,384]{2,1,0:T(8,128)(2,1)S(1)}, u32[]{:S(2)}, u32[]{:S(2)}) collective-permute-start(bf16[4,128,384]{2,1,0:T(8,128)(2,1)S(1)} %get-tuple-element.34), channel_id=1, source_target_pairs={{0,3},{1,0},{2,1},{3,2},{4,7},{5,4},{6,5},{7,6},{8,11},{9,8},{10,9... | collective-permute-start | bytes 1179656 | tf_op jit(solution)/shard_map/ppermute | solution.py:380
  57.4 2.8 %collective-permute-done.17.refs_1_ = bf16[4,128,384]{2,1,0:T(8,128)(2,1)S(1)} collective-permute-done((bf16[4,128,384]{2,1,0:T(8,128)(2,1)S(1)}, bf16[4,128,384]{2,1,0:T(8,128)(2,1)S(1)}, u32[]{:S(2)}, u32[]{:S(2)}) %collective-permute-start.17) | collective-permute-done | bytes 393248 | tf_op jit(solution)/shard_map/ppermute | solution.py:380
  60.2 3.1 %collective-permute-done.18.refs_2_ = bf16[4,128,384]{2,1,0:T(8,128)(2,1)S(1)} collective-permute-done((bf16[4,128,384]{2,1,0:T(8,128)(2,1)S(1)}, bf16[4,128,384]{2,1,0:T(8,128)(2,1)S(1)}, u32[]{:S(2)}, u32[]{:S(2)}) %collective-permute-start.18) | collective-permute-done | bytes 393248 | tf_op jit(solution)/shard_map/ppermute | solution.py:380
  63.3 3.7 %collective-permute-done.19.refs_3_ = bf16[4,128,384]{2,1,0:T(8,128)(2,1)S(1)} collective-permute-done((bf16[4,128,384]{2,1,0:T(8,128)(2,1)S(1)}, bf16[4,128,384]{2,1,0:T(8,128)(2,1)S(1)}, u32[]{:S(2)}, u32[]{:S(2)}) %collective-permute-start.19) | collective-permute-done | bytes 393248 | tf_op jit(solution)/shard_map/ppermute | solution.py:380
  69.9 2.7 %collective-permute-start.21 = (bf16[4,128,384]{2,1,0:T(8,128)(2,1)S(1)}, bf16[4,128,384]{2,1,0:T(8,128)(2,1)S(1)}, u32[]{:S(2)}, u32[]{:S(2)}) collective-permute-start(bf16[4,128,384]{2,1,0:T(8,128)(2,1)S(1)} %shard_map.82.refs_1_), channel_id=1, source_target_pairs={{0,8},{1,9},{2,10},{3,11},{4,12},{5,13},{6,14},{7,15},{8,0},{9,1},... | collective-permute-start | bytes 1179656 | tf_op jit(solution)/shard_map/ppermute | solution.py:380
  72.6 3.8 %collective-permute-done.20.refs_2_ = bf16[4,128,384]{2,1,0:T(8,128)(2,1)S(1)} collective-permute-done((bf16[4,128,384]{2,1,0:T(8,128)(2,1)S(1)}, bf16[4,128,384]{2,1,0:T(8,128)(2,1)S(1)}, u32[]{:S(2)}, u32[]{:S(2)}) %collective-permute-start.20) | collective-permute-done | bytes 393248 | tf_op jit(solution)/shard_map/ppermute | solution.py:380
  79.9 2.2 %collective-permute-done.21.refs_3_ = bf16[4,128,384]{2,1,0:T(8,128)(2,1)S(1)} collective-permute-done((bf16[4,128,384]{2,1,0:T(8,128)(2,1)S(1)}, bf16[4,128,384]{2,1,0:T(8,128)(2,1)S(1)}, u32[]{:S(2)}, u32[]{:S(2)}) %collective-permute-start.21) | collective-permute-done | bytes 393248 | tf_op jit(solution)/shard_map/ppermute | solution.py:380
  89.4 3.6 %collective-permute-done.23.refs_1_ = bf16[4,128,384]{2,1,0:T(8,128)(2,1)S(1)} collective-permute-done((bf16[4,128,384]{2,1,0:T(8,128)(2,1)S(1)}, bf16[4,128,384]{2,1,0:T(8,128)(2,1)S(1)}, u32[]{:S(2)}, u32[]{:S(2)}) %collective-permute-start.23) | collective-permute-done | bytes 393248 | tf_op jit(solution)/shard_map/ppermute | solution.py:380
  93.1 2.6 %collective-permute-done.24.refs_2_ = bf16[4,128,384]{2,1,0:T(8,128)(2,1)S(1)} collective-permute-done((bf16[4,128,384]{2,1,0:T(8,128)(2,1)S(1)}, bf16[4,128,384]{2,1,0:T(8,128)(2,1)S(1)}, u32[]{:S(2)}, u32[]{:S(2)}) %collective-permute-start.24) | collective-permute-done | bytes 393248 | tf_op jit(solution)/shard_map/ppermute | solution.py:380
  95.7 4.0 %collective-permute-done.25.refs_3_ = bf16[4,128,384]{2,1,0:T(8,128)(2,1)S(1)} collective-permute-done((bf16[4,128,384]{2,1,0:T(8,128)(2,1)S(1)}, bf16[4,128,384]{2,1,0:T(8,128)(2,1)S(1)}, u32[]{:S(2)}, u32[]{:S(2)}) %collective-permute-start.25) | collective-permute-done | bytes 393248 | tf_op jit(solution)/shard_map/ppermute | solution.py:380
  99.7 6.3 %later_both.1 = (bf16[4,128,384]{2,1,0:T(8,128)(2,1)S(1)}, bf16[4,128,384]{2,1,0:T(8,128)(2,1)S(1)}, bf16[4,128,384]{2,1,0:T(8,128)(2,1)S(1)}, bf16[4,128,384]{2,1,0:T(8,128)(2,1)S(1)}) custom-call(s32[5]{0:T(128)S(1)} %stack.32.place_ref, f32[48,1,128]{2,1,0:T(1,128)S(1)} %get-tuple-element.53.gain_ref, bf16[4,128,384]{2,1,0:T(8,128)(2,1)S(1)} %get-tuple-element.36.refs_0_, ...), custom_call_target="tpu_custom_call" | custom-call | flops 4294967296 | bytes 16777216 | tf_op jit(solution)/shard_map/later_both/pallas_call | solution.py:316
  109.6 4.3 %collective-permute-done.33.refs_1_ = bf16[4,128,384]{2,1,0:T(8,128)(2,1)S(1)} collective-permute-done((bf16[4,128,384]{2,1,0:T(8,128)(2,1)S(1)}, bf16[4,128,384]{2,1,0:T(8,128)(2,1)S(1)}, u32[]{:S(2)}, u32[]{:S(2)}) %collective-permute-start.33) | collective-permute-done | bytes 393248 | tf_op jit(solution)/shard_map/ppermute | solution.py:380
  115.6 4.8 %collective-permute-done.35.refs_3_ = bf16[4,128,384]{2,1,0:T(8,128)(2,1)S(1)} collective-permute-done((bf16[4,128,384]{2,1,0:T(8,128)(2,1)S(1)}, bf16[4,128,384]{2,1,0:T(8,128)(2,1)S(1)}, u32[]{:S(2)}, u32[]{:S(2)}) %collective-permute-start.35) | collective-permute-done | bytes 393248 | tf_op jit(solution)/shard_map/ppermute | solution.py:380
  120.6 4.4 %collective-permute-start.38 = (bf16[128,384]{1,0:T(8,128)(2,1)S(1)}, bf16[128,384]{1,0:T(8,128)(2,1)S(1)}, u32[]{:S(2)}, u32[]{:S(2)}) collective-permute-start(bf16[128,384]{1,0:T(8,128)(2,1)S(1)} %get-tuple-element.48), channel_id=1, source_target_pairs={{0,12},{1,13},{2,14},{3,15},{4,0},{5,1},{6,2},{7,3},{8,4},{9,5},{1... | collective-permute-start | bytes 294920 | tf_op jit(solution)/shard_map/ppermute | solution.py:380
  125.9 2.3 %collective-permute-done.38 = bf16[128,384]{1,0:T(8,128)(2,1)S(1)} collective-permute-done((bf16[128,384]{1,0:T(8,128)(2,1)S(1)}, bf16[128,384]{1,0:T(8,128)(2,1)S(1)}, u32[]{:S(2)}, u32[]{:S(2)}) %collective-permute-start.38) | collective-permute-done | bytes 98336 | tf_op jit(solution)/shard_map/ppermute | solution.py:380
  128.2 3.0 %collective-permute-done.37 = bf16[128,384]{1,0:T(8,128)(2,1)S(1)} collective-permute-done((bf16[128,384]{1,0:T(8,128)(2,1)S(1)}, bf16[128,384]{1,0:T(8,128)(2,1)S(1)}, u32[]{:S(2)}, u32[]{:S(2)}) %collective-permute-start.37) | collective-permute-done | bytes 98336 | tf_op jit(solution)/shard_map/ppermute | solution.py:380
  (77 shorter events, 42.1 us)
Async XLA Ops:
  4.7 10.3 %collective-permute-start.2 = (bf16[1040,128]{1,0:T(8,128)(2,1)S(1)}, bf16[1040,128]{1,0:T(8,128)(2,1)S(1)}, u32[]{:S(2)}, u32[]{:S(2)}) collective-permute-start(bf16[1040,128]{1,0:T(8,128)(2,1)S(1)} %broadcast_select_fusion.3.refs_0_), channel_id=1, source_target_pairs={{0,16},{16,32},{32,48},{48,64},{64,80},{80,96},{96,112},{112,0},{1... | collective-permute-start | bytes 798728 | tf_op jit(solution)/shard_map/ppermute | solution.py:376
  6.7 11.1 %collective-permute-start.10 = (bf16[1040,128]{1,0:T(8,128)(2,1)S(1)}, bf16[1040,128]{1,0:T(8,128)(2,1)S(1)}, u32[]{:S(2)}, u32[]{:S(2)}) collective-permute-start(bf16[1040,128]{1,0:T(8,128)(2,1)S(1)} %broadcast_select_fusion.2.refs_0_), channel_id=1, source_target_pairs={{0,16},{16,32},{32,48},{48,64},{64,80},{80,96},{96,112},{112,0},{1... | collective-permute-start | bytes 798728 | tf_op jit(solution)/shard_map/ppermute | solution.py:376
  15.0 15.5 %collective-permute-start.6 = (bf16[1040,128]{1,0:T(8,128)(2,1)S(1)}, bf16[1040,128]{1,0:T(8,128)(2,1)S(1)}, u32[]{:S(2)}, u32[]{:S(2)}) collective-permute-start(bf16[1040,128]{1,0:T(8,128)(2,1)S(1)} %collective-permute-done.2.refs_1_), channel_id=1, source_target_pairs={{0,128},{16,144},{32,160},{48,176},{64,192},{80,208},{96,224},{112... | collective-permute-start | bytes 798728 | tf_op jit(solution)/shard_map/ppermute | solution.py:376
  22.9 20.3 %collective-permute-start.26 = (bf16[2080,128]{1,0:T(8,128)(2,1)S(1)}, bf16[2080,128]{1,0:T(8,128)(2,1)S(1)}, u32[]{:S(2)}, u32[]{:S(2)}) collective-permute-start(bf16[2080,128]{1,0:T(8,128)(2,1)S(1)} %pad_maximum_fusion.refs_4_), channel_id=1, source_target_pairs={{0,16},{16,32},{32,48},{48,64},{64,80},{80,96},{96,112},{112,0},{1... | collective-permute-start | bytes 1597448 | tf_op jit(solution)/shard_map/ppermute | solution.py:376
  25.5 13.5 %collective-permute-start.12 = (bf16[1040,128]{1,0:T(8,128)(2,1)S(1)}, bf16[1040,128]{1,0:T(8,128)(2,1)S(1)}, u32[]{:S(2)}, u32[]{:S(2)}) collective-permute-start(bf16[1040,128]{1,0:T(8,128)(2,1)S(1)} %collective-permute-done.11.refs_2_), channel_id=1, source_target_pairs={{0,16},{16,32},{32,48},{48,64},{64,80},{80,96},{96,112},{112,0},{1... | collective-permute-start | bytes 798728 | tf_op jit(solution)/shard_map/ppermute | solution.py:376
  30.4 11.4 %collective-permute-start.5 = (bf16[1040,128]{1,0:T(8,128)(2,1)S(1)}, bf16[1040,128]{1,0:T(8,128)(2,1)S(1)}, u32[]{:S(2)}, u32[]{:S(2)}) collective-permute-start(bf16[1040,128]{1,0:T(8,128)(2,1)S(1)} %collective-permute-done.4.refs_3_), channel_id=1, source_target_pairs={{0,16},{16,32},{32,48},{48,64},{64,80},{80,96},{96,112},{112,0},{1... | collective-permute-start | bytes 798728 | tf_op jit(solution)/shard_map/ppermute | solution.py:376
  30.6 11.3 %collective-permute-start.8 = (bf16[1040,128]{1,0:T(8,128)(2,1)S(1)}, bf16[1040,128]{1,0:T(8,128)(2,1)S(1)}, u32[]{:S(2)}, u32[]{:S(2)}) collective-permute-start(bf16[1040,128]{1,0:T(8,128)(2,1)S(1)} %collective-permute-done.4.refs_3_), channel_id=1, source_target_pairs={{0,128},{16,144},{32,160},{48,176},{64,192},{80,208},{96,224},{112... | collective-permute-start | bytes 798728 | tf_op jit(solution)/shard_map/ppermute | solution.py:376
  30.6 15.5 %collective-permute-start.14 = (bf16[1040,128]{1,0:T(8,128)(2,1)S(1)}, bf16[1040,128]{1,0:T(8,128)(2,1)S(1)}, u32[]{:S(2)}, u32[]{:S(2)}) collective-permute-start(bf16[1040,128]{1,0:T(8,128)(2,1)S(1)} %collective-permute-done.10.refs_1_), channel_id=1, source_target_pairs={{0,128},{16,144},{32,160},{48,176},{64,192},{80,208},{96,224},{112... | collective-permute-start | bytes 798728 | tf_op jit(solution)/shard_map/ppermute | solution.py:376
  43.2 26.2 %collective-permute-start.27 = (bf16[2080,128]{1,0:T(8,128)(2,1)S(1)}, bf16[2080,128]{1,0:T(8,128)(2,1)S(1)}, u32[]{:S(2)}, u32[]{:S(2)}) collective-permute-start(bf16[2080,128]{1,0:T(8,128)(2,1)S(1)} %collective-permute-done.26.refs_5_), channel_id=1, source_target_pairs={{0,16},{16,32},{32,48},{48,64},{64,80},{80,96},{96,112},{112,0},{1... | collective-permute-start | bytes 1597448 | tf_op jit(solution)/shard_map/ppermute | solution.py:376
  52.4 7.9 %collective-permute-start.17 = (bf16[4,128,384]{2,1,0:T(8,128)(2,1)S(1)}, bf16[4,128,384]{2,1,0:T(8,128)(2,1)S(1)}, u32[]{:S(2)}, u32[]{:S(2)}) collective-permute-start(bf16[4,128,384]{2,1,0:T(8,128)(2,1)S(1)} %get-tuple-element.32), channel_id=1, source_target_pairs={{0,1},{1,2},{2,3},{3,0},{4,5},{5,6},{6,7},{7,4},{8,9},{9,10},{10,1... | collective-permute-start | bytes 1179656 | tf_op jit(solution)/shard_map/ppermute | solution.py:380
  54.0 9.4 %collective-permute-start.18 = (bf16[4,128,384]{2,1,0:T(8,128)(2,1)S(1)}, bf16[4,128,384]{2,1,0:T(8,128)(2,1)S(1)}, u32[]{:S(2)}, u32[]{:S(2)}) collective-permute-start(bf16[4,128,384]{2,1,0:T(8,128)(2,1)S(1)} %get-tuple-element.33), channel_id=1, source_target_pairs={{0,2},{1,3},{2,0},{3,1},{4,6},{5,7},{6,4},{7,5},{8,10},{9,11},{10,... | collective-permute-start | bytes 1179656 | tf_op jit(solution)/shard_map/ppermute | solution.py:380
  55.1 12.0 %collective-permute-start.19 = (bf16[4,128,384]{2,1,0:T(8,128)(2,1)S(1)}, bf16[4,128,384]{2,1,0:T(8,128)(2,1)S(1)}, u32[]{:S(2)}, u32[]{:S(2)}) collective-permute-start(bf16[4,128,384]{2,1,0:T(8,128)(2,1)S(1)} %get-tuple-element.34), channel_id=1, source_target_pairs={{0,3},{1,0},{2,1},{3,2},{4,7},{5,4},{6,5},{7,6},{8,11},{9,8},{10,9... | collective-permute-start | bytes 1179656 | tf_op jit(solution)/shard_map/ppermute | solution.py:380
  67.3 9.1 %collective-permute-start.20 = (bf16[4,128,384]{2,1,0:T(8,128)(2,1)S(1)}, bf16[4,128,384]{2,1,0:T(8,128)(2,1)S(1)}, u32[]{:S(2)}, u32[]{:S(2)}) collective-permute-start(bf16[4,128,384]{2,1,0:T(8,128)(2,1)S(1)} %shard_map.82.refs_1_), channel_id=1, source_target_pairs={{0,4},{1,5},{2,6},{3,7},{4,8},{5,9},{6,10},{7,11},{8,12},{9,13},{1... | collective-permute-start | bytes 1179656 | tf_op jit(solution)/shard_map/ppermute | solution.py:380
  69.4 10.5 %collective-permute-start.28 = (bf16[2080,128]{1,0:T(8,128)(2,1)S(1)}, bf16[2080,128]{1,0:T(8,128)(2,1)S(1)}, u32[]{:S(2)}, u32[]{:S(2)}) collective-permute-start(bf16[2080,128]{1,0:T(8,128)(2,1)S(1)} %collective-permute-done.27.refs_6_), channel_id=1, source_target_pairs={{0,16},{16,32},{32,48},{48,64},{64,80},{80,96},{96,112},{112,0},{1... | collective-permute-start | bytes 1597448 | tf_op jit(solution)/shard_map/ppermute | solution.py:376
  69.4 16.9 %collective-permute-start.30 = (bf16[2080,128]{1,0:T(8,128)(2,1)S(1)}, bf16[2080,128]{1,0:T(8,128)(2,1)S(1)}, u32[]{:S(2)}, u32[]{:S(2)}) collective-permute-start(bf16[2080,128]{1,0:T(8,128)(2,1)S(1)} %collective-permute-done.26.refs_5_), channel_id=1, source_target_pairs={{0,128},{16,144},{32,160},{48,176},{64,192},{80,208},{96,224},{112... | collective-permute-start | bytes 1597448 | tf_op jit(solution)/shard_map/ppermute | solution.py:376
  69.4 18.3 %collective-permute-start.31 = (bf16[2080,128]{1,0:T(8,128)(2,1)S(1)}, bf16[2080,128]{1,0:T(8,128)(2,1)S(1)}, u32[]{:S(2)}, u32[]{:S(2)}) collective-permute-start(bf16[2080,128]{1,0:T(8,128)(2,1)S(1)} %collective-permute-done.27.refs_6_), channel_id=1, source_target_pairs={{0,128},{16,144},{32,160},{48,176},{64,192},{80,208},{96,224},{112... | collective-permute-start | bytes 1597448 | tf_op jit(solution)/shard_map/ppermute | solution.py:376
  69.9 12.1 %collective-permute-start.21 = (bf16[4,128,384]{2,1,0:T(8,128)(2,1)S(1)}, bf16[4,128,384]{2,1,0:T(8,128)(2,1)S(1)}, u32[]{:S(2)}, u32[]{:S(2)}) collective-permute-start(bf16[4,128,384]{2,1,0:T(8,128)(2,1)S(1)} %shard_map.82.refs_1_), channel_id=1, source_target_pairs={{0,8},{1,9},{2,10},{3,11},{4,12},{5,13},{6,14},{7,15},{8,0},{9,1},... | collective-permute-start | bytes 1179656 | tf_op jit(solution)/shard_map/ppermute | solution.py:380
  79.9 19.8 %collective-permute-start.29 = (bf16[2080,128]{1,0:T(8,128)(2,1)S(1)}, bf16[2080,128]{1,0:T(8,128)(2,1)S(1)}, u32[]{:S(2)}, u32[]{:S(2)}) collective-permute-start(bf16[2080,128]{1,0:T(8,128)(2,1)S(1)} %collective-permute-done.28.refs_7_), channel_id=1, source_target_pairs={{0,16},{16,32},{32,48},{48,64},{64,80},{80,96},{96,112},{112,0},{1... | collective-permute-start | bytes 1597448 | tf_op jit(solution)/shard_map/ppermute | solution.py:376
  82.0 17.7 %collective-permute-start.32 = (bf16[2080,128]{1,0:T(8,128)(2,1)S(1)}, bf16[2080,128]{1,0:T(8,128)(2,1)S(1)}, u32[]{:S(2)}, u32[]{:S(2)}) collective-permute-start(bf16[2080,128]{1,0:T(8,128)(2,1)S(1)} %collective-permute-done.28.refs_7_), channel_id=1, source_target_pairs={{0,128},{16,144},{32,160},{48,176},{64,192},{80,208},{96,224},{112... | collective-permute-start | bytes 1597448 | tf_op jit(solution)/shard_map/ppermute | solution.py:376
  85.0 8.1 %collective-permute-start.23 = (bf16[4,128,384]{2,1,0:T(8,128)(2,1)S(1)}, bf16[4,128,384]{2,1,0:T(8,128)(2,1)S(1)}, u32[]{:S(2)}, u32[]{:S(2)}) collective-permute-start(bf16[4,128,384]{2,1,0:T(8,128)(2,1)S(1)} %get-tuple-element.36.refs_0_), channel_id=1, source_target_pairs={{0,1},{1,2},{2,3},{3,0},{4,5},{5,6},{6,7},{7,4},{8,9},{9,10},{10,1... | collective-permute-start | bytes 1179656 | tf_op jit(solution)/shard_map/ppermute | solution.py:380
  86.3 9.4 %collective-permute-start.24 = (bf16[4,128,384]{2,1,0:T(8,128)(2,1)S(1)}, bf16[4,128,384]{2,1,0:T(8,128)(2,1)S(1)}, u32[]{:S(2)}, u32[]{:S(2)}) collective-permute-start(bf16[4,128,384]{2,1,0:T(8,128)(2,1)S(1)} %get-tuple-element.36.refs_0_), channel_id=1, source_target_pairs={{0,2},{1,3},{2,0},{3,1},{4,6},{5,7},{6,4},{7,5},{8,10},{9,11},{10,... | collective-permute-start | bytes 1179656 | tf_op jit(solution)/shard_map/ppermute | solution.py:380
  87.7 12.0 %collective-permute-start.25 = (bf16[4,128,384]{2,1,0:T(8,128)(2,1)S(1)}, bf16[4,128,384]{2,1,0:T(8,128)(2,1)S(1)}, u32[]{:S(2)}, u32[]{:S(2)}) collective-permute-start(bf16[4,128,384]{2,1,0:T(8,128)(2,1)S(1)} %get-tuple-element.36.refs_0_), channel_id=1, source_target_pairs={{0,3},{1,0},{2,1},{3,2},{4,7},{5,4},{6,5},{7,6},{8,11},{9,8},{10,9... | collective-permute-start | bytes 1179656 | tf_op jit(solution)/shard_map/ppermute | solution.py:380
  106.1 9.5 %collective-permute-start.34 = (bf16[4,128,384]{2,1,0:T(8,128)(2,1)S(1)}, bf16[4,128,384]{2,1,0:T(8,128)(2,1)S(1)}, u32[]{:S(2)}, u32[]{:S(2)}) collective-permute-start(bf16[4,128,384]{2,1,0:T(8,128)(2,1)S(1)} %get-tuple-element.43), channel_id=1, source_target_pairs={{0,2},{1,3},{2,0},{3,1},{4,6},{5,7},{6,4},{7,5},{8,10},{9,11},{10,... | collective-permute-start | bytes 1179656 | tf_op jit(solution)/shard_map/ppermute | solution.py:380
  108.0 12.4 %collective-permute-start.35 = (bf16[4,128,384]{2,1,0:T(8,128)(2,1)S(1)}, bf16[4,128,384]{2,1,0:T(8,128)(2,1)S(1)}, u32[]{:S(2)}, u32[]{:S(2)}) collective-permute-start(bf16[4,128,384]{2,1,0:T(8,128)(2,1)S(1)} %get-tuple-element.44), channel_id=1, source_target_pairs={{0,3},{1,0},{2,1},{3,2},{4,7},{5,4},{6,5},{7,6},{8,11},{9,8},{10,9... | collective-permute-start | bytes 1179656 | tf_op jit(solution)/shard_map/ppermute | solution.py:380
  (18 other events, 147.2 us)
